TPU v7x, 128 devices: a whole 4x4x4 slice. The times are simulated.
128 devices in a mesh: req: 8 (over x, y_hi), hid: 16 (over y_lo, z, core).
Axes of the slice: x: 4, y: 4 (y_hi: 2, y_lo: 2; y = y_hi * 2 + y_lo), z: 4, core: 2. Of those that a mesh axis runs over, the one named last changes fastest.
Arguments:
- input_activations: bfloat16 [8, 512, 4096], P('req'), may hold values from -6 to 6
- prompt_extents: int32 [8], P('req'), may hold values from 1 to 512, as said below
- continuing_flags: int32 [8], P('req'), may hold values from 0 to 1, as said below
- owning_index: int32 [8], P('req'), may hold values from 0 to 15
- partition_arrangement: int32 [128], replicated, may hold values from 0 to 127, each once
- training_accept_pieces: float32 [4096, 4096], P(('req', 'hid')), may hold values from -0.09375 to 0.09375
- training_lookup_pieces: float32 [4096, 4096], P(('req', 'hid')), may hold values from -0.09375 to 0.09375
- training_content_pieces: float32 [4096, 4096], P(('req', 'hid')), may hold values from -0.09375 to 0.09375
- normalizer_scales: bfloat16 [2, 4096], replicated, may hold values from 0.5 to 1.5
- prior_step_blends: bfloat16 [7, 4096], replicated, may hold values from 0.049804688 to 0.94921875
- forgetting_bias_vector: float32 [4096], P('hid'), may hold values from -7 to -3
- forgetting_left_lowrank: bfloat16 [4096, 128], replicated, may hold values from -0.09375 to 0.09375
- forgetting_right_lowrank: bfloat16 [128, 4096], P(None, 'hid'), may hold values from -0.5 to 0.5
- instant_emphasis: float32 [4096], P('hid'), may hold values from -3 to 3
- group_normalizer_scale: float32 [4096], P('hid'), may hold values from 0.5 to 1.5
- gating_projection: bfloat16 [4096, 4096], P(None, 'hid'), may hold values from -0.09375 to 0.09375
- mixing_exit_projection: bfloat16 [4096, 4096], P('hid'), may hold values from -0.09375 to 0.09375
- kept_summary_places: float32 [8, 16, 64, 64, 64], P('req', 'hid'), may hold values from -6 to 6
- previous_normed_entries: bfloat16 [8, 2, 4096], P('req'), may hold values from -6 to 6
- feedforward_entry_proj: bfloat16 [14336, 4096], P(('req', 'hid')), may hold values from -0.09375 to 0.09375
- feedforward_exit_proj: bfloat16 [14336, 4096], P(('req', 'hid')), may hold values from -0.046875 to 0.046875
- feedforward_accept_proj: bfloat16 [4096, 4096], P(None, 'hid'), may hold values from -0.09375 to 0.09375
Outputs:
- layer_out: bfloat16 [8, 512, 4096], P('req', None, 'hid')
- new_states: float32 [8, 64, 64, 64], P('req', 'hid')
- new_shift: bfloat16 [8, 2, 4096], P('req')
Inputs may be any that keep to these rules, and one draw needn't show every extreme that they name: `prompt_extents`: in every draw some request has length 512. `continuing_flags`: at least one request has 1 and at least one has 0. `owning_index`: read only where continuing_flags is 1. `partition_arrangement`: each of 0 to 127 appears once.
All inputs are finite; a program needn't handle non-finite values.
Results may differ from a plain program's by a relative error of at most 0.02.
Values may be sent and summed in bfloat16 or wider, within the bound.
A program may use at most 192 MiB of HBM per device.

v0:
```python
from functools import partial

import jax
import jax.numpy as jnp
from jax import lax
from jax.sharding import PartitionSpec as P

GROUP_DIMENSION = 64


def layer_norm(values, gain):
    center = values - jnp.mean(values, axis=-1, keepdims=True)
    spread = jnp.mean(center * center, axis=-1, keepdims=True)
    return center / jnp.sqrt(spread + 1e-05) * gain


def head_norm(outputs, gain_rows):
    center = outputs - jnp.mean(outputs, axis=-1, keepdims=True)
    spread = jnp.mean(center * center, axis=-1, keepdims=True)
    return center / jnp.sqrt(spread + 0.00064) * gain_rows


def shifted(values, first_row):
    return jnp.concatenate([first_row[None, :], values[:-1]], axis=0)


def segment_step(extra_diagonal_term, carried_summary, piece_sequence):
    acceptance_vectors, present_lookup_vectors, content_vectors, decays = piece_sequence
    inclusive = jnp.cumsum(decays, axis=0)
    exclusive = inclusive - decays
    closing = inclusive[-1]
    resulting_activations = jnp.einsum(
        "thi,hij->thj",
        acceptance_vectors * jnp.exp(exclusive),
        carried_summary,
        precision=lax.Precision.HIGHEST,
    )
    distance = exclusive[:, None] - inclusive[None, :]
    sizing = decays.shape[0]
    earlier = (jnp.arange(sizing)[:, None] > jnp.arange(sizing)[None, :]).astype(jnp.float32)
    factor = jnp.exp(jnp.minimum(distance, 0.0)) * earlier[:, :, None, None]
    scores = jnp.sum(
        acceptance_vectors[:, None] * factor * present_lookup_vectors[None, :], axis=-1
    )
    resulting_activations = resulting_activations + jnp.einsum(
        "tsh,shj->thj", scores, content_vectors, precision=lax.Precision.HIGHEST
    )
    resulting_activations = (
        resulting_activations
        + jnp.sum(
            acceptance_vectors * extra_diagonal_term * present_lookup_vectors,
            axis=-1,
            keepdims=True,
        )
        * content_vectors
    )
    weighted = present_lookup_vectors * jnp.exp(closing[None] - inclusive)
    carried_summary = jnp.exp(closing)[:, :, None] * carried_summary + jnp.einsum(
        "shi,shj->hij", weighted, content_vectors, precision=lax.Precision.HIGHEST
    )
    return (carried_summary, resulting_activations)


def local(
    input_activations,
    prompt_extents,
    continuing_flags,
    owning_index,
    partition_arrangement,
    training_accept_pieces,
    training_lookup_pieces,
    training_content_pieces,
    normalizer_scales,
    prior_step_blends,
    forgetting_bias_vector,
    forgetting_left_lowrank,
    forgetting_right_lowrank,
    instant_emphasis,
    group_normalizer_scale,
    gating_projection,
    mixing_exit_projection,
    kept_summary_places,
    previous_normed_entries,
    feedforward_entry_proj,
    feedforward_exit_proj,
    feedforward_accept_proj,
):
    token_rows = input_activations[0]
    seq_len, width = token_rows.shape
    local_width = mixing_exit_projection.shape[0]
    groups_on_device = local_width // GROUP_DIMENSION
    shards = partition_arrangement.shape[0]
    shard_rows = width // shards
    length = prompt_extents[0]
    resuming = continuing_flags[0]
    present = jnp.arange(seq_len) < length
    gain_rows = normalizer_scales.astype(jnp.float32)
    mix_rows = prior_step_blends.astype(jnp.float32)
    carried = previous_normed_entries[0].astype(jnp.float32)
    normed_in = layer_norm(token_rows.astype(jnp.float32), gain_rows[0])
    before = shifted(normed_in, jnp.where(resuming == 1, carried[0], 0.0))
    blended = (normed_in[None] + (before - normed_in)[None] * mix_rows[:5, None, :]).astype(
        jnp.bfloat16
    )
    permuted = jnp.take(
        blended[:3].reshape(3, seq_len, shards, shard_rows), partition_arrangement, axis=2
    ).reshape(3, seq_len, width)
    local_rows = jnp.stack(
        [training_accept_pieces, training_lookup_pieces, training_content_pieces]
    ).astype(jnp.bfloat16)
    collected = lax.all_gather(local_rows, "req", axis=1, tiled=True)
    swapped = lax.all_to_all(collected, "hid", split_axis=2, concat_axis=1, tiled=True)
    hid_count = lax.axis_size("hid")
    req_count = lax.axis_size("req")
    ordered = (
        swapped.reshape(3, hid_count, req_count, shard_rows, local_width)
        .transpose(0, 2, 1, 3, 4)
        .reshape(3, width, local_width)
    )
    projected = jnp.einsum("mtd,mdc->mtc", permuted, ordered, preferred_element_type=jnp.float32)
    low_rank = jnp.tanh(
        jnp.dot(blended[3], forgetting_left_lowrank, preferred_element_type=jnp.float32)
    ).astype(jnp.bfloat16)
    log_decay = -jnp.exp(
        forgetting_bias_vector
        + jnp.dot(low_rank, forgetting_right_lowrank, preferred_element_type=jnp.float32)
    )
    log_decay = jnp.where(present[:, None], log_decay, 0.0)
    gate = jax.nn.silu(jnp.dot(blended[4], gating_projection, preferred_element_type=jnp.float32))
    present_lookup_vectors = jnp.where(present[:, None], projected[1], 0.0)
    fetched = lax.all_to_all(
        kept_summary_places.astype(jnp.bfloat16), "hid", split_axis=2, concat_axis=1, tiled=True
    ).astype(kept_summary_places.dtype)
    chosen = lax.dynamic_index_in_dim(fetched[0], owning_index[0], 0, keepdims=False)
    carried_summary = jnp.where(resuming == 1, chosen, 0.0)
    block_len = min(64, seq_len)
    count_blocks = seq_len // block_len

    def by_blocks(values):
        return values.reshape(count_blocks, block_len, groups_on_device, GROUP_DIMENSION)

    sequences = (
        by_blocks(projected[0]),
        by_blocks(present_lookup_vectors),
        by_blocks(projected[2]),
        by_blocks(log_decay),
    )
    segment_cursor = partial(
        segment_step, instant_emphasis.reshape(groups_on_device, GROUP_DIMENSION)
    )
    carried_summary, outputs = lax.scan(segment_cursor, carried_summary, sequences)
    outputs = outputs.reshape(seq_len, groups_on_device, GROUP_DIMENSION)
    grouped = head_norm(
        outputs, group_normalizer_scale.reshape(groups_on_device, GROUP_DIMENSION)
    ).reshape(seq_len, local_width)
    gated = (grouped * gate).astype(jnp.bfloat16)
    head_terms = jnp.dot(gated, mixing_exit_projection, preferred_element_type=jnp.float32)
    attended = lax.psum(head_terms.astype(jnp.bfloat16), "hid").astype(jnp.float32)
    middle = (token_rows.astype(jnp.float32) + attended).astype(jnp.bfloat16)
    mid_share = lax.dynamic_slice_in_dim(
        middle, lax.axis_index("hid") * local_width, local_width, 1
    )
    chan_in = layer_norm(middle.astype(jnp.float32), gain_rows[1])
    chan_before = shifted(chan_in, jnp.where(resuming == 1, carried[1], 0.0))
    chan_mixed = (chan_in[None] + (chan_before - chan_in)[None] * mix_rows[5:, None, :]).astype(
        jnp.bfloat16
    )
    key_rows = lax.all_gather(feedforward_entry_proj, "req", axis=0, tiled=True)
    value_rows = lax.all_gather(feedforward_exit_proj, "req", axis=0, tiled=True)
    inner = lax.dot_general(
        chan_mixed[0], key_rows, (((1,), (1,)), ((), ())), preferred_element_type=jnp.float32
    )
    hidden = jnp.square(jnp.maximum(inner, 0.0)).astype(jnp.bfloat16)
    channel_terms = jnp.dot(hidden, value_rows, preferred_element_type=jnp.float32)
    mixed_out = lax.psum_scatter(
        channel_terms.astype(jnp.bfloat16), "hid", scatter_dimension=1, tiled=True
    ).astype(jnp.float32)
    gate_rows = jax.nn.sigmoid(
        jnp.dot(chan_mixed[1], feedforward_accept_proj, preferred_element_type=jnp.float32)
    )
    combined = mid_share.astype(jnp.float32) + gate_rows * mixed_out
    layer_out = jnp.where(present[:, None], combined, 0.0).astype(jnp.bfloat16)[None]
    last_index = length - 1
    shift_out = jnp.stack(
        [
            lax.dynamic_index_in_dim(normed_in, last_index, 0, keepdims=False),
            lax.dynamic_index_in_dim(chan_in, last_index, 0, keepdims=False),
        ]
    ).astype(jnp.bfloat16)[None]
    return (layer_out, carried_summary[None], shift_out)


def solution(mesh):
    placed = (
        P("req", None, None),
        P("req"),
        P("req"),
        P("req"),
        P(),
        P(("req", "hid"), None),
        P(("req", "hid"), None),
        P(("req", "hid"), None),
        P(),
        P(),
        P("hid"),
        P(),
        P(None, "hid"),
        P("hid"),
        P("hid"),
        P(None, "hid"),
        P("hid", None),
        P("req", "hid", None, None, None),
        P("req", None, None),
        P(("req", "hid"), None),
        P(("req", "hid"), None),
        P(None, "hid"),
    )
    return jax.shard_map(
        local,
        mesh=mesh,
        in_specs=placed,
        out_specs=(P("req", None, "hid"), P("req", "hid", None, None), P("req", None, None)),
        check_vma=False,
    )
```

profile of v0, /device:TPU:0, one launch (start us, length us, event | category | flops | bytes accessed | tf_op | source)
XLA Modules:
  0.0 817.2 jit_solution(10165721648546910749)
XLA Ops:
  7.2 1.2 convert_bitcast_fusion.3
  8.4 1.3 convert_bitcast_fusion.1
  10.7 1.8 fusion.60
  12.5 1.5 reshape.260
  14.0 6.5 all-to-all-start
  21.4 3.4 convert_reduce_fusion
  24.8 3.4 fusion.19
  28.3 1.8 fusion.20
  30.2 4.1 slice_bitcast_fusion.1
  34.3 1.7 copy-done.5
  36.6 69.1 %all-gather.4.cloned.1.call-done = bf16[3,256,4096]{2,1,0:T(8,128)(2,1)} async-done(((bf16[3,32,4096]{2,1,0:T(8,128)(2,1)}), bf16[3,256,4096]{2,1,0:T(8,128)(2,1)}) %all-gather.4.cloned.1.call-update) | async-done | bytes 6291472 | tf_op jit(solution)/shard_map/all_gather | solution.py:111
  105.7 13.1 %copy.123 = bf16[3,256,4096]{1,0,2:T(4,128)(2,1)} copy(bf16[3,256,4096]{2,1,0:T(8,128)(2,1)} %all-gather.4.cloned.1.call-done) | data formatting | bytes 12582912 | tf_op jit(solution)/shard_map/all_gather | solution.py:111
  118.8 4.8 all-to-all-start.1
  123.9 10.4 %fusion.27 = (f32[512,4096]{1,0:T(8,128)}, f32[512,4096]{1,0:T(8,128)}) fusion(bf16[1,512,4096]{2,1,0:T(8,128)(2,1)} %param.24, f32[4096]{0:T(1024)S(1)} %bitcast.201, f32[512]{0:T(512)S(1)} %add_sqrt_fusion.1, f32[512]{0:T(512)S(1)} %broadcast_multiply_fusion.1, f32[1,511,4096]{2,1,0:T(8,128)} %slice_bitcast_fusion.1, f32[1,1,4096]{2,1,0:T(1,128)S(1)} %get-tuple-element.126), kind=kLoop, calls=%fused_computation.55 | loop fusion | flops 12582912 | bytes 29380608 | tf_op jit(solution)/shard_map/add | solution.py:102
  134.3 9.0 %copy.120 = f32[512,4096]{0,1:T(8,128)} copy(f32[512,4096]{1,0:T(8,128)} %get-tuple-element.120) | data formatting | bytes 16777216 | tf_op jit(solution)/shard_map/add | solution.py:102
  143.3 9.0 %copy.121 = f32[512,4096]{0,1:T(8,128)} copy(f32[512,4096]{1,0:T(8,128)} %get-tuple-element.121) | data formatting | bytes 16777216 | tf_op jit(solution)/shard_map/mul | solution.py:102
  152.4 10.3 %add_convert_fusion = bf16[5,512,4096]{1,2,0:T(8,128)(2,1)S(1)} fusion(f32[5,4096]{1,0:T(8,128)S(1)} %slice.75, f32[512,4096]{0,1:T(8,128)} %copy.121, f32[512,4096]{0,1:T(8,128)} %copy.120), kind=kLoop, calls=%fused_computation.28 | loop fusion | flops 31457280 | bytes 37830656 | tf_op jit(solution)/shard_map/convert_element_type | solution.py:102
  162.7 6.5 slice.77
  169.2 4.2 copy-done.4
  173.4 12.8 %gather_fusion = bf16[128,3,512,32]{2,3,1,0:T(8,128)(2,1)} fusion(bf16[3,512,128,32]{1,3,2,0:T(8,128)(2,1)} %bitcast.190, s32[1024]{0:T(1024)S(1)} %pad_clamp_fusion), kind=kCustom, calls=%fused_computation | custom fusion | bytes 25166336 | tf_op jit(solution)/shard_map/jit(_take)/gather | solution.py:105
  186.2 10.7 %copy.122 = bf16[3,512,128,32]{1,3,2,0:T(8,128)(2,1)} copy(bf16[3,512,128,32]{1,3,0,2:T(8,128)(2,1)} %bitcast.191) | data formatting | bytes 25165824 | tf_op jit(solution)/shard_map/jit(_take)/gather | solution.py:105
  197.8 3.9 fusion.34
  201.8 1.5 reshape.245
  204.5 11.2 %bitcast_select_fusion = bf16[3,512,4096]{1,2,0:T(8,128)(2,1)} fusion(bf16[3,512,128,32]{1,3,2,0:T(8,128)(2,1)} %copy.122, pred[4096]{0:T(1024)(128)(4,1)S(1)} %broadcast_in_dim.95), kind=kLoop, calls=%fused_computation.30 | loop fusion | flops 6291456 | bytes 25169920 | tf_op jit(solution)/shard_map/jit(_take)/select_n | solution.py:105
  215.6 1.7 reshape.261
  218.2 27.1 %all-to-all-done.1 = bf16[3,256,4096]{1,0,2:T(4,128)(2,1)} async-done(((bf16[3,256,4096]{1,0,2:T(4,128)(2,1)}), bf16[3,256,4096]{1,0,2:T(4,128)(2,1)}, u32[]{:S(2)}, u32[]{:S(2)}) %all-to-all-start.1) | async-done | bytes 6291488 | tf_op jit(solution)/shard_map/all_to_all | solution.py:112
  245.3 6.9 copy.124
  252.2 9.1 %copy.125 = bf16[3,16,256,256]{3,2,1,0:T(8,128)(2,1)} copy(bf16[3,16,256,256]{2,3,1,0:T(8,128)(2,1)} %bitcast.193) | data formatting | bytes 12582912 | tf_op jit(solution)/shard_map/all_to_all | solution.py:112
  261.2 6.5 copy.126
  267.7 12.0 %fusion.61 = f32[3,512,256]{2,1,0:T(8,128)} fusion(bf16[3,512,4096]{1,2,0:T(8,128)(2,1)} %bitcast_select_fusion, bf16[3,4096,256]{2,1,0:T(8,128)(2,1)} %bitcast.196), kind=kOutput, calls=%fused_computation.119 | convolution fusion | flops 3221225472 | bytes 20447232 | tf_op jit(solution)/shard_map/mtd,mdc->mtc/dot_general | solution.py:120
  279.7 2.6 fusion.58
  282.2 1.5 squeeze.51
  283.7 2.5 reshape_squeeze.6
  286.2 2.4 reshape_squeeze.7
  288.6 1.5 broadcast_select_fusion
  290.1 79.8 %while.12 = (s32[]{:T(128)}, f32[4,64,64]{2,1,0:T(8,128)S(1)}, f32[8,64,4,64]{3,1,2,0:T(8,128)}, f32[8,64,4,64]{3,2,1,0:T(4,128)}, f32[8,64,4,64]{3,2,1,0:T(4,12...) while((s32[]{:T(128)}, f32[4,64,64]{2,1,0:T(8,128)S(1)}, ...), condition=%wide.region_6.7_spmd, body=%wide.region_2.6_spmd.sunk | while | flops 45260544 | bytes 2537577 | solution.py:151
  290.8 1.1 multiply_reduce_fusion.5
  294.0 3.4 multiply_reduce_fusion.6
  304.0 3.4 multiply_reduce_fusion.6
  310.7 1.1 multiply_reduce_fusion.5
  313.9 3.4 multiply_reduce_fusion.6
  323.9 3.4 multiply_reduce_fusion.6
  333.8 3.4 multiply_reduce_fusion.6
  343.8 3.4 multiply_reduce_fusion.6
  350.5 1.1 multiply_reduce_fusion.5
  353.7 3.4 multiply_reduce_fusion.6
  360.5 1.1 multiply_reduce_fusion.5
  363.7 3.4 multiply_reduce_fusion.6
  369.9 2.0 copy.130
  371.8 1.6 reduce_sum.74
  373.5 1.4 reshape.249
  374.9 1.9 multiply_reduce_fusion.2
  378.2 9.6 %convolution_convert_fusion.1 = bf16[512,4096]{1,0:T(8,128)(2,1)} fusion(bf16[256,4096]{1,0:T(8,128)(2,1)S(1)} %copy-done, bf16[4096,256]{1,0:T(8,128)(2,1)} %param.39, bf16[5,512,4096]{1,2,0:T(8,128)(2,1)} %copy-done.4, f32[512,256]{1,0:T(8,128)S(1)} %copy.135, f32[512,256]{1,0:T(8,128)} %reshape.249, f32[512,256]{1,0:T(8,128)} %copy.132, ...), kind=kOutput, calls=%fused_computation.54 | convolution fusion | flops 2150760448 | bytes 14156800 | tf_op jit(solution)/shard_map/dot_general | solution.py:157
  389.2 133.6 %all-reduce.2.cloned.1.call-done = bf16[512,4096]{1,0:T(8,128)(2,1)} async-done(((bf16[512,4096]{1,0:T(8,128)(2,1)}), bf16[512,4096]{1,0:T(8,128)(2,1)}) %all-reduce.2.cloned.1.call-update) | async-done | bytes 4194320 | tf_op jit(solution)/shard_map/psum | solution.py:158
  522.8 5.2 convert_reduce_fusion.1
  528.0 1.2 fusion.21
  529.3 2.1 fusion.22
  531.4 3.5 maximum_subtract_fusion.1
  534.9 4.8 add_convert_fusion.1
  539.7 85.3 %all-gather.6.cloned.1.call-done = bf16[896,4096]{1,0:T(8,128)(2,1)} async-done(((bf16[112,4096]{1,0:T(8,128)(2,1)}), bf16[896,4096]{1,0:T(8,128)(2,1)}) %all-gather.6.cloned.1.call-update) | async-done | bytes 7340048 | tf_op jit(solution)/shard_map/all_gather | solution.py:168
  625.0 99.4 %all-gather.8.cloned.1.call-done = bf16[896,4096]{1,0:T(8,128)(2,1)} async-done(((bf16[112,4096]{1,0:T(8,128)(2,1)}), bf16[896,4096]{1,0:T(8,128)(2,1)}) %all-gather.8.cloned.1.call-update) | async-done | bytes 7340048 | tf_op jit(solution)/shard_map/all_gather | solution.py:169
  724.4 16.2 %convolution_convert_fusion = bf16[512,4096]{1,0:T(8,128)(2,1)} fusion(bf16[896,4096]{1,0:T(8,128)(2,1)} %all-gather.8.cloned.1.call-done, bf16[896,4096]{1,0:T(8,128)(2,1)} %all-gather.6.cloned.1.call-done, bf16[2,512,4096]{2,1,0:T(8,128)(2,1)} %add_convert_fusion.1), kind=kOutput, calls=%fused_computation.53 | convolution fusion | flops 7519666176 | bytes 23068672 | tf_op jit(solution)/shard_map/dot_general | solution.py:174
  743.1 62.5 %reduce-scatter.2.cloned.1.call-done = bf16[512,256]{1,0:T(8,128)(2,1)} async-done(((bf16[512,4096]{1,0:T(8,128)(2,1)}), bf16[512,256]{1,0:T(8,128)(2,1)}) %reduce-scatter.2.cloned.1.call-update) | async-done | bytes 262160 | tf_op jit(solution)/shard_map/reduce_scatter | solution.py:175
  805.6 4.9 fusion.45
  (186 shorter events, 56.6 us)
Async XLA Ops:
  7.2 371.1 %copy-start = (bf16[256,4096]{1,0:T(8,128)(2,1)S(1)}, bf16[256,4096]{1,0:T(8,128)(2,1)}, u32[]{:S(2)}) copy-start(bf16[256,4096]{1,0:T(8,128)(2,1)} %param.40) | copy-start | bytes 6291460
  7.2 14.2 %copy-start.11 = (bf16[1,2,4096]{2,1,0:T(2,128)(2,1)S(1)}, bf16[1,2,4096]{2,1,0:T(2,128)(2,1)}, u32[]{:S(2)}) copy-start(bf16[1,2,4096]{2,1,0:T(2,128)(2,1)} %param.42) | copy-start | bytes 49156
  7.2 98.5 %all-gather.4.cloned.1.call-start = ((), (), s32[]{:S(2)}) async-start(), calls=%async_computation.3 | async-start | bytes 7077888 | tf_op jit(solution)/shard_map/all_gather | solution.py:111
  9.7 18.6 %copy-start.9 = (bf16[2,4096]{1,0:T(2,128)(2,1)S(1)}, bf16[2,4096]{1,0:T(2,128)(2,1)}, u32[]{:S(2)}) copy-start(bf16[2,4096]{1,0:T(2,128)(2,1)} %param.32) | copy-start | bytes 49156
  14.0 104.8 %all-to-all-start = ((bf16[16,2,8192]{2,1,0:T(2,128)(2,1)}), bf16[16,2,8192]{2,1,0:T(2,128)(2,1)S(1)}, u32[]{:S(2)}, u32[]{:S(2)}) async-start(bf16[16,2,8192]{2,1,0:T(2,128)(2,1)} %reshape.260), calls=%async_computation | async-start | bytes 1048576 | tf_op jit(solution)/shard_map/all_to_all | solution.py:131
  20.6 7.8 copy-start.1
  30.2 5.8 copy-start.5
  118.8 126.4 %all-to-all-start.1 = ((bf16[3,256,4096]{1,0,2:T(4,128)(2,1)}), bf16[3,256,4096]{1,0,2:T(4,128)(2,1)}, u32[]{:S(2)}, u32[]{:S(2)}) async-start(bf16[3,256,4096]{1,0,2:T(4,128)(2,1)} %copy.123), calls=%async_computation.1 | async-start | bytes 16777216 | tf_op jit(solution)/shard_map/all_to_all | solution.py:112
  123.6 399.2 %all-reduce.2.cloned.1.call-start = ((), (), s32[]{:S(2)}) async-start(), calls=%async_computation.4 | async-start | bytes 8388608 | tf_op jit(solution)/shard_map/psum | solution.py:158
  143.3 9.0 %copy-start.7 = (bf16[7,4096]{1,0:T(8,128)(2,1)S(1)}, bf16[7,4096]{1,0:T(8,128)(2,1)}, u32[]{:S(2)}) copy-start(bf16[7,4096]{1,0:T(8,128)(2,1)} %param.33) | copy-start | bytes 172036
  162.7 10.7 %copy-start.4 = (bf16[5,512,4096]{1,2,0:T(8,128)(2,1)}, bf16[5,512,4096]{1,2,0:T(8,128)(2,1)S(1)}, u32[]{:S(2)}) copy-start(bf16[5,512,4096]{1,2,0:T(8,128)(2,1)S(1)} %add_convert_fusion) | copy-start | bytes 62914564
  162.7 10.7 %copy-start.16 = (s32[128]{0:T(128)S(1)}, s32[128]{0:T(128)}, u32[]{:S(2)}) copy-start(s32[128]{0:T(128)} %param.28) | copy-start | bytes 1540
  186.2 11.6 %copy-start.13 = (bf16[128,256]{1,0:T(8,128)(2,1)S(1)}, bf16[128,256]{1,0:T(8,128)(2,1)}, u32[]{:S(2)}) copy-start(bf16[128,256]{1,0:T(8,128)(2,1)} %param.36) | copy-start | bytes 196612
  186.2 11.6 %copy-start.14 = (f32[256]{0:T(256)S(1)}, f32[256]{0:T(256)}, u32[]{:S(2)}) copy-start(f32[256]{0:T(256)} %param.34) | copy-start | bytes 3076
  197.8 17.8 %copy-start.17 = (pred[512]{0:T(512)(128)(4,1)}, pred[512]{0:T(512)(128)(4,1)S(1)}, u32[]{:S(2)}) copy-start(pred[512]{0:T(512)(128)(4,1)S(1)} %iota_compare_fusion.1) | copy-start | bytes 1540
  267.7 20.9 %copy-start.12 = (pred[8,64]{1,0:T(8,128)(4,1)S(1)}, pred[8,64]{1,0:T(8,128)(4,1)}, u32[]{:S(2)}) copy-start(pred[8,64]{1,0:T(8,128)(4,1)} %add_compare_fusion) | copy-start | bytes 1540
  369.8 18.0 %copy-start.6 = (f32[4,64,64]{2,1,0:T(8,128)}, f32[4,64,64]{2,1,0:T(8,128)S(1)}, u32[]{:S(2)}) copy-start(f32[4,64,64]{2,1,0:T(8,128)S(1)} %get-tuple-element.47) | copy-start | bytes 196612
  369.9 8.4 %copy-start.15 = (f32[256]{0:T(256)S(1)}, f32[256]{0:T(256)}, u32[]{:S(2)}) copy-start(f32[256]{0:T(256)} %param.38) | copy-start | bytes 3076
  378.2 11.0 %copy-start.8 = (bf16[7,4096]{1,0:T(8,128)(2,1)S(1)}, bf16[7,4096]{1,0:T(8,128)(2,1)}, u32[]{:S(2)}) copy-start(bf16[7,4096]{1,0:T(8,128)(2,1)} %param.33) | copy-start | bytes 172036
  387.8 237.2 %all-gather.6.cloned.1.call-start = ((), (), s32[]{:S(2)}) async-start(), calls=%async_computation.5 | async-start | bytes 8257536 | tf_op jit(solution)/shard_map/all_gather | solution.py:168
  388.6 335.8 %all-gather.8.cloned.1.call-start = ((), (), s32[]{:S(2)}) async-start(), calls=%async_computation.6 | async-start | bytes 8257536 | tf_op jit(solution)/shard_map/all_gather | solution.py:169
  389.1 416.5 %reduce-scatter.2.cloned.1.call-start = ((), (), s32[]{:S(2)}) async-start(), calls=%async_computation.7 | async-start | bytes 4456448 | tf_op jit(solution)/shard_map/reduce_scatter | solution.py:175
  528.0 3.4 copy-start.3
  528.0 3.4 copy-start.10
  531.4 3.5 copy-start.2
  539.7 265.9 %copy-start.18 = (pred[512]{0:T(512)(128)(4,1)S(1)}, pred[512]{0:T(512)(128)(4,1)}, u32[]{:S(2)}) copy-start(pred[512]{0:T(512)(128)(4,1)} %copy-done.17) | copy-start | bytes 1540
Sparse Core Ops, SparseCore 0:
  10.8 94.8 all-gather.3
  388.0 134.8 all-reduce.1
  525.1 99.8 all-gather.5
  627.2 97.1 all-gather.7
  740.7 64.8 reduce-scatter.1
where the time goes:
time: 824 us; the launch traced here: 817 us
  waiting for transfers between devices  478 us (58%)
  local copies, waits for them, and re-layouts  128 us (16%)
  other arithmetic  122 us (15%)
  matrix products  59.2 us (7%)
  between operations  16.6 us (2%)
  starting transfers between devices  11.8 us (1%)
    psum x1, waiting for transfers between devices, local(): lax.psum(head_terms.astype(jnp.bfloat16), 'hid').astype(jnp.float32)  134 us
    all_gather x1, waiting for transfers between devices, local(): lax.all_gather(feedforward_exit_proj, 'req', axis=0, tiled=True)  99.4 us
    all_gather x1, waiting for transfers between devices, local(): key_rows = lax.all_gather(feedforward_entry_proj, 'req', axis=0, tiled=True)  85.3 us
    all_gather x1, waiting for transfers between devices, local(): collected = lax.all_gather(local_rows, 'req', axis=1, tiled=True)  69.1 us
    reduce_scatter x1, waiting for transfers between devices, local(): lax.psum_scatter(channel_terms.astype(jnp.bfloat16), 'hid', scatter_dimen...  62.5 us
    all_to_all x1, waiting for transfers between devices, local(): lax.all_to_all(collected, 'hid', split_axis=2, concat_axis=1, tiled=True)  27.1 us
    reduce_sum x8, other arithmetic, segment_step(): jnp.sum(acceptance_vectors[:, None] * factor * present_lookup_vectors[Non...  27 us
    gather x2, local copies, waits for them, and re-layouts, local(): jnp.take(blended[:3].reshape(3, seq_len, shards, shard_rows), partition_a...  23.5 us
  transfers between devices with their start and end apart: 7, of which 6 were waited for; matrix products, arithmetic and copies ran while one was open for 17% of the time, Pallas kernels for 0%

commit v1 on v0

v1 whole, which is shorter than its diff:
```python
from functools import partial

import jax
import jax.numpy as jnp
from jax import lax
from jax.experimental import pallas as pl
from jax.experimental.pallas import tpu as pltpu
from jax.sharding import PartitionSpec as P

HEAD = 64
CHUNK = 16
TILE = 64
PAIR = 128
KC = 512
VMEM_LIMIT = 58 * 1024 * 1024
F32 = jnp.float32
BF16 = jnp.bfloat16
VM = pl.BlockSpec(memory_space=pltpu.VMEM)
SM = pl.BlockSpec(memory_space=pltpu.SMEM)
HB = pl.BlockSpec(memory_space=pl.ANY)


def nt_dot(a, b):
    return lax.dot_general(a, b, (((1,), (1,)), ((), ())), preferred_element_type=F32)


def tn_dot(a, b):
    return lax.dot_general(a, b, (((0,), (0,)), ((), ())), preferred_element_type=F32)


def nn_dot(a, b):
    return jnp.dot(a, b, preferred_element_type=F32)


def row_stats(x_ref, eps):
    rows, width = x_ref.shape

    def add_sum(c, total):
        part = x_ref[:, pl.ds(pl.multiple_of(c * KC, KC), KC)].astype(F32)
        return total + jnp.sum(part, axis=1, keepdims=True)

    def add_square(c, total):
        part = x_ref[:, pl.ds(pl.multiple_of(c * KC, KC), KC)].astype(F32) - mean
        return total + jnp.sum(part * part, axis=1, keepdims=True)

    zero = jnp.zeros((rows, 1), F32)
    mean = lax.fori_loop(0, width // KC, add_sum, zero) / width
    var = lax.fori_loop(0, width // KC, add_square, zero) / width
    return mean, 1.0 / jnp.sqrt(var + eps)


def normed_and_delta(x_ref, first_ref, gain_ref, which, cols, mean, inv):
    part = x_ref[:, cols].astype(F32)
    normed = (part - mean) * inv * gain_ref[:, cols].astype(F32)[which : which + 1]
    before = pltpu.roll(normed, 1, 0)
    row = lax.broadcasted_iota(jnp.int32, normed.shape, 0)
    before = jnp.where(row == 0, first_ref[:, cols], before)
    return normed, before - normed


def time_mix_kernel(
    perm_ref, len_ref, x_ref, first_ref, gain_ref, mix_ref, w_ref, gating_ref, left_ref,
    right_ref, bias_ref, bonus_ref, gscale_ref, s0_ref, exit_ref,
    terms_ref, state_ref,
    w_scr, acc, acc_low, acc_gate, logw_scr, prod_scr, gated_scr, st_scr, sem,
):
    rows, width = x_ref.shape
    blocks = w_scr.shape[0]
    block_rows = w_scr.shape[1]
    lw = acc_gate.shape[1]

    def start(j, carry):
        pltpu.make_async_copy(w_ref.at[j], w_scr.at[perm_ref[j]], sem).start()
        return carry

    lax.fori_loop(0, blocks, start, 0)
    mean, inv = row_stats(x_ref, 1e-05)
    acc[...] = jnp.zeros_like(acc)
    acc_low[...] = jnp.zeros_like(acc_low)
    acc_gate[...] = jnp.zeros_like(acc_gate)
    pltpu.make_async_copy(w_ref, w_scr, sem).wait()
    per = KC // block_rows

    def project(c, carry):
        cols = pl.ds(pl.multiple_of(c * KC, KC), KC)
        normed, delta = normed_and_delta(x_ref, first_ref, gain_ref, 0, cols, mean, inv)
        mix = mix_ref[:, cols].astype(F32)

        def blend(m):
            return (normed + delta * mix[m : m + 1]).astype(BF16)

        for m in range(3):
            wm = w_scr[pl.ds(c * per, per), :, m * lw : (m + 1) * lw].reshape(KC, lw)
            acc[:, m * lw : (m + 1) * lw] += nn_dot(blend(m), wm)
        acc_low[...] += nn_dot(blend(3), left_ref[cols, :])
        acc_gate[...] += nn_dot(blend(4), gating_ref[cols, :])
        return carry

    lax.fori_loop(0, width // KC, project, 0)
    length = len_ref[0]
    present = lax.broadcasted_iota(jnp.int32, (rows, lw), 0) < length
    low = jnp.tanh(acc_low[...]).astype(BF16)
    log_decay = -jnp.exp(bias_ref[...] + nn_dot(low, right_ref[...]))
    logw_scr[...] = jnp.where(present, log_decay, 0.0)
    acc[:, lw : 2 * lw] = jnp.where(present, acc[:, lw : 2 * lw], 0.0)

    pairs = lw // PAIR
    hole = jnp.zeros((HEAD, HEAD), F32)
    for p in range(pairs):
        top = jnp.concatenate([s0_ref[2 * p], hole], axis=1)
        bottom = jnp.concatenate([hole, s0_ref[2 * p + 1]], axis=1)
        st_scr[p] = jnp.concatenate([top, bottom], axis=0).T

    def same_head(size):
        a = lax.broadcasted_iota(jnp.int32, (size, size), 0) // HEAD
        b = lax.broadcasted_iota(jnp.int32, (size, size), 1) // HEAD
        return a == b

    ones = jnp.where(same_head(lw), 1.0, 0.0).astype(BF16)
    pair_mask = same_head(PAIR)
    slot = lax.broadcasted_iota(jnp.int32, (TILE, lw), 0) % CHUNK

    def head_sum(values):
        high = values.astype(BF16)
        rest = (values - high.astype(F32)).astype(BF16)
        return nn_dot(high, ones) + nn_dot(rest, ones)

    def tile_step(t, carry):
        here = pl.ds(pl.multiple_of(t * TILE, TILE), TILE)
        r = acc[here, 0:lw]
        k = acc[here, lw : 2 * lw]
        v = acc[here, 2 * lw : 3 * lw]
        decay = logw_scr[here, :]
        incl = decay
        step = 1
        while step < CHUNK:
            incl = incl + jnp.where(slot >= step, pltpu.roll(incl, step, 0), 0.0)
            step *= 2
        excl = incl - decay
        prod_scr[0:TILE, :] = (r * bonus_ref[...] * k).astype(BF16)
        for d in range(1, CHUNK):
            gap = jnp.minimum(excl - pltpu.roll(incl, d, 0), 0.0)
            term = jnp.where(slot >= d, r * pltpu.roll(k, d, 0) * jnp.exp(gap), 0.0)
            prod_scr[d * TILE : (d + 1) * TILE, :] = term.astype(BF16)
        scores = nn_dot(prod_scr[...], ones)
        out = scores[0:TILE] * v
        for d in range(1, CHUNK):
            out = out + scores[d * TILE : (d + 1) * TILE] * pltpu.roll(v, d, 0)
        rw = (r * jnp.exp(excl)).astype(BF16)
        vb = v.astype(BF16)
        pieces = []
        for c in range(TILE // CHUNK):
            lo, hi = c * CHUNK, (c + 1) * CHUNK
            closing = incl[hi - 1 : hi]
            kw = (k[lo:hi] * jnp.exp(closing - incl[lo:hi])).astype(BF16)
            fade = jnp.exp(closing)
            parts = []
            for p in range(pairs):
                a, b = p * PAIR, (p + 1) * PAIR
                st = st_scr[p]
                parts.append(nt_dot(rw[lo:hi, a:b], st.astype(BF16)))
                grown = tn_dot(vb[lo:hi, a:b], kw[:, a:b])
                st_scr[p] = st * fade[:, a:b] + jnp.where(pair_mask, grown, 0.0)
            pieces.append(jnp.concatenate(parts, axis=1))
        out = out + jnp.concatenate(pieces, axis=0)
        center = out - head_sum(out) * (1.0 / HEAD)
        spread = head_sum(center * center) * (1.0 / HEAD)
        grouped = center / jnp.sqrt(spread + 0.00064) * gscale_ref[...]
        g = acc_gate[here, :]
        gate = g / (1.0 + jnp.exp(-g))
        gated_scr[here, :] = (grouped * gate).astype(BF16)
        return carry

    lax.fori_loop(0, rows // TILE, tile_step, 0)
    for p in range(pairs):
        full = st_scr[p].T
        state_ref[2 * p] = full[0:HEAD, 0:HEAD]
        state_ref[2 * p + 1] = full[HEAD:PAIR, HEAD:PAIR]

    def leave(c, carry):
        cols = pl.ds(pl.multiple_of(c * KC, KC), KC)
        terms_ref[:, cols] = nn_dot(gated_scr[...], exit_ref[:, cols]).astype(BF16)
        return carry

    lax.fori_loop(0, width // KC, leave, 0)


def time_mix(perm, length, x, first, gains, mixes, w, gating, left, right, bias, bonus, gscale, s0, exit_w):
    rows, width = x.shape
    lw = gating.shape[1]
    return pl.pallas_call(
        time_mix_kernel,
        out_shape=(
            jax.ShapeDtypeStruct((rows, width), BF16),
            jax.ShapeDtypeStruct(s0.shape, F32),
        ),
        in_specs=[SM, SM, VM, VM, VM, VM, HB] + [VM] * 8,
        out_specs=(VM, VM),
        scratch_shapes=[
            pltpu.VMEM(w.shape, BF16),
            pltpu.VMEM((rows, 3 * lw), F32),
            pltpu.VMEM((rows, left.shape[1]), F32),
            pltpu.VMEM((rows, lw), F32),
            pltpu.VMEM((rows, lw), F32),
            pltpu.VMEM((CHUNK * TILE, lw), BF16),
            pltpu.VMEM((rows, lw), BF16),
            pltpu.VMEM((lw // PAIR, PAIR, PAIR), F32),
            pltpu.SemaphoreType.DMA,
        ],
        compiler_params=pltpu.CompilerParams(vmem_limit_bytes=VMEM_LIMIT),
        name="time_mix",
    )(perm, length, x, first, gains, mixes, w, gating, left, right, bias, bonus, gscale, s0, exit_w)


def channel_mix_kernel(
    x_ref, first_ref, gain_ref, mix_ref, accept_ref, key_ref, value_ref,
    terms_ref, gate_ref,
    key_scr, value_scr, inner, acc_gate, hidden, sems,
):
    width = x_ref.shape[1]
    key_copy = pltpu.make_async_copy(key_ref, key_scr, sems.at[0])
    value_copy = pltpu.make_async_copy(value_ref, value_scr, sems.at[1])
    key_copy.start()
    value_copy.start()
    mean, inv = row_stats(x_ref, 1e-05)
    inner[...] = jnp.zeros_like(inner)
    acc_gate[...] = jnp.zeros_like(acc_gate)
    key_copy.wait()

    def project(c, carry):
        cols = pl.ds(pl.multiple_of(c * KC, KC), KC)
        normed, delta = normed_and_delta(x_ref, first_ref, gain_ref, 1, cols, mean, inv)
        mix = mix_ref[:, cols].astype(F32)
        inner[...] += nt_dot((normed + delta * mix[5:6]).astype(BF16), key_scr[:, cols])
        acc_gate[...] += nn_dot((normed + delta * mix[6:7]).astype(BF16), accept_ref[cols, :])
        return carry

    lax.fori_loop(0, width // KC, project, 0)
    positive = jnp.maximum(inner[...], 0.0)
    hidden[...] = (positive * positive).astype(BF16)
    gate_ref[...] = jax.nn.sigmoid(acc_gate[...])
    value_copy.wait()

    def leave(c, carry):
        cols = pl.ds(pl.multiple_of(c * KC, KC), KC)
        terms_ref[:, cols] = nn_dot(hidden[...], value_scr[:, cols]).astype(BF16)
        return carry

    lax.fori_loop(0, width // KC, leave, 0)


def channel_mix(x, first, gains, mixes, accept, key_rows, value_rows):
    rows, width = x.shape
    lw = accept.shape[1]
    units = key_rows.shape[0]
    return pl.pallas_call(
        channel_mix_kernel,
        out_shape=(
            jax.ShapeDtypeStruct((rows, width), BF16),
            jax.ShapeDtypeStruct((rows, lw), F32),
        ),
        in_specs=[VM] * 5 + [HB] * 2,
        out_specs=(VM, VM),
        scratch_shapes=[
            pltpu.VMEM(key_rows.shape, BF16),
            pltpu.VMEM(value_rows.shape, BF16),
            pltpu.VMEM((rows, units), F32),
            pltpu.VMEM((rows, lw), F32),
            pltpu.VMEM((rows, units), BF16),
            pltpu.SemaphoreType.DMA((2,)),
        ],
        compiler_params=pltpu.CompilerParams(vmem_limit_bytes=VMEM_LIMIT),
        name="channel_mix",
    )(x, first, gains, mixes, accept, key_rows, value_rows)


def norm_row(row, gain):
    center = row - jnp.mean(row)
    return center / jnp.sqrt(jnp.mean(center * center) + 1e-05) * gain


def local(
    input_activations,
    prompt_extents,
    continuing_flags,
    owning_index,
    partition_arrangement,
    training_accept_pieces,
    training_lookup_pieces,
    training_content_pieces,
    normalizer_scales,
    prior_step_blends,
    forgetting_bias_vector,
    forgetting_left_lowrank,
    forgetting_right_lowrank,
    instant_emphasis,
    group_normalizer_scale,
    gating_projection,
    mixing_exit_projection,
    kept_summary_places,
    previous_normed_entries,
    feedforward_entry_proj,
    feedforward_exit_proj,
    feedforward_accept_proj,
):
    x = input_activations[0]
    rows, width = x.shape
    lw = mixing_exit_projection.shape[0]
    hid = lax.axis_size("hid")
    block_rows = training_accept_pieces.shape[0]
    length = prompt_extents[0]
    resuming = continuing_flags[0]
    gains = normalizer_scales.astype(F32)
    carried = jnp.where(resuming == 1, previous_normed_entries[0].astype(F32), 0.0)

    own = jnp.stack([training_accept_pieces, training_lookup_pieces, training_content_pieces])
    own = own.astype(BF16).reshape(3, block_rows, hid, lw).transpose(2, 1, 0, 3)
    own = own.reshape(hid, block_rows, 3 * lw)
    swapped = lax.all_to_all(own, "hid", split_axis=0, concat_axis=0, tiled=True)
    fetched = lax.all_to_all(
        kept_summary_places[0, 0].astype(BF16).reshape(hid, -1, HEAD, HEAD),
        "hid", split_axis=0, concat_axis=0, tiled=True,
    )
    chosen = lax.dynamic_index_in_dim(fetched, owning_index[0], 0, keepdims=False)
    s0 = jnp.where(resuming == 1, chosen.astype(F32), 0.0)
    w = lax.all_gather(swapped, "req", axis=0, tiled=True)
    entry, w = lax.optimization_barrier((feedforward_entry_proj, w))
    key_rows = lax.all_gather(entry, "req", axis=0, tiled=True)
    exit_proj, w = lax.optimization_barrier((feedforward_exit_proj, w))
    value_rows = lax.all_gather(exit_proj, "req", axis=0, tiled=True)

    terms, state = time_mix(
        partition_arrangement, prompt_extents, x, carried[0:1], gains, prior_step_blends, w,
        gating_projection, forgetting_left_lowrank, forgetting_right_lowrank,
        forgetting_bias_vector[None], instant_emphasis[None], group_normalizer_scale[None],
        s0, mixing_exit_projection,
    )
    attended = lax.psum(terms, "hid").astype(F32)
    middle = (x.astype(F32) + attended).astype(BF16)
    out_terms, gate_rows = channel_mix(
        middle, carried[1:2], gains, prior_step_blends, feedforward_accept_proj, key_rows, value_rows
    )
    summed = lax.psum_scatter(out_terms, "hid", scatter_dimension=1, tiled=True).astype(F32)
    mid_share = lax.dynamic_slice_in_dim(middle, lax.axis_index("hid") * lw, lw, 1).astype(F32)
    present = jnp.arange(rows) < length
    combined = mid_share + gate_rows * summed
    layer_out = jnp.where(present[:, None], combined, 0.0).astype(BF16)[None]
    last = length - 1
    shift_out = jnp.stack(
        [
            norm_row(lax.dynamic_index_in_dim(x, last, 0, keepdims=False).astype(F32), gains[0]),
            norm_row(lax.dynamic_index_in_dim(middle, last, 0, keepdims=False).astype(F32), gains[1]),
        ]
    ).astype(BF16)[None]
    return (layer_out, state[None], shift_out)


def solution(mesh):
    placed = (
        P("req", None, None),
        P("req"),
        P("req"),
        P("req"),
        P(),
        P(("req", "hid"), None),
        P(("req", "hid"), None),
        P(("req", "hid"), None),
        P(),
        P(),
        P("hid"),
        P(),
        P(None, "hid"),
        P("hid"),
        P("hid"),
        P(None, "hid"),
        P("hid", None),
        P("req", "hid", None, None, None),
        P("req", None, None),
        P(("req", "hid"), None),
        P(("req", "hid"), None),
        P(None, "hid"),
    )
    return jax.shard_map(
        local,
        mesh=mesh,
        in_specs=placed,
        out_specs=(P("req", None, "hid"), P("req", "hid", None, None), P("req", None, None)),
        check_vma=False,
    )
```

time: 824 us -> 585 us (0.71)
  local copies, waits for them, and re-layouts: 128 us -> 5.4 us
  other arithmetic: 122 us -> 23.8 us
  matrix products: 59.2 us -> 0 us
  Pallas kernels: 0 us -> 54.9 us
  waiting for transfers between devices: 478 us -> 457 us
  blocking collectives: 0 us -> 20.1 us
    dot_general x29 -> x0, matrix products: 59.2 us -> none  [the longest x1 16.2 us: local(): jnp.dot(hidden, value_rows, preferred_element_type=jnp.float32)]
    pallas_call x0 -> x2, Pallas kernels: none -> 54.9 us  [the longest x1 31 us: time_mix(): pl.pallas_call(time_mix_kernel, out_shape=(jax.ShapeDtypeStruct((rows, wi...]
    reduce_sum x22 -> x4, other arithmetic: 52.7 us -> 6 us  [the longest x2 3.02 us: norm_row(): center = row - jnp.mean(row)]
    gather x2 -> x0, local copies, waits for them, and re-layouts: 23.5 us -> none  [local(): jnp.take(blended[:3].reshape(3, seq_len, shards, shard_rows), partition_a...]
    all_to_all x0 -> x1, blocking collectives: none -> 20.1 us  [local(): lax.all_to_all(own, 'hid', split_axis=0, concat_axis=0, tiled=True)]
    all_to_all x2 -> x1, waiting for transfers between devices: 27.1 us -> 10.7 us  [local(): lax.all_to_all(kept_summary_places[0, 0].astype(BF16).reshape(hid, -1, HE...]
    all_to_all x2 -> x0, local copies, waits for them, and re-layouts: 16 us -> none  [local(): lax.all_to_all(collected, 'hid', split_axis=2, concat_axis=1, tiled=True)]
    mul x9 -> x0, local copies, waits for them, and re-layouts: 15.1 us -> none  [the longest x1 9.03 us: local(): (before - normed_in)[None] * mix_rows[:5, None, :]]
  transfers between devices with their start and end apart: 7 -> 6, of which waited for: 6 -> 6; matrix products, arithmetic and copies ran while one was open for 17% -> 4% of each run, Pallas kernels for 0% -> 0%
where the time goes in v1:
time: 585 us; the launch traced here: 584 us
  waiting for transfers between devices  457 us (78%)
  Pallas kernels  54.9 us (9%)
  other arithmetic  23.8 us (4%)
  blocking collectives  20.1 us (3%)
  between operations  18.7 us (3%)
    psum x1, waiting for transfers between devices, local(): attended = lax.psum(terms, 'hid').astype(F32)  126 us
    all_gather x1, waiting for transfers between devices, local(): value_rows = lax.all_gather(exit_proj, 'req', axis=0, tiled=True)  99.4 us
    all_gather x1, waiting for transfers between devices, local(): key_rows = lax.all_gather(entry, 'req', axis=0, tiled=True)  95 us
    all_gather x1, waiting for transfers between devices, local(): w = lax.all_gather(swapped, 'req', axis=0, tiled=True)  69.7 us
    reduce_scatter x1, waiting for transfers between devices, local(): lax.psum_scatter(out_terms, 'hid', scatter_dimension=1, tiled=True)  54.9 us
    pallas_call x1, Pallas kernels, time_mix(): pl.pallas_call(time_mix_kernel, out_shape=(jax.ShapeDtypeStruct((rows, wi...  31 us
    pallas_call x1, Pallas kernels, channel_mix(): pl.pallas_call(channel_mix_kernel, out_shape=(jax.ShapeDtypeStruct((rows,...  23.8 us
    all_to_all x1, blocking collectives, local(): lax.all_to_all(own, 'hid', split_axis=0, concat_axis=0, tiled=True)  20.1 us
  transfers between devices with their start and end apart: 6, of which 6 were waited for; matrix products, arithmetic and copies ran while one was open for 4% of the time, Pallas kernels for 0%

profile of v1, /device:TPU:0, one launch (start us, length us, event | category | flops | bytes accessed | tf_op | source)
XLA Modules:
  0.0 584.0 jit_solution(1464759143517149158)
XLA Ops:
  7.2 0.0 copy-start.1
  7.2 0.0 all-gather.4.cloned.1.call-start
  7.2 1.1 convert.22
  8.4 0.5 copy.33
  8.9 1.1 convert.21
  10.0 0.5 copy.32
  10.5 0.0 copy-done.1
  10.6 0.5 copy.31
  11.2 1.8 maximum_bitcast_fusion
  13.0 0.9 reshape.100
  13.9 0.0 copy-start.3
  13.9 0.0 copy-start.4
  13.9 20.1 %all_to_all.10 = bf16[16,32,768]{2,1,0:T(8,128)(2,1)} all-to-all(bf16[16,32,768]{2,1,0:T(8,128)(2,1)S(1)} %reshape.100), channel_id=1, replica_groups=mesh['req'=8,'hid'=16] {'hid'}, dimensions={0} | all-to-all | bytes 1572864 | tf_op jit(solution)/shard_map/all_to_all | solution.py:319
  34.0 0.0 all-gather.4.cloned.1.call-update
  34.1 1.8 convert_element_type.66
  35.9 1.5 reshape.101
  37.4 3.6 all-to-all-start.1
  40.9 0.0 all-reduce.2.cloned.1.call-start
  42.3 0.0 copy-done.3
  42.3 0.6 convert_element_type.65.gain_ref
  43.6 0.0 copy-done.4
  43.6 0.6 slice_bitcast_fusion
  44.3 10.7 %all-to-all-done.1 = bf16[16,2,8192]{2,1,0:T(2,128)(2,1)S(1)} async-done(((bf16[16,2,8192]{2,1,0:T(2,128)(2,1)}), bf16[16,2,8192]{2,1,0:T(2,128)(2,1)S(1)}, u32[]{:S(2)}, u32[]{:S(2)}) %all-to-all-start.1) | async-done | bytes 524320 | tf_op jit(solution)/shard_map/all_to_all | solution.py:320
  55.0 0.7 reshape.102
  55.7 0.7 select_bitcast_fusion.s0_ref
  56.3 69.7 %all-gather.4.cloned.1.call-done.w_ref = bf16[128,32,768]{2,1,0:T(8,128)(2,1)} async-done(((bf16[16,32,768]{2,1,0:T(8,128)(2,1)}), bf16[128,32,768]{2,1,0:T(8,128)(2,1)}) %all-gather.4.cloned.1.call-update) | async-done | bytes 6291472 | tf_op jit(solution)/shard_map/all_gather | solution.py:326
  126.1 31.0 %time_mix.1 = (bf16[512,4096]{1,0:T(8,128)(2,1)}, f32[4,64,64]{2,1,0:T(8,128)}) custom-call(s32[128]{0:T(128)} %perm_ref.1, s32[1]{0:T(128)} %copy.38.len_ref, bf16[512,4096]{1,0:T(8,128)(2,1)} %bitcast.41, f32[1,4096]{1,0:T(1,128)} %get-tuple-element.22.first_ref, f32[2,4096]{1,0:T(2,128)} %convert_element_type.65.gain_ref, bf16[7,4096]{1,0:T(8,128)(2,1)} %mix_ref.3, ...), custom_call_target="tpu_custom_call" | custom-call | tf_op jit(solution)/shard_map/time_mix/pallas_call | solution.py:191
  157.1 0.0 all-reduce.2.cloned.1.call-update
  157.2 0.0 all-gather.6.cloned.1.call-start
  157.2 0.7 all-gather.6.cloned.1.call-update
  157.9 0.0 all-gather.8.cloned.1.call-start
  157.9 0.5 all-gather.8.cloned.1.call-update
  158.5 0.2 reduce-scatter.2.cloned.1.call-start
  158.7 126.2 %all-reduce.2.cloned.1.call-done = bf16[512,4096]{1,0:T(8,128)(2,1)} async-done(((bf16[512,4096]{1,0:T(8,128)(2,1)}), bf16[512,4096]{1,0:T(8,128)(2,1)}) %all-reduce.2.cloned.1.call-update) | async-done | bytes 4194320 | tf_op jit(solution)/shard_map/psum | solution.py:338
  284.9 7.2 %add_convert_fusion.x_ref = bf16[512,4096]{1,0:T(8,128)(2,1)} fusion(bf16[512,4096]{1,0:T(8,128)(2,1)} %all-reduce.2.cloned.1.call-done, bf16[1,512,4096]{2,1,0:T(8,128)(2,1)} %param.22), kind=kLoop, calls=%fused_computation | loop fusion | flops 8388608 | bytes 12582912 | tf_op jit(solution)/shard_map/convert_element_type | solution.py:339
  292.1 95.0 %all-gather.6.cloned.1.call-done.key_ref = bf16[896,4096]{1,0:T(8,128)(2,1)} async-done(((bf16[112,4096]{1,0:T(8,128)(2,1)}), bf16[896,4096]{1,0:T(8,128)(2,1)}) %all-gather.6.cloned.1.call-update) | async-done | bytes 7340048 | tf_op jit(solution)/shard_map/all_gather | solution.py:328
  387.1 99.4 %all-gather.8.cloned.1.call-done.value_ref = bf16[896,4096]{1,0:T(8,128)(2,1)} async-done(((bf16[112,4096]{1,0:T(8,128)(2,1)}), bf16[896,4096]{1,0:T(8,128)(2,1)}) %all-gather.8.cloned.1.call-update) | async-done | bytes 7340048 | tf_op jit(solution)/shard_map/all_gather | solution.py:330
  486.4 23.8 %channel_mix.1 = (bf16[512,4096]{1,0:T(8,128)(2,1)}, f32[512,256]{1,0:T(8,128)}) custom-call(bf16[512,4096]{1,0:T(8,128)(2,1)} %add_convert_fusion.x_ref, f32[1,4096]{1,0:T(1,128)} %get-tuple-element.21.first_ref, f32[2,4096]{1,0:T(2,128)} %convert_element_type.65.gain_ref, bf16[7,4096]{1,0:T(8,128)(2,1)} %mix_ref.3, bf16[4096,256]{1,0:T(8,128)(2,1)} %accept_ref.1, ...), custom_call_target="tpu_custom_call" | custom-call | tf_op jit(solution)/shard_map/channel_mix/pallas_call | solution.py:256
  510.3 0.0 copy-start
  510.3 0.0 copy-start.2
  510.3 0.0 reduce-scatter.2.cloned.1.call-update
  510.3 1.5 convert_reduce_fusion.1
  512.5 1.5 multiply_reduce_fusion.1
  514.7 1.5 convert_reduce_fusion
  516.9 1.5 multiply_reduce_fusion
  519.0 0.0 copy-done
  519.0 1.0 fusion.2
  520.0 0.6 pad_maximum_fusion
  520.7 54.9 %reduce-scatter.2.cloned.1.call-done = bf16[512,256]{1,0:T(8,128)(2,1)} async-done(((bf16[512,4096]{1,0:T(8,128)(2,1)}), bf16[512,256]{1,0:T(8,128)(2,1)}) %reduce-scatter.2.cloned.1.call-update) | async-done | bytes 262160 | tf_op jit(solution)/shard_map/reduce_scatter | solution.py:343
  575.6 0.0 copy-done.2
  575.6 1.9 fusion
  (6 shorter events, 0.2 us)
Async XLA Ops:
  7.2 3.4 copy-start.1
  7.2 118.9 %all-gather.4.cloned.1.call-start = ((), (), s32[]{:S(2)}) async-start(), calls=%async_computation.3 | async-start | bytes 7077888 | tf_op jit(solution)/shard_map/all_gather | solution.py:326
  13.9 28.4 %copy-start.3 = (bf16[2,4096]{1,0:T(2,128)(2,1)S(1)}, bf16[2,4096]{1,0:T(2,128)(2,1)}, u32[]{:S(2)}) copy-start(bf16[2,4096]{1,0:T(2,128)(2,1)} %param.30) | copy-start | bytes 49156
  13.9 29.7 %copy-start.4 = (bf16[1,2,4096]{2,1,0:T(2,128)(2,1)S(1)}, bf16[1,2,4096]{2,1,0:T(2,128)(2,1)}, u32[]{:S(2)}) copy-start(bf16[1,2,4096]{2,1,0:T(2,128)(2,1)} %param.40) | copy-start | bytes 49156
  37.4 17.6 %all-to-all-start.1 = ((bf16[16,2,8192]{2,1,0:T(2,128)(2,1)}), bf16[16,2,8192]{2,1,0:T(2,128)(2,1)S(1)}, u32[]{:S(2)}, u32[]{:S(2)}) async-start(bf16[16,2,8192]{2,1,0:T(2,128)(2,1)} %reshape.101), calls=%async_computation.1 | async-start | bytes 1048576 | tf_op jit(solution)/shard_map/all_to_all | solution.py:320
  40.9 243.9 %all-reduce.2.cloned.1.call-start = ((), (), s32[]{:S(2)}) async-start(), calls=%async_computation.4 | async-start | bytes 8388608 | tf_op jit(solution)/shard_map/psum | solution.py:338
  157.2 229.9 %all-gather.6.cloned.1.call-start = ((), (), s32[]{:S(2)}) async-start(), calls=%async_computation.5 | async-start | bytes 8257536 | tf_op jit(solution)/shard_map/all_gather | solution.py:328
  157.9 328.5 %all-gather.8.cloned.1.call-start = ((), (), s32[]{:S(2)}) async-start(), calls=%async_computation.6 | async-start | bytes 8257536 | tf_op jit(solution)/shard_map/all_gather | solution.py:330
  158.5 417.1 %reduce-scatter.2.cloned.1.call-start = ((), (), s32[]{:S(2)}) async-start(), calls=%async_computation.7 | async-start | bytes 4456448 | tf_op jit(solution)/shard_map/reduce_scatter | solution.py:343
  510.3 8.8 %copy-start = (f32[2,4096]{1,0:T(2,128)S(1)}, f32[2,4096]{1,0:T(2,128)}, u32[]{:S(2)}) copy-start(f32[2,4096]{1,0:T(2,128)} %convert_element_type.65.gain_ref) | copy-start | bytes 98308
  510.3 65.3 %copy-start.2 = (f32[512,256]{1,0:T(8,128)S(1)}, f32[512,256]{1,0:T(8,128)}, u32[]{:S(2)}) copy-start(f32[512,256]{1,0:T(8,128)} %get-tuple-element.16) | copy-start | bytes 1572868
Sparse Core Ops, SparseCore 0:
  34.2 91.8 all-gather.3
  157.3 127.5 all-reduce.1
  287.2 99.8 all-gather.5
  389.2 97.1 all-gather.7
  510.4 65.0 reduce-scatter.1

commit v2 on v1

--- a/solution.py
+++ b/solution.py
@@ -15,6 +15,11 @@
 VMEM_LIMIT = 58 * 1024 * 1024
 F32 = jnp.float32
 BF16 = jnp.bfloat16
+MESH = pl.DeviceIdType.MESH
+NY, NZ, NC = 2, 4, 2
+NX, NW = 4, 2
+PIECES = NX * NW
+COST = pl.CostEstimate(flops=40_000_000_000, bytes_accessed=40_000_000, transcendentals=0)
 VM = pl.BlockSpec(memory_space=pltpu.VMEM)
 SM = pl.BlockSpec(memory_space=pltpu.SMEM)
 HB = pl.BlockSpec(memory_space=pl.ANY)
@@ -32,25 +37,49 @@
     return jnp.dot(a, b, preferred_element_type=F32)
 
 
-def row_stats(x_ref, eps):
-    rows, width = x_ref.shape
-
+def piece_owners():
+    x, w = lax.axis_index("req") // NW, lax.axis_index("req") % NW
+
+    def at(dx, other):
+        return (x + dx) % NX * NW + (1 - w if other else w)
+
+    return [at(0, 0), at(0, 1), at(NX - 1, 0), at(1, 0), at(NX - 1, 1), at(1, 1), at(2, 0), at(2, 1)]
+
+
+def collect(own):
+    def send(value, dx, dw):
+        pairs = [
+            (x * NW + w, (x + dx) % NX * NW + (w + dw) % NW) for x in range(NX) for w in range(NW)
+        ]
+        return lax.ppermute(value, "req", pairs)
+
+    other = send(own, 0, 1)
+    before, after = send(own, 1, 0), send(own, NX - 1, 0)
+    before_other, after_other = send(other, 1, 0), send(other, NX - 1, 0)
+    far, far_other = send(before, 1, 0), send(after_other, NX - 1, 0)
+    return [own, other, before, after, before_other, after_other, far, far_other]
+
+
+def group_columns(g, lw):
+    block = (g % NY) * (NZ * NC) + (g // NY % NZ) * NC + g // (NY * NZ)
+    return pl.ds(pl.multiple_of(block * lw, lw), lw)
+
+
+def row_stats(part, count, rows, width, eps):
     def add_sum(c, total):
-        part = x_ref[:, pl.ds(pl.multiple_of(c * KC, KC), KC)].astype(F32)
-        return total + jnp.sum(part, axis=1, keepdims=True)
+        return total + jnp.sum(part(c), axis=1, keepdims=True)
 
     def add_square(c, total):
-        part = x_ref[:, pl.ds(pl.multiple_of(c * KC, KC), KC)].astype(F32) - mean
-        return total + jnp.sum(part * part, axis=1, keepdims=True)
+        center = part(c) - mean
+        return total + jnp.sum(center * center, axis=1, keepdims=True)
 
     zero = jnp.zeros((rows, 1), F32)
-    mean = lax.fori_loop(0, width // KC, add_sum, zero) / width
-    var = lax.fori_loop(0, width // KC, add_square, zero) / width
+    mean = lax.fori_loop(0, count, add_sum, zero) / width
+    var = lax.fori_loop(0, count, add_square, zero) / width
     return mean, 1.0 / jnp.sqrt(var + eps)
 
 
-def normed_and_delta(x_ref, first_ref, gain_ref, which, cols, mean, inv):
-    part = x_ref[:, cols].astype(F32)
+def normed_and_delta(part, first_ref, gain_ref, which, cols, mean, inv):
     normed = (part - mean) * inv * gain_ref[:, cols].astype(F32)[which : which + 1]
     before = pltpu.roll(normed, 1, 0)
     row = lax.broadcasted_iota(jnp.int32, normed.shape, 0)
@@ -58,32 +87,47 @@
     return normed, before - normed
 
 
+def pick_row(values, index):
+    row = lax.broadcasted_iota(jnp.int32, values.shape, 0)
+    return jnp.sum(jnp.where(row == index, values, 0.0), axis=0, keepdims=True)
+
+
 def time_mix_kernel(
-    perm_ref, len_ref, x_ref, first_ref, gain_ref, mix_ref, w_ref, gating_ref, left_ref,
-    right_ref, bias_ref, bonus_ref, gscale_ref, s0_ref, exit_ref,
-    terms_ref, state_ref,
-    w_scr, acc, acc_low, acc_gate, logw_scr, prod_scr, gated_scr, st_scr, sem,
+    perm_ref, len_ref, x_ref, first_ref, gain_ref, mix_ref, gating_ref, left_ref,
+    right_ref, bias_ref, bonus_ref, gscale_ref, s0_ref, exit_ref, *refs,
 ):
+    pieces = refs[:PIECES]
+    terms_ref, state_ref, last_ref = refs[PIECES : PIECES + 3]
+    (
+        w_scr, acc, acc_low, acc_gate, logw_scr, prod_scr, gated_scr, st_scr, sem,
+    ) = refs[PIECES + 3 :]
     rows, width = x_ref.shape
-    blocks = w_scr.shape[0]
     block_rows = w_scr.shape[1]
     lw = acc_gate.shape[1]
 
-    def start(j, carry):
-        pltpu.make_async_copy(w_ref.at[j], w_scr.at[perm_ref[j]], sem).start()
-        return carry
-
-    lax.fori_loop(0, blocks, start, 0)
-    mean, inv = row_stats(x_ref, 1e-05)
+    for piece, owner in zip(pieces, piece_owners()):
+        count = piece.shape[0]
+
+        def start(j, carry, piece=piece, base=owner * count):
+            pltpu.make_async_copy(piece.at[j], w_scr.at[perm_ref[base + j]], sem).start()
+            return carry
+
+        lax.fori_loop(0, count, start, 0)
+
+    def part(c):
+        return x_ref[:, pl.ds(pl.multiple_of(c * KC, KC), KC)].astype(F32)
+
+    mean, inv = row_stats(part, width // KC, rows, width, 1e-05)
     acc[...] = jnp.zeros_like(acc)
     acc_low[...] = jnp.zeros_like(acc_low)
     acc_gate[...] = jnp.zeros_like(acc_gate)
-    pltpu.make_async_copy(w_ref, w_scr, sem).wait()
+    pltpu.make_async_copy(w_scr, w_scr, sem).wait()
     per = KC // block_rows
 
     def project(c, carry):
         cols = pl.ds(pl.multiple_of(c * KC, KC), KC)
-        normed, delta = normed_and_delta(x_ref, first_ref, gain_ref, 0, cols, mean, inv)
+        normed, delta = normed_and_delta(part(c), first_ref, gain_ref, 0, cols, mean, inv)
+        last_ref[:, cols] = pick_row(normed, len_ref[0] - 1)
         mix = mix_ref[:, cols].astype(F32)
 
         def blend(m):
@@ -177,27 +221,28 @@
         state_ref[2 * p] = full[0:HEAD, 0:HEAD]
         state_ref[2 * p + 1] = full[HEAD:PAIR, HEAD:PAIR]
 
-    def leave(c, carry):
-        cols = pl.ds(pl.multiple_of(c * KC, KC), KC)
-        terms_ref[:, cols] = nn_dot(gated_scr[...], exit_ref[:, cols]).astype(BF16)
+    def leave(g, carry):
+        terms_ref[g] = nn_dot(gated_scr[...], exit_ref[:, group_columns(g, lw)]).astype(BF16)
         return carry
 
-    lax.fori_loop(0, width // KC, leave, 0)
-
-
-def time_mix(perm, length, x, first, gains, mixes, w, gating, left, right, bias, bonus, gscale, s0, exit_w):
+    lax.fori_loop(0, width // lw, leave, 0)
+
+
+def time_mix(perm, length, x, first, gains, mixes, gating, left, right, bias, bonus, gscale, s0, exit_w, pieces):
     rows, width = x.shape
     lw = gating.shape[1]
+    piece_blocks, block_rows, piece_width = pieces[0].shape
     return pl.pallas_call(
         time_mix_kernel,
         out_shape=(
-            jax.ShapeDtypeStruct((rows, width), BF16),
+            jax.ShapeDtypeStruct((width // lw, rows, lw), BF16),
             jax.ShapeDtypeStruct(s0.shape, F32),
+            jax.ShapeDtypeStruct((1, width), F32),
         ),
-        in_specs=[SM, SM, VM, VM, VM, VM, HB] + [VM] * 8,
-        out_specs=(VM, VM),
+        in_specs=[SM, SM] + [VM] * 12 + [HB] * PIECES,
+        out_specs=(VM, VM, VM),
         scratch_shapes=[
-            pltpu.VMEM(w.shape, BF16),
+            pltpu.VMEM((PIECES * piece_blocks, block_rows, piece_width), BF16),
             pltpu.VMEM((rows, 3 * lw), F32),
             pltpu.VMEM((rows, left.shape[1]), F32),
             pltpu.VMEM((rows, lw), F32),
@@ -208,75 +253,257 @@
             pltpu.SemaphoreType.DMA,
         ],
         compiler_params=pltpu.CompilerParams(vmem_limit_bytes=VMEM_LIMIT),
+        cost_estimate=COST,
         name="time_mix",
-    )(perm, length, x, first, gains, mixes, w, gating, left, right, bias, bonus, gscale, s0, exit_w)
+    )(perm, length, x, first, gains, mixes, gating, left, right, bias, bonus, gscale, s0, exit_w, *pieces)
 
 
 def channel_mix_kernel(
-    x_ref, first_ref, gain_ref, mix_ref, accept_ref, key_ref, value_ref,
-    terms_ref, gate_ref,
-    key_scr, value_scr, inner, acc_gate, hidden, sems,
+    len_ref, x_ref, first_ref, gain_ref, mix_ref, accept_ref, *refs,
 ):
-    width = x_ref.shape[1]
-    key_copy = pltpu.make_async_copy(key_ref, key_scr, sems.at[0])
-    value_copy = pltpu.make_async_copy(value_ref, value_scr, sems.at[1])
-    key_copy.start()
-    value_copy.start()
-    mean, inv = row_stats(x_ref, 1e-05)
+    keys, values = refs[:PIECES], refs[PIECES : 2 * PIECES]
+    terms_ref, gate_ref, last_ref = refs[2 * PIECES : 2 * PIECES + 3]
+    key_scr, value_scr, inner, acc_gate, hidden, key_sems, value_sems = refs[2 * PIECES + 3 :]
+    groups, rows, lw = x_ref.shape
+    units = keys[0].shape[0]
+
+    def fetch(pieces, scr, sems):
+        copies = [
+            pltpu.make_async_copy(piece, scr.at[pl.ds(i * units, units)], sems.at[i])
+            for i, piece in enumerate(pieces)
+        ]
+        for copy in copies:
+            copy.start()
+        return copies
+
+    key_copies = fetch(keys, key_scr, key_sems)
+    value_copies = fetch(values, value_scr, value_sems)
+
+    def part(g):
+        return x_ref[g].astype(F32)
+
+    mean, inv = row_stats(part, groups, rows, groups * lw, 1e-05)
     inner[...] = jnp.zeros_like(inner)
     acc_gate[...] = jnp.zeros_like(acc_gate)
-    key_copy.wait()
-
-    def project(c, carry):
-        cols = pl.ds(pl.multiple_of(c * KC, KC), KC)
-        normed, delta = normed_and_delta(x_ref, first_ref, gain_ref, 1, cols, mean, inv)
+    for copy in key_copies:
+        copy.wait()
+
+    def project(g, carry):
+        cols = group_columns(g, lw)
+        normed, delta = normed_and_delta(part(g), first_ref, gain_ref, 1, cols, mean, inv)
+        last_ref[:, cols] = pick_row(normed, len_ref[0] - 1)
         mix = mix_ref[:, cols].astype(F32)
         inner[...] += nt_dot((normed + delta * mix[5:6]).astype(BF16), key_scr[:, cols])
         acc_gate[...] += nn_dot((normed + delta * mix[6:7]).astype(BF16), accept_ref[cols, :])
         return carry
 
-    lax.fori_loop(0, width // KC, project, 0)
+    lax.fori_loop(0, groups, project, 0)
     positive = jnp.maximum(inner[...], 0.0)
     hidden[...] = (positive * positive).astype(BF16)
     gate_ref[...] = jax.nn.sigmoid(acc_gate[...])
-    value_copy.wait()
-
-    def leave(c, carry):
-        cols = pl.ds(pl.multiple_of(c * KC, KC), KC)
-        terms_ref[:, cols] = nn_dot(hidden[...], value_scr[:, cols]).astype(BF16)
+    for copy in value_copies:
+        copy.wait()
+
+    def leave(g, carry):
+        terms_ref[g] = nn_dot(hidden[...], value_scr[:, group_columns(g, lw)]).astype(BF16)
         return carry
 
-    lax.fori_loop(0, width // KC, leave, 0)
-
-
-def channel_mix(x, first, gains, mixes, accept, key_rows, value_rows):
-    rows, width = x.shape
-    lw = accept.shape[1]
-    units = key_rows.shape[0]
+    lax.fori_loop(0, groups, leave, 0)
+
+
+def channel_mix(length, x, first, gains, mixes, accept, keys, values):
+    groups, rows, lw = x.shape
+    units = PIECES * keys[0].shape[0]
+    width = groups * lw
     return pl.pallas_call(
         channel_mix_kernel,
         out_shape=(
-            jax.ShapeDtypeStruct((rows, width), BF16),
+            jax.ShapeDtypeStruct((groups, rows, lw), BF16),
             jax.ShapeDtypeStruct((rows, lw), F32),
+            jax.ShapeDtypeStruct((1, groups * lw), F32),
         ),
-        in_specs=[VM] * 5 + [HB] * 2,
-        out_specs=(VM, VM),
+        in_specs=[SM] + [VM] * 5 + [HB] * (2 * PIECES),
+        out_specs=(VM, VM, VM),
         scratch_shapes=[
-            pltpu.VMEM(key_rows.shape, BF16),
-            pltpu.VMEM(value_rows.shape, BF16),
+            pltpu.VMEM((units, width), BF16),
+            pltpu.VMEM((units, width), BF16),
             pltpu.VMEM((rows, units), F32),
             pltpu.VMEM((rows, lw), F32),
             pltpu.VMEM((rows, units), BF16),
-            pltpu.SemaphoreType.DMA((2,)),
+            pltpu.SemaphoreType.DMA((PIECES,)),
+            pltpu.SemaphoreType.DMA((PIECES,)),
         ],
         compiler_params=pltpu.CompilerParams(vmem_limit_bytes=VMEM_LIMIT),
+        cost_estimate=COST,
         name="channel_mix",
-    )(x, first, gains, mixes, accept, key_rows, value_rows)
-
-
-def norm_row(row, gain):
-    center = row - jnp.mean(row)
-    return center / jnp.sqrt(jnp.mean(center * center) + 1e-05) * gain
+    )(length, x, first, gains, mixes, accept, *keys, *values)
+
+
+def hid_place():
+    me = lax.axis_index("hid")
+    y, z, c = me // (NZ * NC), me // NC % NZ, me % NC
+
+    def at(yy, zz, cc):
+        return {"hid": (yy * NZ + zz) * NC + cc}
+
+    zu, zd = (z + 1) % NZ, (z + 3) % NZ
+    peers = {"core": at(y, z, 1 - c), "up": at(y, zu, c), "down": at(y, zd, c), "y": at(1 - y, z, c)}
+    return y, z, c, zu, (z + 2) % NZ, zd, peers
+
+
+def meet(peers):
+    barrier = pltpu.get_barrier_semaphore()
+    for device in peers.values():
+        pl.semaphore_signal(barrier, inc=1, device_id=device, device_id_type=MESH)
+    pl.semaphore_wait(barrier, len(peers))
+
+
+class Copies:
+    def __init__(self, send, recv):
+        self.send, self.recv, self.made = send, recv, []
+
+    def start(self, src, dst, device):
+        i = len(self.made)
+        copy = pltpu.make_async_remote_copy(
+            src_ref=src, dst_ref=dst, send_sem=self.send.at[i], recv_sem=self.recv.at[i],
+            device_id=device, device_id_type=MESH,
+        )
+        copy.start()
+        self.made.append(copy)
+        return copy
+
+    def finish(self):
+        for copy in self.made:
+            copy.wait_send()
+
+
+def sum_terms(terms, acc, core_buf, pass_buf, near_buf, y_buf, copies, place):
+    y, z, c, zu, z2, zd, peers = place
+    half = terms.shape[3] // 2
+    from_core = [
+        copies.start(terms.at[1 - c, g], core_buf.at[g], peers["core"]) for g in (z2, zu, zd, z)
+    ]
+
+    def add_core(i, g):
+        from_core[i].wait_recv()
+        acc[g] = (terms[c, g].astype(F32) + core_buf[g].astype(F32)).astype(BF16)
+
+    add_core(0, z2)
+    first_up = copies.start(acc.at[z2, :, 0:half], pass_buf.at[0], peers["up"])
+    first_down = copies.start(acc.at[z2, :, half : 2 * half], pass_buf.at[1], peers["down"])
+    add_core(1, zu)
+    add_core(2, zd)
+    first_up.wait_recv()
+    acc[zu, :, 0:half] = (acc[zu, :, 0:half].astype(F32) + pass_buf[0].astype(F32)).astype(BF16)
+    second_up = copies.start(acc.at[zu], near_buf.at[0], peers["up"])
+    first_down.wait_recv()
+    acc[zd, :, half : 2 * half] = (
+        acc[zd, :, half : 2 * half].astype(F32) + pass_buf[1].astype(F32)
+    ).astype(BF16)
+    second_down = copies.start(acc.at[zd], near_buf.at[1], peers["down"])
+    add_core(3, z)
+    second_up.wait_recv()
+    second_down.wait_recv()
+
+    def total_of(yy):
+        return acc[z, yy].astype(F32) + near_buf[0, yy].astype(F32) + near_buf[1, yy].astype(F32)
+
+    acc[z, 1 - y] = total_of(1 - y).astype(BF16)
+    across = copies.start(acc.at[z, 1 - y], y_buf, peers["y"])
+    own = total_of(y)
+    across.wait_recv()
+    return own + y_buf[...].astype(F32)
+
+
+def sum_scratch(shape, copies):
+    nc, nz, ny, rows, lw = shape
+    return [
+        pltpu.VMEM((nz, ny, rows, lw), BF16),
+        pltpu.VMEM((nz, ny, rows, lw), BF16),
+        pltpu.VMEM((2, ny, rows // 2, lw), BF16),
+        pltpu.VMEM((2, ny, rows, lw), BF16),
+        pltpu.VMEM((rows, lw), BF16),
+        pltpu.SemaphoreType.DMA((copies,)),
+        pltpu.SemaphoreType.DMA((copies,)),
+    ]
+
+
+def join_kernel(terms, x_ref, mid_ref, own_ref, acc, core_buf, pass_buf, near_buf, y_buf, send, recv):
+    place = hid_place()
+    y, z, c, zu, z2, zd, peers = place
+    meet(peers)
+    copies = Copies(send, recv)
+    half = x_ref.shape[0] // 2
+    total = sum_terms(terms, acc, core_buf, pass_buf, near_buf, y_buf, copies, place)
+    own = (x_ref[...].astype(F32) + total).astype(BF16)
+    own_ref[...] = own
+    mid_ref[c, z, y] = own
+
+    def pass_on(index, device):
+        return copies.start(mid_ref.at[index], mid_ref.at[index], device)
+
+    pass_on((c, z, y), peers["y"]).wait_recv()
+    up = pass_on((c, z), peers["up"])
+    down = pass_on((c, z), peers["down"])
+    waits = [pass_on((c, z), peers["core"])]
+    up.wait_recv()
+    far = [pass_on((c, zd, slice(None), slice(0, half)), peers["up"])]
+    waits.append(pass_on((c, zd), peers["core"]))
+    down.wait_recv()
+    far.append(pass_on((c, zu, slice(None), slice(half, 2 * half)), peers["down"]))
+    waits.append(pass_on((c, zu), peers["core"]))
+    for copy in far:
+        copy.wait_recv()
+    waits.append(pass_on((c, z2), peers["core"]))
+    for copy in waits:
+        copy.wait_recv()
+    copies.finish()
+
+
+def join(terms, x_share):
+    rows, lw = x_share.shape
+    shape = (NC, NZ, NY, rows, lw)
+    return pl.pallas_call(
+        join_kernel,
+        out_shape=(jax.ShapeDtypeStruct(shape, BF16), jax.ShapeDtypeStruct((rows, lw), BF16)),
+        in_specs=[VM, VM],
+        out_specs=(VM, VM),
+        scratch_shapes=sum_scratch(shape, 18),
+        compiler_params=pltpu.CompilerParams(
+            collective_id=0, has_side_effects=True, vmem_limit_bytes=VMEM_LIMIT
+        ),
+        cost_estimate=COST,
+        name="join",
+    )(terms.reshape(shape), x_share)
+
+
+def close_kernel(
+    len_ref, terms, own_ref, gate_ref, out_ref, acc, core_buf, pass_buf, near_buf, y_buf, send, recv
+):
+    place = hid_place()
+    meet(place[-1])
+    copies = Copies(send, recv)
+    total = sum_terms(terms, acc, core_buf, pass_buf, near_buf, y_buf, copies, place)
+    combined = own_ref[...].astype(F32) + gate_ref[...] * total
+    row = lax.broadcasted_iota(jnp.int32, combined.shape, 0)
+    out_ref[...] = jnp.where(row < len_ref[0], combined, 0.0).astype(BF16)
+    copies.finish()
+
+
+def close(length, terms, own, gate_rows):
+    rows, lw = own.shape
+    shape = (NC, NZ, NY, rows, lw)
+    return pl.pallas_call(
+        close_kernel,
+        out_shape=jax.ShapeDtypeStruct((rows, lw), BF16),
+        in_specs=[SM, VM, VM, VM],
+        out_specs=VM,
+        scratch_shapes=sum_scratch(shape, 9),
+        compiler_params=pltpu.CompilerParams(
+            collective_id=1, has_side_effects=True, vmem_limit_bytes=VMEM_LIMIT
+        ),
+        name="close",
+    )(length, terms.reshape(shape), own, gate_rows)
 
 
 def local(
@@ -308,7 +535,6 @@
     lw = mixing_exit_projection.shape[0]
     hid = lax.axis_size("hid")
     block_rows = training_accept_pieces.shape[0]
-    length = prompt_extents[0]
     resuming = continuing_flags[0]
     gains = normalizer_scales.astype(F32)
     carried = jnp.where(resuming == 1, previous_normed_entries[0].astype(F32), 0.0)
@@ -323,35 +549,27 @@
     )
     chosen = lax.dynamic_index_in_dim(fetched, owning_index[0], 0, keepdims=False)
     s0 = jnp.where(resuming == 1, chosen.astype(F32), 0.0)
-    w = lax.all_gather(swapped, "req", axis=0, tiled=True)
-    entry, w = lax.optimization_barrier((feedforward_entry_proj, w))
-    key_rows = lax.all_gather(entry, "req", axis=0, tiled=True)
-    exit_proj, w = lax.optimization_barrier((feedforward_exit_proj, w))
-    value_rows = lax.all_gather(exit_proj, "req", axis=0, tiled=True)
-
-    terms, state = time_mix(
-        partition_arrangement, prompt_extents, x, carried[0:1], gains, prior_step_blends, w,
+    pieces = collect(swapped)
+    entry, exit_proj, pieces[4], pieces[5] = lax.optimization_barrier(
+        (feedforward_entry_proj, feedforward_exit_proj, pieces[4], pieces[5])
+    )
+    keys = collect(entry)
+    values = collect(exit_proj)
+
+    terms, state, last_in = time_mix(
+        partition_arrangement, prompt_extents, x, carried[0:1], gains, prior_step_blends,
         gating_projection, forgetting_left_lowrank, forgetting_right_lowrank,
         forgetting_bias_vector[None], instant_emphasis[None], group_normalizer_scale[None],
-        s0, mixing_exit_projection,
+        s0, mixing_exit_projection, pieces,
     )
-    attended = lax.psum(terms, "hid").astype(F32)
-    middle = (x.astype(F32) + attended).astype(BF16)
-    out_terms, gate_rows = channel_mix(
-        middle, carried[1:2], gains, prior_step_blends, feedforward_accept_proj, key_rows, value_rows
+    x_share = lax.dynamic_slice_in_dim(x, lax.axis_index("hid") * lw, lw, 1)
+    middle, own_middle = join(terms, x_share)
+    out_terms, gate_rows, last_chan = channel_mix(
+        prompt_extents, middle.reshape(hid, rows, lw), carried[1:2], gains, prior_step_blends,
+        feedforward_accept_proj, keys, values,
     )
-    summed = lax.psum_scatter(out_terms, "hid", scatter_dimension=1, tiled=True).astype(F32)
-    mid_share = lax.dynamic_slice_in_dim(middle, lax.axis_index("hid") * lw, lw, 1).astype(F32)
-    present = jnp.arange(rows) < length
-    combined = mid_share + gate_rows * summed
-    layer_out = jnp.where(present[:, None], combined, 0.0).astype(BF16)[None]
-    last = length - 1
-    shift_out = jnp.stack(
-        [
-            norm_row(lax.dynamic_index_in_dim(x, last, 0, keepdims=False).astype(F32), gains[0]),
-            norm_row(lax.dynamic_index_in_dim(middle, last, 0, keepdims=False).astype(F32), gains[1]),
-        ]
-    ).astype(BF16)[None]
+    layer_out = close(prompt_extents, out_terms, own_middle, gate_rows)[None]
+    shift_out = jnp.concatenate([last_in, last_chan]).astype(BF16)[None]
     return (layer_out, state[None], shift_out)
 
 

time: 585 us -> 321 us (0.55)
  waiting for transfers between devices: 457 us -> 92.6 us
  Pallas kernels: 54.9 us -> 163 us
  starting transfers between devices: 3.95 us -> 25 us
  other arithmetic: 23.8 us -> 6.8 us
  between operations: 18.7 us -> 2.98 us
    all_gather x3 -> x0, waiting for transfers between devices: 264 us -> none  [the longest x1 99.4 us: local(): value_rows = lax.all_gather(exit_proj, 'req', axis=0, tiled=True)]
    psum x1 -> x0, waiting for transfers between devices: 126 us -> none  [local(): attended = lax.psum(terms, 'hid').astype(F32)]
    pallas_call x2 -> x4, Pallas kernels: 54.9 us -> 163 us  [the longest x1 63.3 us: join(): pl.pallas_call(join_kernel, out_shape=(jax.ShapeDtypeStruct(shape, BF16),...]
    ppermute x0 -> x21, waiting for transfers between devices: none -> 92.6 us  [send(): return lax.ppermute(value, 'req', pairs)]
    reduce_scatter x1 -> x0, waiting for transfers between devices: 54.9 us -> none  [local(): lax.psum_scatter(out_terms, 'hid', scatter_dimension=1, tiled=True)]
    ppermute x0 -> x21, starting transfers between devices: none -> 21.3 us  [send(): return lax.ppermute(value, 'req', pairs)]
    all_to_all x1, waiting for transfers between devices: 10.7 us -> 0.01 us  [local(): lax.all_to_all(kept_summary_places[0, 0].astype(BF16).reshape(hid, -1, HE...]
    convert_element_type x1 -> x0, other arithmetic: 7.22 us -> none  [local(): middle = (x.astype(F32) + attended).astype(BF16)]
  transfers between devices with their start and end apart: 6 -> 22, of which waited for: 6 -> 8; matrix products, arithmetic and copies ran while one was open for 4% -> 2% of each run, Pallas kernels for 0% -> 31%
where the time goes in v2:
time: 321 us; the launch traced here: 320 us
  Pallas kernels  163 us (51%)
  waiting for transfers between devices  92.6 us (29%)
  starting transfers between devices  25 us (8%)
  blocking collectives  20 us (6%)
  local copies, waits for them, and re-layouts  10.1 us (3%)
  other arithmetic  6.8 us (2%)
    ppermute x21, waiting for transfers between devices, send(): return lax.ppermute(value, 'req', pairs)  92.6 us
    pallas_call x1, Pallas kernels, join(): pl.pallas_call(join_kernel, out_shape=(jax.ShapeDtypeStruct(shape, BF16),...  63.3 us
    pallas_call x1, Pallas kernels, close(): pl.pallas_call(close_kernel, out_shape=jax.ShapeDtypeStruct((rows, lw), B...  36.2 us
    pallas_call x1, Pallas kernels, time_mix(): pl.pallas_call(time_mix_kernel, out_shape=(jax.ShapeDtypeStruct((width //...  34.5 us
    pallas_call x1, Pallas kernels, channel_mix(): pl.pallas_call(channel_mix_kernel, out_shape=(jax.ShapeDtypeStruct((group...  29.1 us
    ppermute x21, starting transfers between devices, send(): return lax.ppermute(value, 'req', pairs)  21.3 us
    all_to_all x1, blocking collectives, local(): lax.all_to_all(own, 'hid', split_axis=0, concat_axis=0, tiled=True)  20 us
  transfers between devices with their start and end apart: 22, of which 8 were waited for; matrix products, arithmetic and copies ran while one was open for 2% of the time, Pallas kernels for 31%

profile of v2, /device:TPU:0, one launch (start us, length us, event | category | flops | bytes accessed | tf_op | source)
XLA Modules:
  0.0 320.5 jit_solution(10278384145169618587)
XLA Ops:
  0.7 1.2 convert.20
  1.9 0.5 copy.28
  2.5 0.5 copy.29
  3.1 0.5 copy.30
  3.6 1.8 maximum_bitcast_fusion
  5.4 0.9 reshape.75
  6.4 20.0 %all_to_all.10.refs_0_ = bf16[16,32,768]{2,1,0:T(8,128)(2,1)S(1)} all-to-all(bf16[16,32,768]{2,1,0:T(8,128)(2,1)S(1)} %reshape.75), channel_id=1, replica_groups=mesh['req'=8,'hid'=16] {'hid'}, dimensions={0} | all-to-all | bytes 1572864 | tf_op jit(solution)/shard_map/all_to_all | solution.py:545
  26.3 2.9 collective-permute-start
  29.2 1.5 collective-permute-start.1
  30.7 1.8 convert_element_type.30
  32.5 0.0 copy-start.3
  32.5 0.0 copy-start.7
  32.6 0.0 copy-start.4
  32.6 1.5 reshape.79
  34.1 3.7 %all-to-all-start = ((bf16[16,2,8192]{2,1,0:T(2,128)(2,1)}), bf16[16,2,8192]{2,1,0:T(2,128)(2,1)S(1)}, u32[]{:S(2)}, u32[]{:S(2)}) async-start(bf16[16,2,8192]{2,1,0:T(2,128)(2,1)} %reshape.79), calls=%async_computation | async-start | bytes 1048576 | tf_op jit(solution)/shard_map/all_to_all | solution.py:546
  38.5 1.8 collective-permute-start.2
  40.3 8.1 %collective-permute-done.refs_1_ = bf16[16,32,768]{2,1,0:T(8,128)(2,1)} collective-permute-done((bf16[16,32,768]{2,1,0:T(8,128)(2,1)S(1)}, bf16[16,32,768]{2,1,0:T(8,128)(2,1)}, u32[]{:S(2)}, u32[]{:S(2)}) %collective-permute-start) | collective-permute-done | bytes 786464 | tf_op jit(solution)/shard_map/ppermute | solution.py:54
  48.4 2.8 collective-permute-start.4
  51.2 0.0 collective-permute-start.3
  51.2 0.0 collective-permute-done.1.refs_2_
  51.2 0.8 collective-permute-start.5
  52.0 23.3 %collective-permute-done.4.refs_5_ = bf16[16,32,768]{2,1,0:T(8,128)(2,1)} collective-permute-done((bf16[16,32,768]{2,1,0:T(8,128)(2,1)}, bf16[16,32,768]{2,1,0:T(8,128)(2,1)}, u32[]{:S(2)}, u32[]{:S(2)}) %collective-permute-start.4) | collective-permute-done | bytes 786464 | tf_op jit(solution)/shard_map/ppermute | solution.py:54
  75.2 0.0 collective-permute-done.3.refs_4_
  75.3 0.7 collective-permute-start.7
  76.0 1.5 collective-permute-start.8
  77.5 2.9 collective-permute-start.14
  80.4 0.0 collective-permute-done.2.refs_3_
  80.4 1.2 collective-permute-start.15
  81.6 8.4 %collective-permute-done.5.refs_6_ = bf16[16,32,768]{2,1,0:T(8,128)(2,1)S(1)} collective-permute-done((bf16[16,32,768]{2,1,0:T(8,128)(2,1)}, bf16[16,32,768]{2,1,0:T(8,128)(2,1)S(1)}, u32[]{:S(2)}, u32[]{:S(2)}) %collective-permute-start.5) | collective-permute-done | bytes 786464 | tf_op jit(solution)/shard_map/ppermute | solution.py:54
  89.9 0.0 collective-permute-start.6
  89.9 0.7 slice_bitcast_fusion
  92.0 0.6 convert_element_type.29.gain_ref
  92.6 1.7 dynamic-slice_bitcast_fusion.x_ref
  94.3 0.0 all-to-all-done
  94.3 0.7 reshape.80
  94.9 0.7 select_bitcast_fusion.s0_ref
  95.6 12.9 %collective-permute-done.6.refs_7_ = bf16[16,32,768]{2,1,0:T(8,128)(2,1)} collective-permute-done((bf16[16,32,768]{2,1,0:T(8,128)(2,1)}, bf16[16,32,768]{2,1,0:T(8,128)(2,1)}, u32[]{:S(2)}, u32[]{:S(2)}) %collective-permute-start.6) | collective-permute-done | bytes 786464 | tf_op jit(solution)/shard_map/ppermute | solution.py:54
  108.5 0.0 collective-permute-start.16
  108.5 0.0 collective-permute-done.7.refs_1_
  108.5 0.1 collective-permute-start.9
  108.6 9.7 %collective-permute-done.14.refs_9_ = bf16[112,4096]{1,0:T(8,128)(2,1)} collective-permute-done((bf16[112,4096]{1,0:T(8,128)(2,1)}, bf16[112,4096]{1,0:T(8,128)(2,1)}, u32[]{:S(2)}, u32[]{:S(2)}) %collective-permute-start.14) | collective-permute-done | bytes 917536 | tf_op jit(solution)/shard_map/ppermute | solution.py:54
  118.4 3.0 collective-permute-start.11
  121.3 5.2 %collective-permute-done.15.refs_10_ = bf16[112,4096]{1,0:T(8,128)(2,1)} collective-permute-done((bf16[112,4096]{1,0:T(8,128)(2,1)}, bf16[112,4096]{1,0:T(8,128)(2,1)}, u32[]{:S(2)}, u32[]{:S(2)}) %collective-permute-start.15) | collective-permute-done | bytes 917536 | tf_op jit(solution)/shard_map/ppermute | solution.py:54
  126.5 0.1 collective-permute-start.18
  126.7 34.5 %time_mix.1 = (bf16[16,512,256]{2,1,0:T(8,128)(2,1)}, f32[4,64,64]{2,1,0:T(8,128)}, f32[1,4096]{1,0:T(1,128)}) custom-call(s32[128]{0:T(128)} %perm_ref.1, s32[1]{0:T(128)S(6)} %copy.35.len_ref, bf16[512,4096]{1,0:T(8,128)(2,1)} %bitcast.47, f32[1,4096]{1,0:T(1,128)} %get-tuple-element.28.first_ref, f32[2,4096]{1,0:T(2,128)} %convert_element_type.29.gain_ref, ...), custom_call_target="tpu_custom_call" | custom-call | flops 40000000000 | bytes 40000000 | tf_op jit(solution)/shard_map/time_mix/pallas_call | solution.py:235
  161.1 0.0 collective-permute-done.16.refs_11_
  161.2 2.0 collective-permute-start.17
  163.1 0.0 collective-permute-done.9.refs_3_
  163.1 0.1 collective-permute-start.12
  163.2 7.7 %collective-permute-done.11.refs_5_ = bf16[112,4096]{1,0:T(8,128)(2,1)S(1)} collective-permute-done((bf16[112,4096]{1,0:T(8,128)(2,1)}, bf16[112,4096]{1,0:T(8,128)(2,1)S(1)}, u32[]{:S(2)}, u32[]{:S(2)}) %collective-permute-start.11) | collective-permute-done | bytes 917536 | tf_op jit(solution)/shard_map/ppermute | solution.py:54
  171.0 17.2 %collective-permute-done.18.refs_13_ = bf16[112,4096]{1,0:T(8,128)(2,1)} collective-permute-done((bf16[112,4096]{1,0:T(8,128)(2,1)}, bf16[112,4096]{1,0:T(8,128)(2,1)}, u32[]{:S(2)}, u32[]{:S(2)}) %collective-permute-start.18) | collective-permute-done | bytes 917536 | tf_op jit(solution)/shard_map/ppermute | solution.py:54
  188.1 0.0 collective-permute-start.13
  188.2 0.0 collective-permute-done.10.refs_4_
  188.2 0.0 collective-permute-start.20
  188.2 63.3 %join.1 = (bf16[2,4,2,512,256]{4,3,2,1,0:T(8,128)(2,1)}, bf16[512,256]{1,0:T(8,128)(2,1)}) custom-call(bf16[2,4,2,512,256]{4,3,2,1,0:T(8,128)(2,1)} %bitcast.51, bf16[512,256]{1,0:T(8,128)(2,1)} %dynamic-slice_bitcast_fusion.x_ref), custom_call_target="tpu_custom_call" | custom-call | flops 40000000000 | bytes 40000000 | tf_op jit(solution)/shard_map/join/pallas_call | solution.py:466
  251.5 0.0 collective-permute-done.12.refs_6_
  251.6 0.0 collective-permute-done.20.refs_15_
  251.6 0.9 copy-done.12
  252.4 0.3 copy-done.13
  252.8 29.1 %channel_mix.1 = (bf16[16,512,256]{2,1,0:T(8,128)(2,1)}, f32[512,256]{1,0:T(8,128)}, f32[1,4096]{1,0:T(1,128)}) custom-call(s32[1]{0:T(128)S(6)} %copy.35.len_ref, bf16[16,512,256]{2,1,0:T(8,128)(2,1)} %bitcast.52, f32[1,4096]{1,0:T(1,128)} %get-tuple-element.27.first_ref, f32[2,4096]{1,0:T(2,128)} %convert_element_type.29.gain_ref, ...), custom_call_target="tpu_custom_call" | custom-call | flops 40000000000 | bytes 40000000 | tf_op jit(solution)/shard_map/channel_mix/pallas_call | solution.py:318
  281.9 0.0 copy-start.6
  281.9 36.2 %close.1 = bf16[512,256]{1,0:T(8,128)(2,1)} custom-call(s32[1]{0:T(128)S(6)} %copy.35.len_ref, bf16[2,4,2,512,256]{4,3,2,1,0:T(8,128)(2,1)} %bitcast.39, bf16[512,256]{1,0:T(8,128)(2,1)} %get-tuple-element.22.own_ref, f32[512,256]{1,0:T(8,128)} %get-tuple-element.23.gate_ref), custom_call_target="tpu_custom_call" | custom-call | tf_op jit(solution)/shard_map/close/pallas_call | solution.py:496
  318.1 0.6 pad_maximum_fusion
  318.8 1.7 copy.38
  (41 shorter events, 0.3 us)
Async XLA Ops:
  0.6 1.7 copy-start.1
  0.6 2.3 copy-start.2
  26.3 12.1 %copy-start = (bf16[16,32,768]{2,1,0:T(8,128)(2,1)}, bf16[16,32,768]{2,1,0:T(8,128)(2,1)S(1)}, u32[]{:S(2)}) copy-start(bf16[16,32,768]{2,1,0:T(8,128)(2,1)S(1)} %all_to_all.10.refs_0_) | copy-start | bytes 2359300
  26.3 22.1 %collective-permute-start = (bf16[16,32,768]{2,1,0:T(8,128)(2,1)S(1)}, bf16[16,32,768]{2,1,0:T(8,128)(2,1)}, u32[]{:S(2)}, u32[]{:S(2)}) collective-permute-start(bf16[16,32,768]{2,1,0:T(8,128)(2,1)S(1)} %all_to_all.10.refs_0_), channel_id=1, source_target_pairs={{0,16},{16,0},{32,48},{48,32},{64,80},{80,64},{96,112},{112,96},{1... | collective-permute-start | bytes 2359304 | tf_op jit(solution)/shard_map/ppermute | solution.py:54
  29.2 21.9 %collective-permute-start.1 = (bf16[16,32,768]{2,1,0:T(8,128)(2,1)S(1)}, bf16[16,32,768]{2,1,0:T(8,128)(2,1)}, u32[]{:S(2)}, u32[]{:S(2)}) collective-permute-start(bf16[16,32,768]{2,1,0:T(8,128)(2,1)S(1)} %all_to_all.10.refs_0_), channel_id=1, source_target_pairs={{0,32},{16,48},{32,64},{48,80},{64,96},{80,112},{96,0},{112,16},{1... | collective-permute-start | bytes 2359304 | tf_op jit(solution)/shard_map/ppermute | solution.py:54
  32.5 19.4 %copy-start.3 = (bf16[1,2,4096]{2,1,0:T(2,128)(2,1)S(1)}, bf16[1,2,4096]{2,1,0:T(2,128)(2,1)}, u32[]{:S(2)}) copy-start(bf16[1,2,4096]{2,1,0:T(2,128)(2,1)} %param.40) | copy-start | bytes 49156
  32.5 42.7 %copy-start.7 = (bf16[112,4096]{1,0:T(8,128)(2,1)S(1)}, bf16[112,4096]{1,0:T(8,128)(2,1)}, u32[]{:S(2)}) copy-start(bf16[112,4096]{1,0:T(8,128)(2,1)} %refs_0_) | copy-start | bytes 2752516
  32.6 59.4 %copy-start.4 = (bf16[2,4096]{1,0:T(2,128)(2,1)S(1)}, bf16[2,4096]{1,0:T(2,128)(2,1)}, u32[]{:S(2)}) copy-start(bf16[2,4096]{1,0:T(2,128)(2,1)} %param.30) | copy-start | bytes 49156
  34.1 74.4 %copy-start.8 = (bf16[112,4096]{1,0:T(8,128)(2,1)S(1)}, bf16[112,4096]{1,0:T(8,128)(2,1)}, u32[]{:S(2)}) copy-start(bf16[112,4096]{1,0:T(8,128)(2,1)} %refs_8_) | copy-start | bytes 2752516
  34.1 60.2 %all-to-all-start = ((bf16[16,2,8192]{2,1,0:T(2,128)(2,1)}), bf16[16,2,8192]{2,1,0:T(2,128)(2,1)S(1)}, u32[]{:S(2)}, u32[]{:S(2)}) async-start(bf16[16,2,8192]{2,1,0:T(2,128)(2,1)} %reshape.79), calls=%async_computation | async-start | bytes 1048576 | tf_op jit(solution)/shard_map/all_to_all | solution.py:546
  38.5 41.9 %collective-permute-start.2 = (bf16[16,32,768]{2,1,0:T(8,128)(2,1)S(1)}, bf16[16,32,768]{2,1,0:T(8,128)(2,1)S(1)}, u32[]{:S(2)}, u32[]{:S(2)}) collective-permute-start(bf16[16,32,768]{2,1,0:T(8,128)(2,1)S(1)} %all_to_all.10.refs_0_), channel_id=1, source_target_pairs={{0,96},{16,112},{32,0},{48,16},{64,32},{80,48},{96,64},{112,80},{1... | collective-permute-start | bytes 2359304 | tf_op jit(solution)/shard_map/ppermute | solution.py:54
  48.4 26.8 %collective-permute-start.4 = (bf16[16,32,768]{2,1,0:T(8,128)(2,1)}, bf16[16,32,768]{2,1,0:T(8,128)(2,1)}, u32[]{:S(2)}, u32[]{:S(2)}) collective-permute-start(bf16[16,32,768]{2,1,0:T(8,128)(2,1)} %collective-permute-done.refs_1_), channel_id=1, source_target_pairs={{0,96},{16,112},{32,0},{48,16},{64,32},{80,48},{96,64},{112,80},{1... | collective-permute-start | bytes 2359304 | tf_op jit(solution)/shard_map/ppermute | solution.py:54
  51.2 24.1 %collective-permute-start.3 = (bf16[16,32,768]{2,1,0:T(8,128)(2,1)}, bf16[16,32,768]{2,1,0:T(8,128)(2,1)S(1)}, u32[]{:S(2)}, u32[]{:S(2)}) collective-permute-start(bf16[16,32,768]{2,1,0:T(8,128)(2,1)} %collective-permute-done.refs_1_), channel_id=1, source_target_pairs={{0,32},{16,48},{32,64},{48,80},{64,96},{80,112},{96,0},{112,16},{1... | collective-permute-start | bytes 2359304 | tf_op jit(solution)/shard_map/ppermute | solution.py:54
  51.2 38.7 %collective-permute-start.5 = (bf16[16,32,768]{2,1,0:T(8,128)(2,1)}, bf16[16,32,768]{2,1,0:T(8,128)(2,1)S(1)}, u32[]{:S(2)}, u32[]{:S(2)}) collective-permute-start(bf16[16,32,768]{2,1,0:T(8,128)(2,1)} %collective-permute-done.1.refs_2_), channel_id=1, source_target_pairs={{0,32},{16,48},{32,64},{48,80},{64,96},{80,112},{96,0},{112,16},{1... | collective-permute-start | bytes 2359304 | tf_op jit(solution)/shard_map/ppermute | solution.py:54
  75.3 15.4 %copy-start.15 = (bf16[16,32,768]{2,1,0:T(8,128)(2,1)}, bf16[16,32,768]{2,1,0:T(8,128)(2,1)S(1)}, u32[]{:S(2)}) copy-start(bf16[16,32,768]{2,1,0:T(8,128)(2,1)S(1)} %collective-permute-done.3.refs_4_) | copy-start | bytes 2359300
  75.3 33.3 %collective-permute-start.7 = (bf16[112,4096]{1,0:T(8,128)(2,1)S(1)}, bf16[112,4096]{1,0:T(8,128)(2,1)}, u32[]{:S(2)}, u32[]{:S(2)}) collective-permute-start(bf16[112,4096]{1,0:T(8,128)(2,1)S(1)} %copy-done.7), channel_id=1, source_target_pairs={{0,16},{16,0},{32,48},{48,32},{64,80},{80,64},{96,112},{112,96},{1... | collective-permute-start | bytes 2752520 | tf_op jit(solution)/shard_map/ppermute | solution.py:54
  76.0 45.3 %collective-permute-start.8 = (bf16[112,4096]{1,0:T(8,128)(2,1)S(1)}, bf16[112,4096]{1,0:T(8,128)(2,1)}, u32[]{:S(2)}, u32[]{:S(2)}) collective-permute-start(bf16[112,4096]{1,0:T(8,128)(2,1)S(1)} %copy-done.7), channel_id=1, source_target_pairs={{0,32},{16,48},{32,64},{48,80},{64,96},{80,112},{96,0},{112,16},{1... | collective-permute-start | bytes 2752520 | tf_op jit(solution)/shard_map/ppermute | solution.py:54
  77.5 40.9 %collective-permute-start.14 = (bf16[112,4096]{1,0:T(8,128)(2,1)}, bf16[112,4096]{1,0:T(8,128)(2,1)}, u32[]{:S(2)}, u32[]{:S(2)}) collective-permute-start(bf16[112,4096]{1,0:T(8,128)(2,1)} %refs_8_), channel_id=1, source_target_pairs={{0,16},{16,0},{32,48},{48,32},{64,80},{80,64},{96,112},{112,96},{1... | collective-permute-start | bytes 2752520 | tf_op jit(solution)/shard_map/ppermute | solution.py:54
  80.4 10.3 %copy-start.14 = (bf16[16,32,768]{2,1,0:T(8,128)(2,1)}, bf16[16,32,768]{2,1,0:T(8,128)(2,1)S(1)}, u32[]{:S(2)}) copy-start(bf16[16,32,768]{2,1,0:T(8,128)(2,1)S(1)} %collective-permute-done.2.refs_3_) | copy-start | bytes 2359300
  80.4 46.2 %collective-permute-start.15 = (bf16[112,4096]{1,0:T(8,128)(2,1)}, bf16[112,4096]{1,0:T(8,128)(2,1)}, u32[]{:S(2)}, u32[]{:S(2)}) collective-permute-start(bf16[112,4096]{1,0:T(8,128)(2,1)} %refs_8_), channel_id=1, source_target_pairs={{0,32},{16,48},{32,64},{48,80},{64,96},{80,112},{96,0},{112,16},{1... | collective-permute-start | bytes 2752520 | tf_op jit(solution)/shard_map/ppermute | solution.py:54
  89.9 1.4 copy-start.16
  89.9 18.6 %collective-permute-start.6 = (bf16[16,32,768]{2,1,0:T(8,128)(2,1)}, bf16[16,32,768]{2,1,0:T(8,128)(2,1)}, u32[]{:S(2)}, u32[]{:S(2)}) collective-permute-start(bf16[16,32,768]{2,1,0:T(8,128)(2,1)} %collective-permute-done.4.refs_5_), channel_id=1, source_target_pairs={{0,96},{16,112},{32,0},{48,16},{64,32},{80,48},{96,64},{112,80},{1... | collective-permute-start | bytes 2359304 | tf_op jit(solution)/shard_map/ppermute | solution.py:54
  108.5 52.6 %collective-permute-start.16 = (bf16[112,4096]{1,0:T(8,128)(2,1)S(1)}, bf16[112,4096]{1,0:T(8,128)(2,1)S(1)}, u32[]{:S(2)}, u32[]{:S(2)}) collective-permute-start(bf16[112,4096]{1,0:T(8,128)(2,1)S(1)} %copy-done.8), channel_id=1, source_target_pairs={{0,96},{16,112},{32,0},{48,16},{64,32},{80,48},{96,64},{112,80},{1... | collective-permute-start | bytes 2752520 | tf_op jit(solution)/shard_map/ppermute | solution.py:54
  108.5 54.6 %collective-permute-start.9 = (bf16[112,4096]{1,0:T(8,128)(2,1)S(1)}, bf16[112,4096]{1,0:T(8,128)(2,1)S(1)}, u32[]{:S(2)}, u32[]{:S(2)}) collective-permute-start(bf16[112,4096]{1,0:T(8,128)(2,1)S(1)} %copy-done.7), channel_id=1, source_target_pairs={{0,96},{16,112},{32,0},{48,16},{64,32},{80,48},{96,64},{112,80},{1... | collective-permute-start | bytes 2752520 | tf_op jit(solution)/shard_map/ppermute | solution.py:54
  118.4 52.6 %collective-permute-start.11 = (bf16[112,4096]{1,0:T(8,128)(2,1)}, bf16[112,4096]{1,0:T(8,128)(2,1)S(1)}, u32[]{:S(2)}, u32[]{:S(2)}) collective-permute-start(bf16[112,4096]{1,0:T(8,128)(2,1)} %collective-permute-done.7.refs_1_), channel_id=1, source_target_pairs={{0,96},{16,112},{32,0},{48,16},{64,32},{80,48},{96,64},{112,80},{1... | collective-permute-start | bytes 2752520 | tf_op jit(solution)/shard_map/ppermute | solution.py:54
  121.3 66.8 %collective-permute-start.10 = (bf16[112,4096]{1,0:T(8,128)(2,1)}, bf16[112,4096]{1,0:T(8,128)(2,1)}, u32[]{:S(2)}, u32[]{:S(2)}) collective-permute-start(bf16[112,4096]{1,0:T(8,128)(2,1)} %collective-permute-done.7.refs_1_), channel_id=1, source_target_pairs={{0,32},{16,48},{32,64},{48,80},{64,96},{80,112},{96,0},{112,16},{1... | collective-permute-start | bytes 2752520 | tf_op jit(solution)/shard_map/ppermute | solution.py:54
  126.5 61.6 %collective-permute-start.18 = (bf16[112,4096]{1,0:T(8,128)(2,1)}, bf16[112,4096]{1,0:T(8,128)(2,1)}, u32[]{:S(2)}, u32[]{:S(2)}) collective-permute-start(bf16[112,4096]{1,0:T(8,128)(2,1)} %collective-permute-done.14.refs_9_), channel_id=1, source_target_pairs={{0,96},{16,112},{32,0},{48,16},{64,32},{80,48},{96,64},{112,80},{1... | collective-permute-start | bytes 2752520 | tf_op jit(solution)/shard_map/ppermute | solution.py:54
  161.1 90.3 %copy-start.9 = (bf16[112,4096]{1,0:T(8,128)(2,1)}, bf16[112,4096]{1,0:T(8,128)(2,1)S(1)}, u32[]{:S(2)}) copy-start(bf16[112,4096]{1,0:T(8,128)(2,1)S(1)} %collective-permute-done.16.refs_11_) | copy-start | bytes 2752516
  161.2 90.4 %collective-permute-start.17 = (bf16[112,4096]{1,0:T(8,128)(2,1)}, bf16[112,4096]{1,0:T(8,128)(2,1)S(1)}, u32[]{:S(2)}, u32[]{:S(2)}) collective-permute-start(bf16[112,4096]{1,0:T(8,128)(2,1)} %collective-permute-done.14.refs_9_), channel_id=1, source_target_pairs={{0,32},{16,48},{32,64},{48,80},{64,96},{80,112},{96,0},{112,16},{1... | collective-permute-start | bytes 2752520 | tf_op jit(solution)/shard_map/ppermute | solution.py:54
  163.1 88.4 %copy-start.10 = (bf16[112,4096]{1,0:T(8,128)(2,1)}, bf16[112,4096]{1,0:T(8,128)(2,1)S(1)}, u32[]{:S(2)}) copy-start(bf16[112,4096]{1,0:T(8,128)(2,1)S(1)} %collective-permute-done.9.refs_3_) | copy-start | bytes 2752516
  163.1 88.4 %collective-permute-start.12 = (bf16[112,4096]{1,0:T(8,128)(2,1)}, bf16[112,4096]{1,0:T(8,128)(2,1)S(1)}, u32[]{:S(2)}, u32[]{:S(2)}) collective-permute-start(bf16[112,4096]{1,0:T(8,128)(2,1)} %collective-permute-done.8.refs_2_), channel_id=1, source_target_pairs={{0,32},{16,48},{32,64},{48,80},{64,96},{80,112},{96,0},{112,16},{1... | collective-permute-start | bytes 2752520 | tf_op jit(solution)/shard_map/ppermute | solution.py:54
  171.0 80.5 %copy-start.11 = (bf16[112,4096]{1,0:T(8,128)(2,1)}, bf16[112,4096]{1,0:T(8,128)(2,1)S(1)}, u32[]{:S(2)}) copy-start(bf16[112,4096]{1,0:T(8,128)(2,1)S(1)} %collective-permute-done.11.refs_5_) | copy-start | bytes 2752516
  171.0 80.6 %collective-permute-start.19 = (bf16[112,4096]{1,0:T(8,128)(2,1)}, bf16[112,4096]{1,0:T(8,128)(2,1)}, u32[]{:S(2)}, u32[]{:S(2)}) collective-permute-start(bf16[112,4096]{1,0:T(8,128)(2,1)} %collective-permute-done.15.refs_10_), channel_id=1, source_target_pairs={{0,32},{16,48},{32,64},{48,80},{64,96},{80,112},{96,0},{112,16},{1... | collective-permute-start | bytes 2752520 | tf_op jit(solution)/shard_map/ppermute | solution.py:54
  188.1 63.4 %collective-permute-start.13 = (bf16[112,4096]{1,0:T(8,128)(2,1)S(1)}, bf16[112,4096]{1,0:T(8,128)(2,1)}, u32[]{:S(2)}, u32[]{:S(2)}) collective-permute-start(bf16[112,4096]{1,0:T(8,128)(2,1)S(1)} %collective-permute-done.11.refs_5_), channel_id=1, source_target_pairs={{0,96},{16,112},{32,0},{48,16},{64,32},{80,48},{96,64},{112,80},{1... | collective-permute-start | bytes 2752520 | tf_op jit(solution)/shard_map/ppermute | solution.py:54
  188.2 63.4 %collective-permute-start.20 = (bf16[112,4096]{1,0:T(8,128)(2,1)}, bf16[112,4096]{1,0:T(8,128)(2,1)}, u32[]{:S(2)}, u32[]{:S(2)}) collective-permute-start(bf16[112,4096]{1,0:T(8,128)(2,1)} %collective-permute-done.18.refs_13_), channel_id=1, source_target_pairs={{0,96},{16,112},{32,0},{48,16},{64,32},{80,48},{96,64},{112,80},{1... | collective-permute-start | bytes 2752520 | tf_op jit(solution)/shard_map/ppermute | solution.py:54
  251.5 0.9 copy-start.12
  251.5 1.3 copy-start.13
  281.9 36.2 %copy-start.5 = (f32[1,4096]{1,0:T(1,128)S(1)}, f32[1,4096]{1,0:T(1,128)}, u32[]{:S(2)}) copy-start(f32[1,4096]{1,0:T(1,128)} %get-tuple-element.25) | copy-start | bytes 49156
  281.9 36.2 %copy-start.6 = (f32[1,4096]{1,0:T(1,128)S(1)}, f32[1,4096]{1,0:T(1,128)}, u32[]{:S(2)}) copy-start(f32[1,4096]{1,0:T(1,128)} %get-tuple-element.26) | copy-start | bytes 49156

commit v3 on v2

--- a/solution.py
+++ b/solution.py
@@ -46,18 +46,22 @@
     return [at(0, 0), at(0, 1), at(NX - 1, 0), at(1, 0), at(NX - 1, 1), at(1, 1), at(2, 0), at(2, 1)]
 
 
-def collect(own):
-    def send(value, dx, dw):
-        pairs = [
-            (x * NW + w, (x + dx) % NX * NW + (w + dw) % NW) for x in range(NX) for w in range(NW)
-        ]
-        return lax.ppermute(value, "req", pairs)
-
-    other = send(own, 0, 1)
-    before, after = send(own, 1, 0), send(own, NX - 1, 0)
-    before_other, after_other = send(other, 1, 0), send(other, NX - 1, 0)
-    far, far_other = send(before, 1, 0), send(after_other, NX - 1, 0)
-    return [own, other, before, after, before_other, after_other, far, far_other]
+def send(value, dx, dw):
+    pairs = [(x * NW + w, (x + dx) % NX * NW + (w + dw) % NW) for x in range(NX) for w in range(NW)]
+    return lax.ppermute(value, "req", pairs)
+
+
+def first_hop(own):
+    return [own, send(own, 0, 1), send(own, 1, 0), send(own, NX - 1, 0)]
+
+
+def second_hop(have):
+    other = have[1]
+    return have + [send(other, 1, 0), send(other, NX - 1, 0)]
+
+
+def third_hop(have):
+    return have + [send(have[2], 1, 0), send(have[5], NX - 1, 0)]
 
 
 def group_columns(g, lw):
@@ -261,23 +265,25 @@
 def channel_mix_kernel(
     len_ref, x_ref, first_ref, gain_ref, mix_ref, accept_ref, *refs,
 ):
-    keys, values = refs[:PIECES], refs[PIECES : 2 * PIECES]
-    terms_ref, gate_ref, last_ref = refs[2 * PIECES : 2 * PIECES + 3]
-    key_scr, value_scr, inner, acc_gate, hidden, key_sems, value_sems = refs[2 * PIECES + 3 :]
+    pieces = refs[:PIECES]
+    terms_ref, gate_ref, last_ref = refs[PIECES : PIECES + 3]
+    key_scr, value_scr, inner, acc_gate, hidden, key_sems, value_sems = refs[PIECES + 3 :]
     groups, rows, lw = x_ref.shape
-    units = keys[0].shape[0]
-
-    def fetch(pieces, scr, sems):
+    units = pieces[0].shape[0] // 2
+
+    def fetch(begin, scr, sems):
         copies = [
-            pltpu.make_async_copy(piece, scr.at[pl.ds(i * units, units)], sems.at[i])
+            pltpu.make_async_copy(
+                piece.at[pl.ds(begin, units)], scr.at[pl.ds(i * units, units)], sems.at[i]
+            )
             for i, piece in enumerate(pieces)
         ]
         for copy in copies:
             copy.start()
         return copies
 
-    key_copies = fetch(keys, key_scr, key_sems)
-    value_copies = fetch(values, value_scr, value_sems)
+    key_copies = fetch(0, key_scr, key_sems)
+    value_copies = fetch(units, value_scr, value_sems)
 
     def part(g):
         return x_ref[g].astype(F32)
@@ -311,9 +317,9 @@
     lax.fori_loop(0, groups, leave, 0)
 
 
-def channel_mix(length, x, first, gains, mixes, accept, keys, values):
+def channel_mix(length, x, first, gains, mixes, accept, pieces):
     groups, rows, lw = x.shape
-    units = PIECES * keys[0].shape[0]
+    units = PIECES * pieces[0].shape[0] // 2
     width = groups * lw
     return pl.pallas_call(
         channel_mix_kernel,
@@ -322,7 +328,7 @@
             jax.ShapeDtypeStruct((rows, lw), F32),
             jax.ShapeDtypeStruct((1, groups * lw), F32),
         ),
-        in_specs=[SM] + [VM] * 5 + [HB] * (2 * PIECES),
+        in_specs=[SM] + [VM] * 5 + [HB] * PIECES,
         out_specs=(VM, VM, VM),
         scratch_shapes=[
             pltpu.VMEM((units, width), BF16),
@@ -336,7 +342,7 @@
         compiler_params=pltpu.CompilerParams(vmem_limit_bytes=VMEM_LIMIT),
         cost_estimate=COST,
         name="channel_mix",
-    )(length, x, first, gains, mixes, accept, *keys, *values)
+    )(length, x, first, gains, mixes, accept, *pieces)
 
 
 def hid_place():
@@ -549,12 +555,10 @@
     )
     chosen = lax.dynamic_index_in_dim(fetched, owning_index[0], 0, keepdims=False)
     s0 = jnp.where(resuming == 1, chosen.astype(F32), 0.0)
-    pieces = collect(swapped)
-    entry, exit_proj, pieces[4], pieces[5] = lax.optimization_barrier(
-        (feedforward_entry_proj, feedforward_exit_proj, pieces[4], pieces[5])
-    )
-    keys = collect(entry)
-    values = collect(exit_proj)
+    both = first_hop(jnp.concatenate([feedforward_entry_proj, feedforward_exit_proj]))
+    pieces = third_hop(second_hop(first_hop(swapped)))
+    pieces, both = lax.optimization_barrier((pieces, both))
+    both = second_hop(both)
 
     terms, state, last_in = time_mix(
         partition_arrangement, prompt_extents, x, carried[0:1], gains, prior_step_blends,
@@ -562,11 +566,13 @@
         forgetting_bias_vector[None], instant_emphasis[None], group_normalizer_scale[None],
         s0, mixing_exit_projection, pieces,
     )
+    terms, both = lax.optimization_barrier((terms, both))
+    both = third_hop(both)
     x_share = lax.dynamic_slice_in_dim(x, lax.axis_index("hid") * lw, lw, 1)
     middle, own_middle = join(terms, x_share)
     out_terms, gate_rows, last_chan = channel_mix(
         prompt_extents, middle.reshape(hid, rows, lw), carried[1:2], gains, prior_step_blends,
-        feedforward_accept_proj, keys, values,
+        feedforward_accept_proj, both,
     )
     layer_out = close(prompt_extents, out_terms, own_middle, gate_rows)[None]
     shift_out = jnp.concatenate([last_in, last_chan]).astype(BF16)[None]

time: 321 us -> 313 us (0.975)
  blocking collectives: 20 us -> 0 us
  starting transfers between devices: 25 us -> 31.6 us
  local copies, waits for them, and re-layouts: 10.1 us -> 13.9 us
    all_to_all x1 -> x0, blocking collectives: 20 us -> none  [local(): lax.all_to_all(own, 'hid', split_axis=0, concat_axis=0, tiled=True)]
    all_to_all x0 -> x1, waiting for transfers between devices: none -> 7.82 us  [local(): lax.all_to_all(own, 'hid', split_axis=0, concat_axis=0, tiled=True)]
    all_to_all x0 -> x1, starting transfers between devices: none -> 6.69 us  [local(): lax.all_to_all(own, 'hid', split_axis=0, concat_axis=0, tiled=True)]
    ppermute x21 -> x14, waiting for transfers between devices: 92.6 us -> 87.3 us  [send(): return lax.ppermute(value, 'req', pairs)]
    ppermute x21 -> x14, starting transfers between devices: 21.3 us -> 21.3 us  [send(): return lax.ppermute(value, 'req', pairs)]
  transfers between devices with their start and end apart: 22 -> 16, of which waited for: 8 -> 6; matrix products, arithmetic and copies ran while one was open for 2% -> 3% of each run, Pallas kernels for 31% -> 32%
where the time goes in v3:
time: 313 us; the launch traced here: 312 us
  Pallas kernels  163 us (52%)
  waiting for transfers between devices  95.1 us (30%)
  starting transfers between devices  31.6 us (10%)
  local copies, waits for them, and re-layouts  13.9 us (4%)
  other arithmetic  5.18 us (2%)
    ppermute x14, waiting for transfers between devices, send(): return lax.ppermute(value, 'req', pairs)  87.3 us
    pallas_call x1, Pallas kernels, join(): pl.pallas_call(join_kernel, out_shape=(jax.ShapeDtypeStruct(shape, BF16),...  65.6 us
    pallas_call x1, Pallas kernels, time_mix(): pl.pallas_call(time_mix_kernel, out_shape=(jax.ShapeDtypeStruct((width //...  34.5 us
    pallas_call x1, Pallas kernels, close(): pl.pallas_call(close_kernel, out_shape=jax.ShapeDtypeStruct((rows, lw), B...  33.8 us
    pallas_call x1, Pallas kernels, channel_mix(): pl.pallas_call(channel_mix_kernel, out_shape=(jax.ShapeDtypeStruct((group...  29.1 us
    ppermute x14, starting transfers between devices, send(): return lax.ppermute(value, 'req', pairs)  21.3 us
    all_to_all x1, waiting for transfers between devices, local(): lax.all_to_all(own, 'hid', split_axis=0, concat_axis=0, tiled=True)  7.82 us
    all_to_all x1, starting transfers between devices, local(): lax.all_to_all(own, 'hid', split_axis=0, concat_axis=0, tiled=True)  6.69 us
  transfers between devices with their start and end apart: 16, of which 6 were waited for; matrix products, arithmetic and copies ran while one was open for 3% of the time, Pallas kernels for 32%

profile of v3, /device:TPU:0, one launch (start us, length us, event | category | flops | bytes accessed | tf_op | source)
XLA Modules:
  0.0 311.7 jit_solution(5368971740004555593)
XLA Ops:
  0.6 0.0 copy-start.2
  0.6 0.0 copy-start.3
  0.7 1.2 convert.20
  1.9 0.5 copy.28
  2.5 0.5 copy.29
  3.1 0.5 copy.30
  3.6 1.8 maximum_bitcast_fusion
  5.4 1.7 reshape.75
  7.1 6.7 %all-to-all-start.1 = ((bf16[16,32,768]{2,1,0:T(8,128)(2,1)}), bf16[16,32,768]{2,1,0:T(8,128)(2,1)}, u32[]{:S(2)}, u32[]{:S(2)}) async-start(bf16[16,32,768]{2,1,0:T(8,128)(2,1)} %reshape.75), calls=%async_computation.1 | async-start | bytes 1572864 | tf_op jit(solution)/shard_map/all_to_all | solution.py:551
  13.8 0.0 copy-start
  13.8 1.0 constant_dynamic-update-slice_fusion.1
  14.8 2.2 constant_dynamic-update-slice_fusion.refs_0_
  17.0 2.8 collective-permute-start.9
  19.8 7.8 %all-to-all-done.1.refs_0_ = bf16[16,32,768]{2,1,0:T(8,128)(2,1)} async-done(((bf16[16,32,768]{2,1,0:T(8,128)(2,1)}), bf16[16,32,768]{2,1,0:T(8,128)(2,1)}, u32[]{:S(2)}, u32[]{:S(2)}) %all-to-all-start.1) | async-done | bytes 786464 | tf_op jit(solution)/shard_map/all_to_all | solution.py:551
  27.6 2.8 collective-permute-start.2
  30.4 2.9 collective-permute-start
  33.3 0.0 collective-permute-start.8
  33.3 0.6 collective-permute-start.7
  33.9 0.0 copy-done
  33.9 0.2 convert_element_type.30
  34.1 0.0 copy-start.4
  34.1 0.0 copy-start.5
  34.1 1.5 reshape.79
  35.6 3.6 %all-to-all-start = ((bf16[16,2,8192]{2,1,0:T(2,128)(2,1)}), bf16[16,2,8192]{2,1,0:T(2,128)(2,1)S(1)}, u32[]{:S(2)}, u32[]{:S(2)}) async-start(bf16[16,2,8192]{2,1,0:T(2,128)(2,1)} %reshape.79), calls=%async_computation | async-start | bytes 1048576 | tf_op jit(solution)/shard_map/all_to_all | solution.py:552
  39.9 36.9 %collective-permute-done.2.refs_3_ = bf16[16,32,768]{2,1,0:T(8,128)(2,1)} collective-permute-done((bf16[16,32,768]{2,1,0:T(8,128)(2,1)}, bf16[16,32,768]{2,1,0:T(8,128)(2,1)}, u32[]{:S(2)}, u32[]{:S(2)}) %collective-permute-start.2) | collective-permute-done | bytes 786464 | tf_op jit(solution)/shard_map/ppermute | solution.py:51
  76.7 1.2 collective-permute-start.1
  77.9 0.0 collective-permute-done.refs_1_
  77.9 2.5 collective-permute-start.4
  80.5 17.4 %collective-permute-done.1.refs_2_ = bf16[16,32,768]{2,1,0:T(8,128)(2,1)S(1)} collective-permute-done((bf16[16,32,768]{2,1,0:T(8,128)(2,1)}, bf16[16,32,768]{2,1,0:T(8,128)(2,1)S(1)}, u32[]{:S(2)}, u32[]{:S(2)}) %collective-permute-start.1) | collective-permute-done | bytes 786464 | tf_op jit(solution)/shard_map/ppermute | solution.py:51
  97.9 0.0 collective-permute-start.3
  97.9 0.0 collective-permute-done.9.refs_3_
  97.9 0.8 collective-permute-start.5
  98.7 0.0 collective-permute-done.4.refs_5_
  98.7 2.5 collective-permute-start.6
  101.2 0.6 slice_bitcast_fusion
  103.2 0.6 convert_element_type.29.gain_ref
  103.8 1.7 dynamic-slice_bitcast_fusion.x_ref
  105.4 0.0 all-to-all-done
  105.4 0.7 reshape.80
  106.1 0.7 select_bitcast_fusion.s0_ref
  106.8 0.0 collective-permute-done.8.refs_2_
  106.8 0.0 collective-permute-done.7.refs_1_
  106.8 27.9 %collective-permute-done.5.refs_6_ = bf16[16,32,768]{2,1,0:T(8,128)(2,1)} collective-permute-done((bf16[16,32,768]{2,1,0:T(8,128)(2,1)S(1)}, bf16[16,32,768]{2,1,0:T(8,128)(2,1)}, u32[]{:S(2)}, u32[]{:S(2)}) %collective-permute-start.5) | collective-permute-done | bytes 786464 | tf_op jit(solution)/shard_map/ppermute | solution.py:51
  134.7 0.0 collective-permute-done.3.refs_4_
  134.7 0.0 collective-permute-done.6.refs_7_
  134.7 0.2 collective-permute-start.11
  134.9 1.8 collective-permute-start.10
  136.7 0.0 copy-done.12
  136.7 34.5 %time_mix.1 = (bf16[16,512,256]{2,1,0:T(8,128)(2,1)}, f32[4,64,64]{2,1,0:T(8,128)}, f32[1,4096]{1,0:T(1,128)}) custom-call(s32[128]{0:T(128)} %perm_ref.1, s32[1]{0:T(128)S(6)} %copy.36.len_ref, bf16[512,4096]{1,0:T(8,128)(2,1)} %bitcast.47, f32[1,4096]{1,0:T(1,128)} %get-tuple-element.58.first_ref, f32[2,4096]{1,0:T(2,128)} %convert_element_type.29.gain_ref, ...), custom_call_target="tpu_custom_call" | custom-call | flops 40000000000 | bytes 40000000 | tf_op jit(solution)/shard_map/time_mix/pallas_call | solution.py:239
  171.2 3.6 %collective-permute-done.11.refs_5_ = bf16[224,4096]{1,0:T(8,128)(2,1)S(1)} collective-permute-done((bf16[224,4096]{1,0:T(8,128)(2,1)}, bf16[224,4096]{1,0:T(8,128)(2,1)S(1)}, u32[]{:S(2)}, u32[]{:S(2)}) %collective-permute-start.11) | collective-permute-done | bytes 1835040 | tf_op jit(solution)/shard_map/ppermute | solution.py:51
  174.8 1.5 collective-permute-done.10.refs_4_
  176.3 0.3 collective-permute-start.12
  176.6 2.9 collective-permute-start.13
  179.5 65.6 %join.1 = (bf16[2,4,2,512,256]{4,3,2,1,0:T(8,128)(2,1)}, bf16[512,256]{1,0:T(8,128)(2,1)}) custom-call(bf16[2,4,2,512,256]{4,3,2,1,0:T(8,128)(2,1)} %bitcast.51, bf16[512,256]{1,0:T(8,128)(2,1)} %dynamic-slice_bitcast_fusion.x_ref), custom_call_target="tpu_custom_call" | custom-call | flops 40000000000 | bytes 40000000 | tf_op jit(solution)/shard_map/join/pallas_call | solution.py:472
  245.1 0.0 collective-permute-done.12.refs_6_
  245.2 0.0 copy-start.10
  245.2 0.0 collective-permute-done.13.refs_7_
  245.2 1.2 copy-done.10
  246.4 29.1 %channel_mix.1 = (bf16[16,512,256]{2,1,0:T(8,128)(2,1)}, f32[512,256]{1,0:T(8,128)}, f32[1,4096]{1,0:T(1,128)}) custom-call(s32[1]{0:T(128)S(6)} %copy.36.len_ref, bf16[16,512,256]{2,1,0:T(8,128)(2,1)} %bitcast.52, f32[1,4096]{1,0:T(1,128)} %get-tuple-element.57.first_ref, f32[2,4096]{1,0:T(2,128)} %convert_element_type.29.gain_ref, ...), custom_call_target="tpu_custom_call" | custom-call | flops 40000000000 | bytes 40000000 | tf_op jit(solution)/shard_map/channel_mix/pallas_call | solution.py:324
  275.5 0.0 copy-start.6
  275.5 0.0 copy-start.7
  275.5 33.8 %close.1 = bf16[512,256]{1,0:T(8,128)(2,1)} custom-call(s32[1]{0:T(128)S(6)} %copy.36.len_ref, bf16[2,4,2,512,256]{4,3,2,1,0:T(8,128)(2,1)} %bitcast.39, bf16[512,256]{1,0:T(8,128)(2,1)} %get-tuple-element.52.own_ref, f32[512,256]{1,0:T(8,128)} %get-tuple-element.53.gate_ref), custom_call_target="tpu_custom_call" | custom-call | tf_op jit(solution)/shard_map/close/pallas_call | solution.py:502
  309.4 0.6 pad_maximum_fusion
  310.0 1.7 copy.39
  (22 shorter events, 0.3 us)
Async XLA Ops:
  0.6 1.7 copy-start.2
  0.6 2.3 copy-start.3
  7.1 6.7 %copy-start.1 = (bf16[112,4096]{1,0:T(8,128)(2,1)S(1)}, bf16[112,4096]{1,0:T(8,128)(2,1)}, u32[]{:S(2)}) copy-start(bf16[112,4096]{1,0:T(8,128)(2,1)} %param.41) | copy-start | bytes 2752516
  7.1 20.5 %all-to-all-start.1 = ((bf16[16,32,768]{2,1,0:T(8,128)(2,1)}), bf16[16,32,768]{2,1,0:T(8,128)(2,1)}, u32[]{:S(2)}, u32[]{:S(2)}) async-start(bf16[16,32,768]{2,1,0:T(8,128)(2,1)} %reshape.75), calls=%async_computation.1 | async-start | bytes 1572864 | tf_op jit(solution)/shard_map/all_to_all | solution.py:551
  13.8 20.1 %copy-start = (f32[1,1,64,64,64]{4,3,2,1,0:T(8,128)S(1)}, f32[1,1,64,64,64]{4,3,2,1,0:T(8,128)}, u32[]{:S(2)}) copy-start(f32[1,1,64,64,64]{4,3,2,1,0:T(8,128)} %param.39) | copy-start | bytes 3145732
  17.0 80.9 %collective-permute-start.9 = (bf16[224,4096]{1,0:T(8,128)(2,1)}, bf16[224,4096]{1,0:T(8,128)(2,1)}, u32[]{:S(2)}, u32[]{:S(2)}) collective-permute-start(bf16[224,4096]{1,0:T(8,128)(2,1)} %constant_dynamic-update-slice_fusion.refs_0_), channel_id=1, source_target_pairs={{0,96},{16,112},{32,0},{48,16},{64,32},{80,48},{96,64},{112,80},{1... | collective-permute-start | bytes 5505032 | tf_op jit(solution)/shard_map/ppermute | solution.py:51
  27.6 49.1 %collective-permute-start.2 = (bf16[16,32,768]{2,1,0:T(8,128)(2,1)}, bf16[16,32,768]{2,1,0:T(8,128)(2,1)}, u32[]{:S(2)}, u32[]{:S(2)}) collective-permute-start(bf16[16,32,768]{2,1,0:T(8,128)(2,1)} %all-to-all-done.1.refs_0_), channel_id=1, source_target_pairs={{0,96},{16,112},{32,0},{48,16},{64,32},{80,48},{96,64},{112,80},{1... | collective-permute-start | bytes 2359304 | tf_op jit(solution)/shard_map/ppermute | solution.py:51
  30.4 47.6 %collective-permute-start = (bf16[16,32,768]{2,1,0:T(8,128)(2,1)}, bf16[16,32,768]{2,1,0:T(8,128)(2,1)}, u32[]{:S(2)}, u32[]{:S(2)}) collective-permute-start(bf16[16,32,768]{2,1,0:T(8,128)(2,1)} %all-to-all-done.1.refs_0_), channel_id=1, source_target_pairs={{0,16},{16,0},{32,48},{48,32},{64,80},{80,64},{96,112},{112,96},{1... | collective-permute-start | bytes 2359304 | tf_op jit(solution)/shard_map/ppermute | solution.py:51
  33.3 73.5 %collective-permute-start.8 = (bf16[224,4096]{1,0:T(8,128)(2,1)}, bf16[224,4096]{1,0:T(8,128)(2,1)}, u32[]{:S(2)}, u32[]{:S(2)}) collective-permute-start(bf16[224,4096]{1,0:T(8,128)(2,1)} %constant_dynamic-update-slice_fusion.refs_0_), channel_id=1, source_target_pairs={{0,32},{16,48},{32,64},{48,80},{64,96},{80,112},{96,0},{112,16},{1... | collective-permute-start | bytes 5505032 | tf_op jit(solution)/shard_map/ppermute | solution.py:51
  33.3 73.5 %collective-permute-start.7 = (bf16[224,4096]{1,0:T(8,128)(2,1)}, bf16[224,4096]{1,0:T(8,128)(2,1)}, u32[]{:S(2)}, u32[]{:S(2)}) collective-permute-start(bf16[224,4096]{1,0:T(8,128)(2,1)} %constant_dynamic-update-slice_fusion.refs_0_), channel_id=1, source_target_pairs={{0,16},{16,0},{32,48},{48,32},{64,80},{80,64},{96,112},{112,96},{1... | collective-permute-start | bytes 5505032 | tf_op jit(solution)/shard_map/ppermute | solution.py:51
  34.1 46.3 %copy-start.4 = (bf16[1,2,4096]{2,1,0:T(2,128)(2,1)S(1)}, bf16[1,2,4096]{2,1,0:T(2,128)(2,1)}, u32[]{:S(2)}) copy-start(bf16[1,2,4096]{2,1,0:T(2,128)(2,1)} %param.40) | copy-start | bytes 49156
  34.1 69.0 %copy-start.5 = (bf16[2,4096]{1,0:T(2,128)(2,1)S(1)}, bf16[2,4096]{1,0:T(2,128)(2,1)}, u32[]{:S(2)}) copy-start(bf16[2,4096]{1,0:T(2,128)(2,1)} %param.30) | copy-start | bytes 49156
  35.6 69.8 %all-to-all-start = ((bf16[16,2,8192]{2,1,0:T(2,128)(2,1)}), bf16[16,2,8192]{2,1,0:T(2,128)(2,1)S(1)}, u32[]{:S(2)}, u32[]{:S(2)}) async-start(bf16[16,2,8192]{2,1,0:T(2,128)(2,1)} %reshape.79), calls=%async_computation | async-start | bytes 1048576 | tf_op jit(solution)/shard_map/all_to_all | solution.py:552
  76.7 21.2 %collective-permute-start.1 = (bf16[16,32,768]{2,1,0:T(8,128)(2,1)}, bf16[16,32,768]{2,1,0:T(8,128)(2,1)S(1)}, u32[]{:S(2)}, u32[]{:S(2)}) collective-permute-start(bf16[16,32,768]{2,1,0:T(8,128)(2,1)} %all-to-all-done.1.refs_0_), channel_id=1, source_target_pairs={{0,32},{16,48},{32,64},{48,80},{64,96},{80,112},{96,0},{112,16},{1... | collective-permute-start | bytes 2359304 | tf_op jit(solution)/shard_map/ppermute | solution.py:51
  77.9 20.7 %collective-permute-start.4 = (bf16[16,32,768]{2,1,0:T(8,128)(2,1)}, bf16[16,32,768]{2,1,0:T(8,128)(2,1)S(1)}, u32[]{:S(2)}, u32[]{:S(2)}) collective-permute-start(bf16[16,32,768]{2,1,0:T(8,128)(2,1)} %collective-permute-done.refs_1_), channel_id=1, source_target_pairs={{0,96},{16,112},{32,0},{48,16},{64,32},{80,48},{96,64},{112,80},{1... | collective-permute-start | bytes 2359304 | tf_op jit(solution)/shard_map/ppermute | solution.py:51
  97.9 38.8 %copy-start.11 = (bf16[16,32,768]{2,1,0:T(8,128)(2,1)}, bf16[16,32,768]{2,1,0:T(8,128)(2,1)S(1)}, u32[]{:S(2)}) copy-start(bf16[16,32,768]{2,1,0:T(8,128)(2,1)S(1)} %collective-permute-done.1.refs_2_) | copy-start | bytes 2359300
  97.9 36.8 %collective-permute-start.3 = (bf16[16,32,768]{2,1,0:T(8,128)(2,1)}, bf16[16,32,768]{2,1,0:T(8,128)(2,1)}, u32[]{:S(2)}, u32[]{:S(2)}) collective-permute-start(bf16[16,32,768]{2,1,0:T(8,128)(2,1)} %collective-permute-done.refs_1_), channel_id=1, source_target_pairs={{0,32},{16,48},{32,64},{48,80},{64,96},{80,112},{96,0},{112,16},{1... | collective-permute-start | bytes 2359304 | tf_op jit(solution)/shard_map/ppermute | solution.py:51
  97.9 36.8 %collective-permute-start.5 = (bf16[16,32,768]{2,1,0:T(8,128)(2,1)S(1)}, bf16[16,32,768]{2,1,0:T(8,128)(2,1)}, u32[]{:S(2)}, u32[]{:S(2)}) collective-permute-start(bf16[16,32,768]{2,1,0:T(8,128)(2,1)S(1)} %collective-permute-done.1.refs_2_), channel_id=1, source_target_pairs={{0,32},{16,48},{32,64},{48,80},{64,96},{80,112},{96,0},{112,16},{1... | collective-permute-start | bytes 2359304 | tf_op jit(solution)/shard_map/ppermute | solution.py:51
  98.7 38.0 %copy-start.12 = (bf16[16,32,768]{2,1,0:T(8,128)(2,1)}, bf16[16,32,768]{2,1,0:T(8,128)(2,1)S(1)}, u32[]{:S(2)}) copy-start(bf16[16,32,768]{2,1,0:T(8,128)(2,1)S(1)} %collective-permute-done.4.refs_5_) | copy-start | bytes 2359300
  98.7 36.0 %collective-permute-start.6 = (bf16[16,32,768]{2,1,0:T(8,128)(2,1)S(1)}, bf16[16,32,768]{2,1,0:T(8,128)(2,1)}, u32[]{:S(2)}, u32[]{:S(2)}) collective-permute-start(bf16[16,32,768]{2,1,0:T(8,128)(2,1)S(1)} %collective-permute-done.4.refs_5_), channel_id=1, source_target_pairs={{0,96},{16,112},{32,0},{48,16},{64,32},{80,48},{96,64},{112,80},{1... | collective-permute-start | bytes 2359304 | tf_op jit(solution)/shard_map/ppermute | solution.py:51
  134.7 40.2 %collective-permute-start.11 = (bf16[224,4096]{1,0:T(8,128)(2,1)}, bf16[224,4096]{1,0:T(8,128)(2,1)S(1)}, u32[]{:S(2)}, u32[]{:S(2)}) collective-permute-start(bf16[224,4096]{1,0:T(8,128)(2,1)} %collective-permute-done.7.refs_1_), channel_id=1, source_target_pairs={{0,96},{16,112},{32,0},{48,16},{64,32},{80,48},{96,64},{112,80},{1... | collective-permute-start | bytes 5505032 | tf_op jit(solution)/shard_map/ppermute | solution.py:51
  134.9 41.4 %collective-permute-start.10 = (bf16[224,4096]{1,0:T(8,128)(2,1)}, bf16[224,4096]{1,0:T(8,128)(2,1)S(1)}, u32[]{:S(2)}, u32[]{:S(2)}) collective-permute-start(bf16[224,4096]{1,0:T(8,128)(2,1)} %collective-permute-done.7.refs_1_), channel_id=1, source_target_pairs={{0,32},{16,48},{32,64},{48,80},{64,96},{80,112},{96,0},{112,16},{1... | collective-permute-start | bytes 5505032 | tf_op jit(solution)/shard_map/ppermute | solution.py:51
  174.8 70.3 %copy-start.8 = (bf16[224,4096]{1,0:T(8,128)(2,1)}, bf16[224,4096]{1,0:T(8,128)(2,1)S(1)}, u32[]{:S(2)}) copy-start(bf16[224,4096]{1,0:T(8,128)(2,1)S(1)} %collective-permute-done.11.refs_5_) | copy-start | bytes 5505028
  176.3 68.8 %copy-start.9 = (bf16[224,4096]{1,0:T(8,128)(2,1)}, bf16[224,4096]{1,0:T(8,128)(2,1)S(1)}, u32[]{:S(2)}) copy-start(bf16[224,4096]{1,0:T(8,128)(2,1)S(1)} %collective-permute-done.10.refs_4_) | copy-start | bytes 5505028
  176.3 68.9 %collective-permute-start.12 = (bf16[224,4096]{1,0:T(8,128)(2,1)}, bf16[224,4096]{1,0:T(8,128)(2,1)S(1)}, u32[]{:S(2)}, u32[]{:S(2)}) collective-permute-start(bf16[224,4096]{1,0:T(8,128)(2,1)} %collective-permute-done.8.refs_2_), channel_id=1, source_target_pairs={{0,32},{16,48},{32,64},{48,80},{64,96},{80,112},{96,0},{112,16},{1... | collective-permute-start | bytes 5505032 | tf_op jit(solution)/shard_map/ppermute | solution.py:51
  176.6 68.6 %collective-permute-start.13 = (bf16[224,4096]{1,0:T(8,128)(2,1)S(1)}, bf16[224,4096]{1,0:T(8,128)(2,1)}, u32[]{:S(2)}, u32[]{:S(2)}) collective-permute-start(bf16[224,4096]{1,0:T(8,128)(2,1)S(1)} %collective-permute-done.11.refs_5_), channel_id=1, source_target_pairs={{0,96},{16,112},{32,0},{48,16},{64,32},{80,48},{96,64},{112,80},{1... | collective-permute-start | bytes 5505032 | tf_op jit(solution)/shard_map/ppermute | solution.py:51
  245.2 1.2 copy-start.10
  275.5 33.8 %copy-start.6 = (f32[1,4096]{1,0:T(1,128)S(1)}, f32[1,4096]{1,0:T(1,128)}, u32[]{:S(2)}) copy-start(f32[1,4096]{1,0:T(1,128)} %get-tuple-element.55) | copy-start | bytes 49156
  275.5 33.8 %copy-start.7 = (f32[1,4096]{1,0:T(1,128)S(1)}, f32[1,4096]{1,0:T(1,128)}, u32[]{:S(2)}) copy-start(f32[1,4096]{1,0:T(1,128)} %get-tuple-element.56) | copy-start | bytes 49156

commit v4 on v3

--- a/solution.py
+++ b/solution.py
@@ -19,6 +19,7 @@
 NY, NZ, NC = 2, 4, 2
 NX, NW = 4, 2
 PIECES = NX * NW
+SPLIT = 9
 COST = pl.CostEstimate(flops=40_000_000_000, bytes_accessed=40_000_000, transcendentals=0)
 VM = pl.BlockSpec(memory_space=pltpu.VMEM)
 SM = pl.BlockSpec(memory_space=pltpu.SMEM)
@@ -37,22 +38,9 @@
     return jnp.dot(a, b, preferred_element_type=F32)
 
 
-def piece_owners():
-    x, w = lax.axis_index("req") // NW, lax.axis_index("req") % NW
-
-    def at(dx, other):
-        return (x + dx) % NX * NW + (1 - w if other else w)
-
-    return [at(0, 0), at(0, 1), at(NX - 1, 0), at(1, 0), at(NX - 1, 1), at(1, 1), at(2, 0), at(2, 1)]
-
-
 def send(value, dx, dw):
     pairs = [(x * NW + w, (x + dx) % NX * NW + (w + dw) % NW) for x in range(NX) for w in range(NW)]
     return lax.ppermute(value, "req", pairs)
-
-
-def first_hop(own):
-    return [own, send(own, 0, 1), send(own, 1, 0), send(own, NX - 1, 0)]
 
 
 def second_hop(have):
@@ -98,25 +86,21 @@
 
 def time_mix_kernel(
     perm_ref, len_ref, x_ref, first_ref, gain_ref, mix_ref, gating_ref, left_ref,
-    right_ref, bias_ref, bonus_ref, gscale_ref, s0_ref, exit_ref, *refs,
+    right_ref, bias_ref, bonus_ref, gscale_ref, s0_ref, exit_ref, w_ref,
+    terms_ref, state_ref, last_ref, share_ref,
+    w_scr, acc, acc_low, acc_gate, logw_scr, prod_scr, gated_scr, st_scr, sem,
 ):
-    pieces = refs[:PIECES]
-    terms_ref, state_ref, last_ref = refs[PIECES : PIECES + 3]
-    (
-        w_scr, acc, acc_low, acc_gate, logw_scr, prod_scr, gated_scr, st_scr, sem,
-    ) = refs[PIECES + 3 :]
     rows, width = x_ref.shape
-    block_rows = w_scr.shape[1]
+    block_rows = w_scr.shape[1] // 3
     lw = acc_gate.shape[1]
 
-    for piece, owner in zip(pieces, piece_owners()):
-        count = piece.shape[0]
-
-        def start(j, carry, piece=piece, base=owner * count):
-            pltpu.make_async_copy(piece.at[j], w_scr.at[perm_ref[base + j]], sem).start()
-            return carry
-
-        lax.fori_loop(0, count, start, 0)
+
+    def start(j, carry):
+        pltpu.make_async_copy(w_ref.at[j], w_scr.at[perm_ref[j]], sem).start()
+        return carry
+
+    lax.fori_loop(0, w_scr.shape[0], start, 0)
+    share_ref[...] = x_ref[:, pl.ds(pl.multiple_of(lax.axis_index("hid") * lw, lw), lw)]
 
     def part(c):
         return x_ref[:, pl.ds(pl.multiple_of(c * KC, KC), KC)].astype(F32)
@@ -138,7 +122,8 @@
             return (normed + delta * mix[m : m + 1]).astype(BF16)
 
         for m in range(3):
-            wm = w_scr[pl.ds(c * per, per), :, m * lw : (m + 1) * lw].reshape(KC, lw)
+            own_rows = slice(m * block_rows, (m + 1) * block_rows)
+            wm = w_scr[pl.ds(c * per, per), own_rows, :].reshape(KC, lw)
             acc[:, m * lw : (m + 1) * lw] += nn_dot(blend(m), wm)
         acc_low[...] += nn_dot(blend(3), left_ref[cols, :])
         acc_gate[...] += nn_dot(blend(4), gating_ref[cols, :])
@@ -153,19 +138,18 @@
     acc[:, lw : 2 * lw] = jnp.where(present, acc[:, lw : 2 * lw], 0.0)
 
     pairs = lw // PAIR
-    hole = jnp.zeros((HEAD, HEAD), F32)
-    for p in range(pairs):
-        top = jnp.concatenate([s0_ref[2 * p], hole], axis=1)
-        bottom = jnp.concatenate([hole, s0_ref[2 * p + 1]], axis=1)
-        st_scr[p] = jnp.concatenate([top, bottom], axis=0).T
 
     def same_head(size):
         a = lax.broadcasted_iota(jnp.int32, (size, size), 0) // HEAD
         b = lax.broadcasted_iota(jnp.int32, (size, size), 1) // HEAD
         return a == b
 
+    pair_mask = same_head(PAIR)
+    for p in range(pairs):
+        two = s0_ref[:, p * PAIR : (p + 1) * PAIR]
+        st_scr[p] = jnp.where(pair_mask, jnp.concatenate([two, two], axis=0), 0.0).T
+
     ones = jnp.where(same_head(lw), 1.0, 0.0).astype(BF16)
-    pair_mask = same_head(PAIR)
     slot = lax.broadcasted_iota(jnp.int32, (TILE, lw), 0) % CHUNK
 
     def head_sum(values):
@@ -232,21 +216,21 @@
     lax.fori_loop(0, width // lw, leave, 0)
 
 
-def time_mix(perm, length, x, first, gains, mixes, gating, left, right, bias, bonus, gscale, s0, exit_w, pieces):
+def time_mix(perm, length, x, first, gains, mixes, gating, left, right, bias, bonus, gscale, s0, exit_w, w):
     rows, width = x.shape
     lw = gating.shape[1]
-    piece_blocks, block_rows, piece_width = pieces[0].shape
     return pl.pallas_call(
         time_mix_kernel,
         out_shape=(
             jax.ShapeDtypeStruct((width // lw, rows, lw), BF16),
-            jax.ShapeDtypeStruct(s0.shape, F32),
+            jax.ShapeDtypeStruct((lw // HEAD, HEAD, HEAD), F32),
             jax.ShapeDtypeStruct((1, width), F32),
+            jax.ShapeDtypeStruct((rows, lw), BF16),
         ),
-        in_specs=[SM, SM] + [VM] * 12 + [HB] * PIECES,
-        out_specs=(VM, VM, VM),
+        in_specs=[SM, SM] + [VM] * 12 + [HB],
+        out_specs=(VM, VM, VM, VM),
         scratch_shapes=[
-            pltpu.VMEM((PIECES * piece_blocks, block_rows, piece_width), BF16),
+            pltpu.VMEM(w.shape, BF16),
             pltpu.VMEM((rows, 3 * lw), F32),
             pltpu.VMEM((rows, left.shape[1]), F32),
             pltpu.VMEM((rows, lw), F32),
@@ -259,7 +243,7 @@
         compiler_params=pltpu.CompilerParams(vmem_limit_bytes=VMEM_LIMIT),
         cost_estimate=COST,
         name="time_mix",
-    )(perm, length, x, first, gains, mixes, gating, left, right, bias, bonus, gscale, s0, exit_w, *pieces)
+    )(perm, length, x, first, gains, mixes, gating, left, right, bias, bonus, gscale, s0, exit_w, w)
 
 
 def channel_mix_kernel(
@@ -383,85 +367,269 @@
             copy.wait_send()
 
 
-def sum_terms(terms, acc, core_buf, pass_buf, near_buf, y_buf, copies, place):
+def sum_terms(terms, acc, core_buf, pass_a, near_a, y_a, pass_b, near_b, y_b, copies, place):
     y, z, c, zu, z2, zd, peers = place
-    half = terms.shape[3] // 2
-    from_core = [
-        copies.start(terms.at[1 - c, g], core_buf.at[g], peers["core"]) for g in (z2, zu, zd, z)
-    ]
-
-    def add_core(i, g):
+    quarter = terms.shape[3] // 4
+    a, a0, a1 = slice(0, 2 * quarter), slice(0, quarter), slice(quarter, 2 * quarter)
+    b, b0, b1 = (slice(p.start + 2 * quarter, p.stop + 2 * quarter) for p in (a, a0, a1))
+    groups = (z2, zu, zd, z)
+    from_core = [copies.start(terms.at[1 - c, g], core_buf.at[g], peers["core"]) for g in groups]
+
+    def add(index, values):
+        acc[index] = (acc[index].astype(F32) + values.astype(F32)).astype(BF16)
+
+    def add_core(i):
+        g = groups[i]
         from_core[i].wait_recv()
         acc[g] = (terms[c, g].astype(F32) + core_buf[g].astype(F32)).astype(BF16)
-
-    add_core(0, z2)
-    first_up = copies.start(acc.at[z2, :, 0:half], pass_buf.at[0], peers["up"])
-    first_down = copies.start(acc.at[z2, :, half : 2 * half], pass_buf.at[1], peers["down"])
-    add_core(1, zu)
-    add_core(2, zd)
-    first_up.wait_recv()
-    acc[zu, :, 0:half] = (acc[zu, :, 0:half].astype(F32) + pass_buf[0].astype(F32)).astype(BF16)
-    second_up = copies.start(acc.at[zu], near_buf.at[0], peers["up"])
-    first_down.wait_recv()
-    acc[zd, :, half : 2 * half] = (
-        acc[zd, :, half : 2 * half].astype(F32) + pass_buf[1].astype(F32)
-    ).astype(BF16)
-    second_down = copies.start(acc.at[zd], near_buf.at[1], peers["down"])
-    add_core(3, z)
-    second_up.wait_recv()
-    second_down.wait_recv()
-
-    def total_of(yy):
-        return acc[z, yy].astype(F32) + near_buf[0, yy].astype(F32) + near_buf[1, yy].astype(F32)
-
-    acc[z, 1 - y] = total_of(1 - y).astype(BF16)
-    across = copies.start(acc.at[z, 1 - y], y_buf, peers["y"])
-    own = total_of(y)
-    across.wait_recv()
-    return own + y_buf[...].astype(F32)
+        return copies.start(acc.at[g, 1 - y, b], y_b.at[g], peers["y"])
+
+    across_b = [add_core(0)]
+    pass_up = copies.start(acc.at[z2, :, a0], pass_a.at[0], peers["up"])
+    pass_down = copies.start(acc.at[z2, :, a1], pass_a.at[1], peers["down"])
+    across_b += [add_core(1), add_core(2)]
+    pass_up.wait_recv()
+    add((zu, slice(None), a0), pass_a[0])
+    near_up = copies.start(acc.at[zu, :, a], near_a.at[0], peers["up"])
+    pass_down.wait_recv()
+    add((zd, slice(None), a1), pass_a[1])
+    near_down = copies.start(acc.at[zd, :, a], near_a.at[1], peers["down"])
+    across_b.append(add_core(3))
+    across_b[0].wait_recv()
+    add((z2, y, b), y_b[z2])
+    pass_b_up = copies.start(acc.at[z2, y, b0], pass_b.at[0], peers["up"])
+    pass_b_down = copies.start(acc.at[z2, y, b1], pass_b.at[1], peers["down"])
+    across_b[1].wait_recv()
+    add((zu, y, b), y_b[zu])
+    across_b[2].wait_recv()
+    add((zd, y, b), y_b[zd])
+    near_up.wait_recv()
+    near_down.wait_recv()
+
+    def total_a(yy):
+        return acc[z, yy, a].astype(F32) + near_a[0, yy].astype(F32) + near_a[1, yy].astype(F32)
+
+    acc[z, 1 - y, a] = total_a(1 - y).astype(BF16)
+    across_a = copies.start(acc.at[z, 1 - y, a], y_a, peers["y"])
+    pass_b_up.wait_recv()
+    add((zu, y, b0), pass_b[0])
+    near_b_up = copies.start(acc.at[zu, y, b], near_b.at[0], peers["up"])
+    pass_b_down.wait_recv()
+    add((zd, y, b1), pass_b[1])
+    near_b_down = copies.start(acc.at[zd, y, b], near_b.at[1], peers["down"])
+    across_a.wait_recv()
+    upper = total_a(y) + y_a[...].astype(F32)
+    across_b[3].wait_recv()
+    lower = acc[z, y, b].astype(F32) + y_b[z].astype(F32)
+    near_b_up.wait_recv()
+    near_b_down.wait_recv()
+    lower = lower + near_b[0].astype(F32) + near_b[1].astype(F32)
+    return (a, upper), (b, lower)
+
+
+SUM_COPIES, COLLECT_COPIES = 17, 17
 
 
 def sum_scratch(shape, copies):
     nc, nz, ny, rows, lw = shape
+    half, quarter = rows // 2, rows // 4
     return [
         pltpu.VMEM((nz, ny, rows, lw), BF16),
         pltpu.VMEM((nz, ny, rows, lw), BF16),
-        pltpu.VMEM((2, ny, rows // 2, lw), BF16),
-        pltpu.VMEM((2, ny, rows, lw), BF16),
-        pltpu.VMEM((rows, lw), BF16),
+        pltpu.VMEM((2, ny, quarter, lw), BF16),
+        pltpu.VMEM((2, ny, half, lw), BF16),
+        pltpu.VMEM((half, lw), BF16),
+        pltpu.VMEM((2, quarter, lw), BF16),
+        pltpu.VMEM((2, half, lw), BF16),
+        pltpu.VMEM((nz, half, lw), BF16),
         pltpu.SemaphoreType.DMA((copies,)),
         pltpu.SemaphoreType.DMA((copies,)),
     ]
 
 
-def join_kernel(terms, x_ref, mid_ref, own_ref, acc, core_buf, pass_buf, near_buf, y_buf, send, recv):
+def spread_kernel(
+    owner_ref, flag_ref, rec_ref, key_ref, val_ref, kept_ref,
+    w_ref, s0_ref,
+    own, got, own_state, got_state, local_sem, sems, state_sems, send_w, recv_w,
+):
+    me, at = lax.axis_index("hid"), lax.axis_index("req")
+    x, w = at // NW, at % NW
+    hid, _, lw = own.shape
+    block_rows = rec_ref.shape[0]
+    heads = lw // HEAD
+    peers = {
+        "mate": {"req": x * NW + 1 - w},
+        "up": {"req": (x + 1) % NX * NW + w},
+        "down": {"req": (x + NX - 1) % NX * NW + w},
+    }
+    barrier = pltpu.get_barrier_semaphore()
+    for i in range(1, hid):
+        pl.semaphore_signal(
+            barrier, inc=1, device_id={"hid": (me + i) % hid}, device_id_type=MESH
+        )
+    for device in peers.values():
+        pl.semaphore_signal(barrier, inc=1, device_id=device, device_id_type=MESH)
+
+    def fill(h):
+        cols = pl.ds(pl.multiple_of(h * lw, lw), lw)
+        for m, ref in enumerate((rec_ref, key_ref, val_ref)):
+            own[h, m * block_rows : (m + 1) * block_rows, :] = ref[:, cols].astype(BF16)
+
+    def fill_state(h):
+        state = jnp.concatenate([kept_ref[h * heads + i] for i in range(heads)], axis=1)
+        own_state[h] = state.astype(BF16)
+
+    def swap(i, src, dst, sems):
+        to = (me + i) % hid
+        return pltpu.make_async_remote_copy(
+            src_ref=src.at[to], dst_ref=dst.at[me], send_sem=sems.at[0, i - 1],
+            recv_sem=sems.at[1, i - 1], device_id={"hid": to}, device_id_type=MESH,
+        )
+
+    def fill_and_send(i, carry):
+        fill((me + i) % hid)
+        swap(i, own, got, sems).start()
+        return carry
+
+    def fill_and_send_state(i, carry):
+        fill_state((me + i) % hid)
+        swap(i, own_state, got_state, state_sems).start()
+        return carry
+
+    def arrive(i, carry):
+        swap(i, own, got, sems).wait_recv()
+        return carry
+
+    def finish(i, carry):
+        swap(i, own, got, sems).wait_send()
+        swap(i, own_state, got_state, state_sems).wait()
+        return carry
+
+    pl.semaphore_wait(barrier, hid - 1 + len(peers))
+    lax.fori_loop(1, hid, fill_and_send, 0)
+    fill(me)
+    got[me] = own[me]
+    lax.fori_loop(1, hid, arrive, 0)
+    copies = Copies(send_w, recv_w)
+    mate = x * NW + 1 - w
+    before, after = (x + NX - 1) % NX * NW, (x + 1) % NX * NW
+    a, b = slice(0, SPLIT), slice(SPLIT, hid)
+    b0, b1 = slice(SPLIT, (SPLIT + hid) // 2), slice((SPLIT + hid) // 2, hid)
+    keep = pltpu.make_async_copy(got, w_ref.at[at], local_sem)
+
+    def pass_on(index, rows, device, first=False):
+        here = w_ref.at[index, rows]
+        return copies.start(got.at[rows] if first else here, here, peers[device])
+
+    a_up, a_down = pass_on(at, a, "up", True), pass_on(at, a, "down", True)
+    a_mate = pass_on(at, a, "mate", True)
+    b_up, b_down = pass_on(at, b, "up", True), pass_on(at, b, "down", True)
+    b_mates = [pass_on(at, b, "mate", True)]
+    keep.start()
+    fill_state(me)
+    got_state[me] = own_state[me]
+    lax.fori_loop(1, hid, fill_and_send_state, 0)
+    a_up.wait_recv()
+    far_up = pass_on(before + w, a, "up")
+    a_mate.wait_recv()
+    mate_up, mate_down = pass_on(mate, a, "up"), pass_on(mate, a, "down")
+    a_down.wait_recv()
+    b_up.wait_recv()
+    b_mates.append(pass_on(before + w, b, "mate"))
+    far_b_up = pass_on(before + w, b0, "up")
+    b_down.wait_recv()
+    far_b_down = pass_on(after + w, b1, "down")
+    b_mates.append(pass_on(after + w, b, "mate"))
+    mate_down.wait_recv()
+    far_down = pass_on(after + 1 - w, a, "down")
+    far_b_up.wait_recv()
+    far_b_down.wait_recv()
+    b_mates.append(pass_on((x + 2) % NX * NW + w, b, "mate"))
+    lax.fori_loop(1, hid, finish, 0)
+    s0_ref[...] = jnp.where(flag_ref[0] == 1, got_state[owner_ref[0]].astype(F32), 0.0)
+    for copy in [mate_up, far_up, far_down] + b_mates:
+        copy.wait_recv()
+    keep.wait()
+    copies.finish()
+
+
+def spread(owner, flag, rec, key, val, kept, hid):
+    block_rows, width = rec.shape
+    lw = width // hid
+    req = NX * NW
+    return pl.pallas_call(
+        spread_kernel,
+        out_shape=(
+            jax.ShapeDtypeStruct((req, hid, 3 * block_rows, lw), BF16),
+            jax.ShapeDtypeStruct((HEAD, lw), F32),
+        ),
+        in_specs=[SM, SM, VM, VM, VM, VM],
+        out_specs=(HB, VM),
+        scratch_shapes=[
+            pltpu.VMEM((hid, 3 * block_rows, lw), BF16),
+            pltpu.VMEM((hid, 3 * block_rows, lw), BF16),
+            pltpu.VMEM((hid, HEAD, lw), BF16),
+            pltpu.VMEM((hid, HEAD, lw), BF16),
+            pltpu.SemaphoreType.DMA,
+            pltpu.SemaphoreType.DMA((2, hid - 1)),
+            pltpu.SemaphoreType.DMA((2, hid - 1)),
+            pltpu.SemaphoreType.DMA((15,)),
+            pltpu.SemaphoreType.DMA((15,)),
+        ],
+        compiler_params=pltpu.CompilerParams(
+            collective_id=2, has_side_effects=True, vmem_limit_bytes=VMEM_LIMIT
+        ),
+        cost_estimate=COST,
+        name="spread",
+    )(owner, flag, rec, key, val, kept)
+
+
+def join_kernel(terms, x_ref, mid_ref, own_ref, *scratch):
     place = hid_place()
     y, z, c, zu, z2, zd, peers = place
     meet(peers)
-    copies = Copies(send, recv)
-    half = x_ref.shape[0] // 2
-    total = sum_terms(terms, acc, core_buf, pass_buf, near_buf, y_buf, copies, place)
-    own = (x_ref[...].astype(F32) + total).astype(BF16)
-    own_ref[...] = own
-    mid_ref[c, z, y] = own
-
-    def pass_on(index, device):
-        return copies.start(mid_ref.at[index], mid_ref.at[index], device)
-
-    pass_on((c, z, y), peers["y"]).wait_recv()
-    up = pass_on((c, z), peers["up"])
-    down = pass_on((c, z), peers["down"])
-    waits = [pass_on((c, z), peers["core"])]
-    up.wait_recv()
-    far = [pass_on((c, zd, slice(None), slice(0, half)), peers["up"])]
-    waits.append(pass_on((c, zd), peers["core"]))
-    down.wait_recv()
-    far.append(pass_on((c, zu, slice(None), slice(half, 2 * half)), peers["down"]))
-    waits.append(pass_on((c, zu), peers["core"]))
-    for copy in far:
-        copy.wait_recv()
-    waits.append(pass_on((c, z2), peers["core"]))
-    for copy in waits:
+    copies = Copies(*scratch[-2:])
+    quarter = x_ref.shape[0] // 4
+    every = slice(None)
+    a, a0, a1 = slice(0, 2 * quarter), slice(0, quarter), slice(quarter, 2 * quarter)
+    b, b0, b1 = (slice(p.start + 2 * quarter, p.stop + 2 * quarter) for p in (a, a0, a1))
+    for rows, total in sum_terms(terms, *scratch[:-2], copies, place):
+        own = (x_ref[rows].astype(F32) + total).astype(BF16)
+        own_ref[rows] = own
+        mid_ref[c, z, y, rows] = own
+
+    def pass_on(device, *index):
+        return copies.start(mid_ref.at[index], mid_ref.at[index], peers[device])
+
+    across_a = pass_on("y", c, z, y, a)
+    near_b_up = pass_on("up", c, z, y, b)
+    near_b_down = pass_on("down", c, z, y, b)
+    across_b = [pass_on("y", c, z, y, b)]
+    across_a.wait_recv()
+    near_a_up = pass_on("up", c, z, every, a)
+    near_a_down = pass_on("down", c, z, every, a)
+    near_b_up.wait_recv()
+    far_b_up = pass_on("up", c, zd, y, b0)
+    across_b.append(pass_on("y", c, zd, y, b))
+    near_b_down.wait_recv()
+    far_b_down = pass_on("down", c, zu, y, b1)
+    across_b.append(pass_on("y", c, zu, y, b))
+    near_a_up.wait_recv()
+    far_a_up = pass_on("up", c, zd, every, a0)
+    near_a_down.wait_recv()
+    far_a_down = pass_on("down", c, zu, every, a1)
+    far_b_up.wait_recv()
+    far_b_down.wait_recv()
+    across_b.append(pass_on("y", c, z2, y, b))
+    to_core = []
+    for i, g in enumerate((z, zd, zu)):
+        across_b[i].wait_recv()
+        to_core.append(pass_on("core", c, g))
+    far_a_up.wait_recv()
+    far_a_down.wait_recv()
+    across_b[3].wait_recv()
+    to_core.append(pass_on("core", c, z2))
+    for copy in to_core:
         copy.wait_recv()
     copies.finish()
 
@@ -474,7 +642,7 @@
         out_shape=(jax.ShapeDtypeStruct(shape, BF16), jax.ShapeDtypeStruct((rows, lw), BF16)),
         in_specs=[VM, VM],
         out_specs=(VM, VM),
-        scratch_shapes=sum_scratch(shape, 18),
+        scratch_shapes=sum_scratch(shape, SUM_COPIES + COLLECT_COPIES),
         compiler_params=pltpu.CompilerParams(
             collective_id=0, has_side_effects=True, vmem_limit_bytes=VMEM_LIMIT
         ),
@@ -483,16 +651,14 @@
     )(terms.reshape(shape), x_share)
 
 
-def close_kernel(
-    len_ref, terms, own_ref, gate_ref, out_ref, acc, core_buf, pass_buf, near_buf, y_buf, send, recv
-):
+def close_kernel(len_ref, terms, own_ref, gate_ref, out_ref, *scratch):
     place = hid_place()
     meet(place[-1])
-    copies = Copies(send, recv)
-    total = sum_terms(terms, acc, core_buf, pass_buf, near_buf, y_buf, copies, place)
-    combined = own_ref[...].astype(F32) + gate_ref[...] * total
-    row = lax.broadcasted_iota(jnp.int32, combined.shape, 0)
-    out_ref[...] = jnp.where(row < len_ref[0], combined, 0.0).astype(BF16)
+    copies = Copies(*scratch[-2:])
+    for rows, total in sum_terms(terms, *scratch[:-2], copies, place):
+        combined = own_ref[rows].astype(F32) + gate_ref[rows] * total
+        row = lax.broadcasted_iota(jnp.int32, combined.shape, 0) + rows.start
+        out_ref[rows] = jnp.where(row < len_ref[0], combined, 0.0).astype(BF16)
     copies.finish()
 
 
@@ -504,7 +670,7 @@
         out_shape=jax.ShapeDtypeStruct((rows, lw), BF16),
         in_specs=[SM, VM, VM, VM],
         out_specs=VM,
-        scratch_shapes=sum_scratch(shape, 9),
+        scratch_shapes=sum_scratch(shape, SUM_COPIES),
         compiler_params=pltpu.CompilerParams(
             collective_id=1, has_side_effects=True, vmem_limit_bytes=VMEM_LIMIT
         ),
@@ -545,30 +711,23 @@
     gains = normalizer_scales.astype(F32)
     carried = jnp.where(resuming == 1, previous_normed_entries[0].astype(F32), 0.0)
 
-    own = jnp.stack([training_accept_pieces, training_lookup_pieces, training_content_pieces])
-    own = own.astype(BF16).reshape(3, block_rows, hid, lw).transpose(2, 1, 0, 3)
-    own = own.reshape(hid, block_rows, 3 * lw)
-    swapped = lax.all_to_all(own, "hid", split_axis=0, concat_axis=0, tiled=True)
-    fetched = lax.all_to_all(
-        kept_summary_places[0, 0].astype(BF16).reshape(hid, -1, HEAD, HEAD),
-        "hid", split_axis=0, concat_axis=0, tiled=True,
+    both = jnp.concatenate([feedforward_entry_proj, feedforward_exit_proj])
+    both = [both, send(both, 0, 1), send(both, 1, 0), send(both, NX - 1, 0)]
+    w, s0 = spread(
+        owning_index, continuing_flags, training_accept_pieces, training_lookup_pieces,
+        training_content_pieces, kept_summary_places[0, 0], hid,
     )
-    chosen = lax.dynamic_index_in_dim(fetched, owning_index[0], 0, keepdims=False)
-    s0 = jnp.where(resuming == 1, chosen.astype(F32), 0.0)
-    both = first_hop(jnp.concatenate([feedforward_entry_proj, feedforward_exit_proj]))
-    pieces = third_hop(second_hop(first_hop(swapped)))
-    pieces, both = lax.optimization_barrier((pieces, both))
+    both, w = lax.optimization_barrier((both, w))
     both = second_hop(both)
-
-    terms, state, last_in = time_mix(
+    w = w.reshape(-1, 3 * block_rows, lw)
+    terms, state, last_in, x_share = time_mix(
         partition_arrangement, prompt_extents, x, carried[0:1], gains, prior_step_blends,
         gating_projection, forgetting_left_lowrank, forgetting_right_lowrank,
         forgetting_bias_vector[None], instant_emphasis[None], group_normalizer_scale[None],
-        s0, mixing_exit_projection, pieces,
+        s0, mixing_exit_projection, w,
     )
     terms, both = lax.optimization_barrier((terms, both))
     both = third_hop(both)
-    x_share = lax.dynamic_slice_in_dim(x, lax.axis_index("hid") * lw, lw, 1)
     middle, own_middle = join(terms, x_share)
     out_terms, gate_rows, last_chan = channel_mix(
         prompt_extents, middle.reshape(hid, rows, lw), carried[1:2], gains, prior_step_blends,

time: 313 us -> 268 us (0.86)
  waiting for transfers between devices: 95.1 us -> 6.62 us
  Pallas kernels: 163 us -> 240 us
  starting transfers between devices: 31.6 us -> 11.4 us
  local copies, waits for them, and re-layouts: 13.9 us -> 5.11 us
  other arithmetic: 5.18 us -> 1.31 us
    pallas_call x0 -> x1, Pallas kernels: none -> 100 us  [spread(): pl.pallas_call(spread_kernel, out_shape=(jax.ShapeDtypeStruct((req, hid,...]
    ppermute x14 -> x7, waiting for transfers between devices: 87.3 us -> 6.62 us  [send(): return lax.ppermute(value, 'req', pairs)]
    pallas_call x1, Pallas kernels: 65.6 us -> 50.2 us  [join(): pl.pallas_call(join_kernel, out_shape=(jax.ShapeDtypeStruct(shape, BF16),...]
    all_to_all x2 -> x0, starting transfers between devices: 10.3 us -> none  [the longest x1 6.69 us: local(): lax.all_to_all(own, 'hid', split_axis=0, concat_axis=0, tiled=True)]
    ppermute x14 -> x7, starting transfers between devices: 21.3 us -> 11.4 us  [send(): return lax.ppermute(value, 'req', pairs)]
    pallas_call x1, Pallas kernels: 33.8 us -> 25.8 us  [close(): pl.pallas_call(close_kernel, out_shape=jax.ShapeDtypeStruct((rows, lw), B...]
    all_to_all x2 -> x0, waiting for transfers between devices: 7.83 us -> none  [the longest x1 7.82 us: local(): lax.all_to_all(own, 'hid', split_axis=0, concat_axis=0, tiled=True)]
    unnamed x33 -> x22, local copies, waits for them, and re-layouts: 6.26 us -> 4.41 us
  transfers between devices with their start and end apart: 16 -> 7, of which waited for: 6 -> 2; matrix products, arithmetic and copies ran while one was open for 3% -> 0% of each run, Pallas kernels for 32% -> 69%
where the time goes in v4:
time: 268 us; the launch traced here: 267 us
  Pallas kernels  240 us (90%)
  starting transfers between devices  11.4 us (4%)
  waiting for transfers between devices  6.62 us (2%)
  local copies, waits for them, and re-layouts  5.11 us (2%)
  between operations  2.8 us (1%)
    pallas_call x1, Pallas kernels, spread(): pl.pallas_call(spread_kernel, out_shape=(jax.ShapeDtypeStruct((req, hid,...  100 us
    pallas_call x1, Pallas kernels, join(): pl.pallas_call(join_kernel, out_shape=(jax.ShapeDtypeStruct(shape, BF16),...  50.2 us
    pallas_call x1, Pallas kernels, time_mix(): pl.pallas_call(time_mix_kernel, out_shape=(jax.ShapeDtypeStruct((width //...  34.5 us
    pallas_call x1, Pallas kernels, channel_mix(): pl.pallas_call(channel_mix_kernel, out_shape=(jax.ShapeDtypeStruct((group...  29.1 us
    pallas_call x1, Pallas kernels, close(): pl.pallas_call(close_kernel, out_shape=jax.ShapeDtypeStruct((rows, lw), B...  25.8 us
    ppermute x7, starting transfers between devices, send(): return lax.ppermute(value, 'req', pairs)  11.4 us
    ppermute x7, waiting for transfers between devices, send(): return lax.ppermute(value, 'req', pairs)  6.62 us
  transfers between devices with their start and end apart: 7, of which 2 were waited for; matrix products, arithmetic and copies ran while one was open for 0% of the time, Pallas kernels for 69%

profile of v4, /device:TPU:0, one launch (start us, length us, event | category | flops | bytes accessed | tf_op | source)
XLA Modules:
  0.0 267.4 jit_solution(519359811788765977)
XLA Ops:
  0.6 0.0 copy-start
  0.6 1.3 constant_dynamic-update-slice_fusion.1
  2.0 0.1 copy-done
  2.1 0.1 constant_dynamic-update-slice_fusion.refs_0_
  2.2 0.0 copy-start.1
  2.2 2.9 %collective-permute-start.2 = (bf16[224,4096]{1,0:T(8,128)(2,1)S(1)}, bf16[224,4096]{1,0:T(8,128)(2,1)S(1)}, u32[]{:S(2)}, u32[]{:S(2)}) collective-permute-start(bf16[224,4096]{1,0:T(8,128)(2,1)S(1)} %constant_dynamic-update-slice_fusion.refs_0_), channel_id=1, source_target_pairs={{0,96},{16,112},{32,0},{48,16},{64,32},{80,48},{96,64},{112,80},{1... | collective-permute-start | bytes 5505032 | tf_op jit(solution)/shard_map/ppermute | solution.py:43
  5.1 0.0 collective-permute-start.1
  5.1 3.2 %collective-permute-start = (bf16[224,4096]{1,0:T(8,128)(2,1)S(1)}, bf16[224,4096]{1,0:T(8,128)(2,1)}, u32[]{:S(2)}, u32[]{:S(2)}) collective-permute-start(bf16[224,4096]{1,0:T(8,128)(2,1)S(1)} %constant_dynamic-update-slice_fusion.refs_0_), channel_id=1, source_target_pairs={{0,16},{16,0},{32,48},{48,32},{64,80},{80,64},{96,112},{112,96},{1... | collective-permute-start | bytes 5505032 | tf_op jit(solution)/shard_map/ppermute | solution.py:43
  9.6 0.0 copy-start.2
  9.6 0.0 copy-start.3
  9.6 100.5 %spread.1 = (bf16[8,16,96,256]{3,2,1,0:T(8,128)(2,1)}, f32[64,256]{1,0:T(8,128)}) custom-call(s32[1]{0:T(128)S(6)} %copy.29.owner_ref, s32[1]{0:T(128)S(6)} %copy.28.flag_ref, f32[32,4096]{1,0:T(8,128)} %rec_ref.1, f32[32,4096]{1,0:T(8,128)} %key_ref.1, f32[32,4096]{1,0:T(8,128)} %val_ref.1, f32[64,64,64]{2,1,0:T(8,128)} %bitcast.23), custom_call_target="tpu_custom_call" | custom-call | flops 40000000000 | bytes 40000000 | tf_op jit(solution)/shard_map/spread/pallas_call | solution.py:560
  110.1 0.0 copy-done.1
  110.7 0.0 copy-done.2
  110.7 0.6 convert_element_type.16.gain_ref
  111.4 0.0 copy-done.3
  111.4 0.6 slice_bitcast_fusion
  112.0 0.0 collective-permute-done.2.refs_3_
  112.0 0.0 copy-start.6
  112.0 0.0 collective-permute-done.1.refs_2_
  112.0 0.0 copy-start.7
  112.1 0.0 collective-permute-done.refs_1_
  112.1 0.1 collective-permute-start.4
  112.1 2.0 collective-permute-start.3
  114.2 34.5 %time_mix.1 = (bf16[16,512,256]{2,1,0:T(8,128)(2,1)}, f32[4,64,64]{2,1,0:T(8,128)}, f32[1,4096]{1,0:T(1,128)}, bf16[512,256]{1,0:T(8,128)(2,1)}) custom-call(s32[128]{0:T(128)} %perm_ref.1, s32[1]{0:T(128)S(6)} %copy.27.len_ref, bf16[512,4096]{1,0:T(8,128)(2,1)} %bitcast.22, f32[1,4096]{1,0:T(1,128)} %get-tuple-element.50.first_ref, ...), custom_call_target="tpu_custom_call" | custom-call | flops 40000000000 | bytes 40000000 | tf_op jit(solution)/shard_map/time_mix/pallas_call | solution.py:222
  148.6 0.0 copy-done.6
  148.6 5.2 %collective-permute-done.4.refs_5_ = bf16[224,4096]{1,0:T(8,128)(2,1)S(1)} collective-permute-done((bf16[224,4096]{1,0:T(8,128)(2,1)}, bf16[224,4096]{1,0:T(8,128)(2,1)S(1)}, u32[]{:S(2)}, u32[]{:S(2)}) %collective-permute-start.4) | collective-permute-done | bytes 1835040 | tf_op jit(solution)/shard_map/ppermute | solution.py:43
  153.9 0.0 copy-start.8
  153.9 1.4 collective-permute-done.3.refs_4_
  155.3 0.0 copy-done.7
  155.3 0.5 collective-permute-start.5
  155.7 2.8 %collective-permute-start.6 = (bf16[224,4096]{1,0:T(8,128)(2,1)S(1)}, bf16[224,4096]{1,0:T(8,128)(2,1)}, u32[]{:S(2)}, u32[]{:S(2)}) collective-permute-start(bf16[224,4096]{1,0:T(8,128)(2,1)S(1)} %collective-permute-done.4.refs_5_), channel_id=1, source_target_pairs={{0,96},{16,112},{32,0},{48,16},{64,32},{80,48},{96,64},{112,80},{1... | collective-permute-start | bytes 5505032 | tf_op jit(solution)/shard_map/ppermute | solution.py:43
  158.5 50.2 %join.1 = (bf16[2,4,2,512,256]{4,3,2,1,0:T(8,128)(2,1)}, bf16[512,256]{1,0:T(8,128)(2,1)}) custom-call(bf16[2,4,2,512,256]{4,3,2,1,0:T(8,128)(2,1)} %bitcast.29, bf16[512,256]{1,0:T(8,128)(2,1)} %get-tuple-element.35.x_ref), custom_call_target="tpu_custom_call" | custom-call | flops 40000000000 | bytes 40000000 | tf_op jit(solution)/shard_map/join/pallas_call | solution.py:640
  208.7 0.0 copy-done.8
  208.8 0.0 collective-permute-done.5.refs_6_
  208.8 0.0 copy-start.9
  208.8 0.0 collective-permute-done.6.refs_7_
  208.8 1.3 copy-done.9
  210.1 29.1 %channel_mix.1 = (bf16[16,512,256]{2,1,0:T(8,128)(2,1)}, f32[512,256]{1,0:T(8,128)}, f32[1,4096]{1,0:T(1,128)}) custom-call(s32[1]{0:T(128)S(6)} %copy.27.len_ref, bf16[16,512,256]{2,1,0:T(8,128)(2,1)} %bitcast.28, f32[1,4096]{1,0:T(1,128)} %get-tuple-element.49.first_ref, f32[2,4096]{1,0:T(2,128)} %convert_element_type.16.gain_ref, ...), custom_call_target="tpu_custom_call" | custom-call | flops 40000000000 | bytes 40000000 | tf_op jit(solution)/shard_map/channel_mix/pallas_call | solution.py:308
  239.2 0.0 copy-start.4
  239.2 0.0 copy-start.5
  239.2 25.8 %close.1 = bf16[512,256]{1,0:T(8,128)(2,1)} custom-call(s32[1]{0:T(128)S(6)} %copy.27.len_ref, bf16[2,4,2,512,256]{4,3,2,1,0:T(8,128)(2,1)} %bitcast.20, bf16[512,256]{1,0:T(8,128)(2,1)} %get-tuple-element.44.own_ref, f32[512,256]{1,0:T(8,128)} %get-tuple-element.45.gate_ref), custom_call_target="tpu_custom_call" | custom-call | tf_op jit(solution)/shard_map/close/pallas_call | solution.py:668
  265.0 0.0 copy-done.4
  265.0 0.0 copy-done.5
  265.1 0.6 pad_maximum_fusion
  265.7 1.7 copy.30
  (2 shorter events, 0.0 us)
Async XLA Ops:
  0.6 1.5 copy-start
  2.2 107.9 %copy-start.1 = (bf16[224,4096]{1,0:T(8,128)(2,1)}, bf16[224,4096]{1,0:T(8,128)(2,1)S(1)}, u32[]{:S(2)}) copy-start(bf16[224,4096]{1,0:T(8,128)(2,1)S(1)} %constant_dynamic-update-slice_fusion.refs_0_) | copy-start | bytes 5505028
  2.2 109.9 %collective-permute-start.2 = (bf16[224,4096]{1,0:T(8,128)(2,1)S(1)}, bf16[224,4096]{1,0:T(8,128)(2,1)S(1)}, u32[]{:S(2)}, u32[]{:S(2)}) collective-permute-start(bf16[224,4096]{1,0:T(8,128)(2,1)S(1)} %constant_dynamic-update-slice_fusion.refs_0_), channel_id=1, source_target_pairs={{0,96},{16,112},{32,0},{48,16},{64,32},{80,48},{96,64},{112,80},{1... | collective-permute-start | bytes 5505032 | tf_op jit(solution)/shard_map/ppermute | solution.py:43
  5.1 107.0 %collective-permute-start.1 = (bf16[224,4096]{1,0:T(8,128)(2,1)S(1)}, bf16[224,4096]{1,0:T(8,128)(2,1)S(1)}, u32[]{:S(2)}, u32[]{:S(2)}) collective-permute-start(bf16[224,4096]{1,0:T(8,128)(2,1)S(1)} %constant_dynamic-update-slice_fusion.refs_0_), channel_id=1, source_target_pairs={{0,32},{16,48},{32,64},{48,80},{64,96},{80,112},{96,0},{112,16},{1... | collective-permute-start | bytes 5505032 | tf_op jit(solution)/shard_map/ppermute | solution.py:43
  5.1 107.0 %collective-permute-start = (bf16[224,4096]{1,0:T(8,128)(2,1)S(1)}, bf16[224,4096]{1,0:T(8,128)(2,1)}, u32[]{:S(2)}, u32[]{:S(2)}) collective-permute-start(bf16[224,4096]{1,0:T(8,128)(2,1)S(1)} %constant_dynamic-update-slice_fusion.refs_0_), channel_id=1, source_target_pairs={{0,16},{16,0},{32,48},{48,32},{64,80},{80,64},{96,112},{112,96},{1... | collective-permute-start | bytes 5505032 | tf_op jit(solution)/shard_map/ppermute | solution.py:43
  9.6 101.2 %copy-start.2 = (bf16[2,4096]{1,0:T(2,128)(2,1)S(1)}, bf16[2,4096]{1,0:T(2,128)(2,1)}, u32[]{:S(2)}) copy-start(bf16[2,4096]{1,0:T(2,128)(2,1)} %param.30) | copy-start | bytes 49156
  9.6 101.8 %copy-start.3 = (bf16[1,2,4096]{2,1,0:T(2,128)(2,1)S(1)}, bf16[1,2,4096]{2,1,0:T(2,128)(2,1)}, u32[]{:S(2)}) copy-start(bf16[1,2,4096]{2,1,0:T(2,128)(2,1)} %param.40) | copy-start | bytes 49156
  112.0 36.6 %copy-start.6 = (bf16[224,4096]{1,0:T(8,128)(2,1)}, bf16[224,4096]{1,0:T(8,128)(2,1)S(1)}, u32[]{:S(2)}) copy-start(bf16[224,4096]{1,0:T(8,128)(2,1)S(1)} %collective-permute-done.2.refs_3_) | copy-start | bytes 5505028
  112.0 43.2 %copy-start.7 = (bf16[224,4096]{1,0:T(8,128)(2,1)}, bf16[224,4096]{1,0:T(8,128)(2,1)S(1)}, u32[]{:S(2)}) copy-start(bf16[224,4096]{1,0:T(8,128)(2,1)S(1)} %collective-permute-done.1.refs_2_) | copy-start | bytes 5505028
  112.1 41.8 %collective-permute-start.4 = (bf16[224,4096]{1,0:T(8,128)(2,1)}, bf16[224,4096]{1,0:T(8,128)(2,1)S(1)}, u32[]{:S(2)}, u32[]{:S(2)}) collective-permute-start(bf16[224,4096]{1,0:T(8,128)(2,1)} %collective-permute-done.refs_1_), channel_id=1, source_target_pairs={{0,96},{16,112},{32,0},{48,16},{64,32},{80,48},{96,64},{112,80},{1... | collective-permute-start | bytes 5505032 | tf_op jit(solution)/shard_map/ppermute | solution.py:43
  112.1 43.1 %collective-permute-start.3 = (bf16[224,4096]{1,0:T(8,128)(2,1)}, bf16[224,4096]{1,0:T(8,128)(2,1)}, u32[]{:S(2)}, u32[]{:S(2)}) collective-permute-start(bf16[224,4096]{1,0:T(8,128)(2,1)} %collective-permute-done.refs_1_), channel_id=1, source_target_pairs={{0,32},{16,48},{32,64},{48,80},{64,96},{80,112},{96,0},{112,16},{1... | collective-permute-start | bytes 5505032 | tf_op jit(solution)/shard_map/ppermute | solution.py:43
  153.9 54.9 %copy-start.8 = (bf16[224,4096]{1,0:T(8,128)(2,1)}, bf16[224,4096]{1,0:T(8,128)(2,1)S(1)}, u32[]{:S(2)}) copy-start(bf16[224,4096]{1,0:T(8,128)(2,1)S(1)} %collective-permute-done.4.refs_5_) | copy-start | bytes 5505028
  155.3 53.5 %collective-permute-start.5 = (bf16[224,4096]{1,0:T(8,128)(2,1)S(1)}, bf16[224,4096]{1,0:T(8,128)(2,1)S(1)}, u32[]{:S(2)}, u32[]{:S(2)}) collective-permute-start(bf16[224,4096]{1,0:T(8,128)(2,1)S(1)} %collective-permute-done.1.refs_2_), channel_id=1, source_target_pairs={{0,32},{16,48},{32,64},{48,80},{64,96},{80,112},{96,0},{112,16},{1... | collective-permute-start | bytes 5505032 | tf_op jit(solution)/shard_map/ppermute | solution.py:43
  155.7 53.1 %collective-permute-start.6 = (bf16[224,4096]{1,0:T(8,128)(2,1)S(1)}, bf16[224,4096]{1,0:T(8,128)(2,1)}, u32[]{:S(2)}, u32[]{:S(2)}) collective-permute-start(bf16[224,4096]{1,0:T(8,128)(2,1)S(1)} %collective-permute-done.4.refs_5_), channel_id=1, source_target_pairs={{0,96},{16,112},{32,0},{48,16},{64,32},{80,48},{96,64},{112,80},{1... | collective-permute-start | bytes 5505032 | tf_op jit(solution)/shard_map/ppermute | solution.py:43
  208.8 1.3 copy-start.9
  239.2 25.8 %copy-start.4 = (f32[1,4096]{1,0:T(1,128)S(1)}, f32[1,4096]{1,0:T(1,128)}, u32[]{:S(2)}) copy-start(f32[1,4096]{1,0:T(1,128)} %get-tuple-element.47) | copy-start | bytes 49156
  239.2 25.8 %copy-start.5 = (f32[1,4096]{1,0:T(1,128)S(1)}, f32[1,4096]{1,0:T(1,128)}, u32[]{:S(2)}) copy-start(f32[1,4096]{1,0:T(1,128)} %get-tuple-element.48) | copy-start | bytes 49156

commit v5 on v4

--- a/solution.py
+++ b/solution.py
@@ -12,6 +12,7 @@
 TILE = 64
 PAIR = 128
 KC = 512
+GROUPS_IN, GROUPS_OUT = 4, 4
 VMEM_LIMIT = 58 * 1024 * 1024
 F32 = jnp.float32
 BF16 = jnp.bfloat16
@@ -43,15 +44,6 @@
     return lax.ppermute(value, "req", pairs)
 
 
-def second_hop(have):
-    other = have[1]
-    return have + [send(other, 1, 0), send(other, NX - 1, 0)]
-
-
-def third_hop(have):
-    return have + [send(have[2], 1, 0), send(have[5], NX - 1, 0)]
-
-
 def group_columns(g, lw):
     block = (g % NY) * (NZ * NC) + (g // NY % NZ) * NC + g // (NY * NZ)
     return pl.ds(pl.multiple_of(block * lw, lw), lw)
@@ -71,11 +63,12 @@
     return mean, 1.0 / jnp.sqrt(var + eps)
 
 
-def normed_and_delta(part, first_ref, gain_ref, which, cols, mean, inv):
+def normed_and_delta(part, flag_ref, first_ref, gain_ref, which, cols, mean, inv):
     normed = (part - mean) * inv * gain_ref[:, cols].astype(F32)[which : which + 1]
     before = pltpu.roll(normed, 1, 0)
     row = lax.broadcasted_iota(jnp.int32, normed.shape, 0)
-    before = jnp.where(row == 0, first_ref[:, cols], before)
+    saved = first_ref[:, cols].astype(F32)[which : which + 1]
+    before = jnp.where(row == 0, jnp.where(flag_ref[0] == 1, saved, 0.0), before)
     return normed, before - normed
 
 
@@ -85,7 +78,7 @@
 
 
 def time_mix_kernel(
-    perm_ref, len_ref, x_ref, first_ref, gain_ref, mix_ref, gating_ref, left_ref,
+    perm_ref, len_ref, flag_ref, x_ref, first_ref, gain_ref, mix_ref, gating_ref, left_ref,
     right_ref, bias_ref, bonus_ref, gscale_ref, s0_ref, exit_ref, w_ref,
     terms_ref, state_ref, last_ref, share_ref,
     w_scr, acc, acc_low, acc_gate, logw_scr, prod_scr, gated_scr, st_scr, sem,
@@ -114,7 +107,7 @@
 
     def project(c, carry):
         cols = pl.ds(pl.multiple_of(c * KC, KC), KC)
-        normed, delta = normed_and_delta(part(c), first_ref, gain_ref, 0, cols, mean, inv)
+        normed, delta = normed_and_delta(part(c), flag_ref, first_ref, gain_ref, 0, cols, mean, inv)
         last_ref[:, cols] = pick_row(normed, len_ref[0] - 1)
         mix = mix_ref[:, cols].astype(F32)
 
@@ -216,7 +209,7 @@
     lax.fori_loop(0, width // lw, leave, 0)
 
 
-def time_mix(perm, length, x, first, gains, mixes, gating, left, right, bias, bonus, gscale, s0, exit_w, w):
+def time_mix(perm, length, flag, x, first, gains, mixes, gating, left, right, bias, bonus, gscale, s0, exit_w, w):
     rows, width = x.shape
     lw = gating.shape[1]
     return pl.pallas_call(
@@ -227,7 +220,7 @@
             jax.ShapeDtypeStruct((1, width), F32),
             jax.ShapeDtypeStruct((rows, lw), BF16),
         ),
-        in_specs=[SM, SM] + [VM] * 12 + [HB],
+        in_specs=[SM, SM, SM] + [VM] * 12 + [HB],
         out_specs=(VM, VM, VM, VM),
         scratch_shapes=[
             pltpu.VMEM(w.shape, BF16),
@@ -243,31 +236,30 @@
         compiler_params=pltpu.CompilerParams(vmem_limit_bytes=VMEM_LIMIT),
         cost_estimate=COST,
         name="time_mix",
-    )(perm, length, x, first, gains, mixes, gating, left, right, bias, bonus, gscale, s0, exit_w, w)
+    )(perm, length, flag, x, first, gains, mixes, gating, left, right, bias, bonus, gscale, s0, exit_w, w)
 
 
 def channel_mix_kernel(
-    len_ref, x_ref, first_ref, gain_ref, mix_ref, accept_ref, *refs,
+    len_ref, flag_ref, last_in_ref, x_ref, first_ref, gain_ref, mix_ref, accept_ref, *refs,
 ):
-    pieces = refs[:PIECES]
-    terms_ref, gate_ref, last_ref = refs[PIECES : PIECES + 3]
-    key_scr, value_scr, inner, acc_gate, hidden, key_sems, value_sems = refs[PIECES + 3 :]
+    entry_ref, exit_ref, *pairs = refs[: PIECES + 1]
+    terms_ref, gate_ref, shift_ref = refs[PIECES + 1 : PIECES + 4]
+    key_scr, value_scr, inner, acc_gate, hidden, key_sems, value_sems = refs[PIECES + 4 :]
     groups, rows, lw = x_ref.shape
-    units = pieces[0].shape[0] // 2
-
-    def fetch(begin, scr, sems):
+    units = entry_ref.shape[0]
+
+    def fetch(own, begin, scr, sems):
+        pieces = [own] + [piece.at[pl.ds(begin, units)] for piece in pairs]
         copies = [
-            pltpu.make_async_copy(
-                piece.at[pl.ds(begin, units)], scr.at[pl.ds(i * units, units)], sems.at[i]
-            )
+            pltpu.make_async_copy(piece, scr.at[pl.ds(i * units, units)], sems.at[i])
             for i, piece in enumerate(pieces)
         ]
         for copy in copies:
             copy.start()
         return copies
 
-    key_copies = fetch(0, key_scr, key_sems)
-    value_copies = fetch(units, value_scr, value_sems)
+    key_copies = fetch(entry_ref, 0, key_scr, key_sems)
+    value_copies = fetch(exit_ref, units, value_scr, value_sems)
 
     def part(g):
         return x_ref[g].astype(F32)
@@ -278,41 +270,53 @@
     for copy in key_copies:
         copy.wait()
 
-    def project(g, carry):
-        cols = group_columns(g, lw)
-        normed, delta = normed_and_delta(part(g), first_ref, gain_ref, 1, cols, mean, inv)
-        last_ref[:, cols] = pick_row(normed, len_ref[0] - 1)
-        mix = mix_ref[:, cols].astype(F32)
-        inner[...] += nt_dot((normed + delta * mix[5:6]).astype(BF16), key_scr[:, cols])
-        acc_gate[...] += nn_dot((normed + delta * mix[6:7]).astype(BF16), accept_ref[cols, :])
-        return carry
-
-    lax.fori_loop(0, groups, project, 0)
+    def project(step, carry):
+        blends, opens, keys, accepts = [], [], [], []
+        for i in range(GROUPS_IN):
+            g = step * GROUPS_IN + i
+            cols = group_columns(g, lw)
+            normed, delta = normed_and_delta(part(g), flag_ref, first_ref, gain_ref, 1, cols, mean, inv)
+            last = pick_row(normed, len_ref[0] - 1)
+            shift_ref[:, cols] = jnp.concatenate([last_in_ref[:, cols], last], axis=0).astype(BF16)
+            mix = mix_ref[:, cols].astype(F32)
+            blends.append((normed + delta * mix[5:6]).astype(BF16))
+            opens.append((normed + delta * mix[6:7]).astype(BF16))
+            keys.append(key_scr[:, cols])
+            accepts.append(accept_ref[cols, :])
+        inner[...] += nt_dot(jnp.concatenate(blends, axis=1), jnp.concatenate(keys, axis=1))
+        acc_gate[...] += nn_dot(jnp.concatenate(opens, axis=1), jnp.concatenate(accepts, axis=0))
+        return carry
+
+    lax.fori_loop(0, groups // GROUPS_IN, project, 0)
     positive = jnp.maximum(inner[...], 0.0)
     hidden[...] = (positive * positive).astype(BF16)
     gate_ref[...] = jax.nn.sigmoid(acc_gate[...])
     for copy in value_copies:
         copy.wait()
 
-    def leave(g, carry):
-        terms_ref[g] = nn_dot(hidden[...], value_scr[:, group_columns(g, lw)]).astype(BF16)
-        return carry
-
-    lax.fori_loop(0, groups, leave, 0)
-
-
-def channel_mix(length, x, first, gains, mixes, accept, pieces):
+    def leave(step, carry):
+        block = [step * GROUPS_OUT + i for i in range(GROUPS_OUT)]
+        values = jnp.concatenate([value_scr[:, group_columns(g, lw)] for g in block], axis=1)
+        out = nn_dot(hidden[...], values).astype(BF16)
+        for i, g in enumerate(block):
+            terms_ref[g] = out[:, i * lw : (i + 1) * lw]
+        return carry
+
+    lax.fori_loop(0, groups // GROUPS_OUT, leave, 0)
+
+
+def channel_mix(length, flag, last_in, x, first, gains, mixes, accept, pieces):
     groups, rows, lw = x.shape
-    units = PIECES * pieces[0].shape[0] // 2
+    units = PIECES * pieces[0].shape[0]
     width = groups * lw
     return pl.pallas_call(
         channel_mix_kernel,
         out_shape=(
             jax.ShapeDtypeStruct((groups, rows, lw), BF16),
             jax.ShapeDtypeStruct((rows, lw), F32),
-            jax.ShapeDtypeStruct((1, groups * lw), F32),
+            jax.ShapeDtypeStruct((2, width), BF16),
         ),
-        in_specs=[SM] + [VM] * 5 + [HB] * PIECES,
+        in_specs=[SM, SM] + [VM] * 6 + [HB] * (PIECES + 1),
         out_specs=(VM, VM, VM),
         scratch_shapes=[
             pltpu.VMEM((units, width), BF16),
@@ -326,7 +330,7 @@
         compiler_params=pltpu.CompilerParams(vmem_limit_bytes=VMEM_LIMIT),
         cost_estimate=COST,
         name="channel_mix",
-    )(length, x, first, gains, mixes, accept, *pieces)
+    )(length, flag, last_in, x, first, gains, mixes, accept, *pieces)
 
 
 def hid_place():
@@ -427,7 +431,7 @@
     return (a, upper), (b, lower)
 
 
-SUM_COPIES, COLLECT_COPIES = 17, 17
+SUM_COPIES, COLLECT_COPIES = 17, 19
 
 
 def sum_scratch(shape, copies):
@@ -448,8 +452,8 @@
 
 
 def spread_kernel(
-    owner_ref, flag_ref, rec_ref, key_ref, val_ref, kept_ref,
-    w_ref, s0_ref,
+    owner_ref, flag_ref, rec_ref, key_ref, val_ref, kept_ref, entry_ref, exit_ref,
+    w_ref, s0_ref, mate_ff, before_ff, after_ff,
     own, got, own_state, got_state, local_sem, sems, state_sems, send_w, recv_w,
 ):
     me, at = lax.axis_index("hid"), lax.axis_index("req")
@@ -506,11 +510,16 @@
         return carry
 
     pl.semaphore_wait(barrier, hid - 1 + len(peers))
+    copies = Copies(send_w, recv_w)
+    units = entry_ref.shape[0]
+    halves = [(src, pl.ds(i * units, units)) for i, src in enumerate((entry_ref, exit_ref))]
+    first_hops = [copies.start(src, before_ff.at[half], peers["up"]) for src, half in halves]
+    first_hops += [copies.start(src, after_ff.at[half], peers["down"]) for src, half in halves]
     lax.fori_loop(1, hid, fill_and_send, 0)
+    first_hops += [copies.start(src, mate_ff.at[half], peers["mate"]) for src, half in halves]
     fill(me)
     got[me] = own[me]
     lax.fori_loop(1, hid, arrive, 0)
-    copies = Copies(send_w, recv_w)
     mate = x * NW + 1 - w
     before, after = (x + NX - 1) % NX * NW, (x + 1) % NX * NW
     a, b = slice(0, SPLIT), slice(SPLIT, hid)
@@ -547,13 +556,15 @@
     b_mates.append(pass_on((x + 2) % NX * NW + w, b, "mate"))
     lax.fori_loop(1, hid, finish, 0)
     s0_ref[...] = jnp.where(flag_ref[0] == 1, got_state[owner_ref[0]].astype(F32), 0.0)
-    for copy in [mate_up, far_up, far_down] + b_mates:
+    for copy in [mate_up, far_up, far_down] + b_mates + first_hops:
         copy.wait_recv()
     keep.wait()
     copies.finish()
 
 
-def spread(owner, flag, rec, key, val, kept, hid):
+def spread(owner, flag, rec, key, val, kept, entry, exit_rows, hid):
+    units = entry.shape[0]
+    pair = jax.ShapeDtypeStruct((2 * units, entry.shape[1]), BF16)
     block_rows, width = rec.shape
     lw = width // hid
     req = NX * NW
@@ -562,9 +573,12 @@
         out_shape=(
             jax.ShapeDtypeStruct((req, hid, 3 * block_rows, lw), BF16),
             jax.ShapeDtypeStruct((HEAD, lw), F32),
+            pair,
+            pair,
+            pair,
         ),
-        in_specs=[SM, SM, VM, VM, VM, VM],
-        out_specs=(HB, VM),
+        in_specs=[SM, SM, VM, VM, VM, VM, HB, HB],
+        out_specs=(HB, VM, HB, HB, HB),
         scratch_shapes=[
             pltpu.VMEM((hid, 3 * block_rows, lw), BF16),
             pltpu.VMEM((hid, 3 * block_rows, lw), BF16),
@@ -573,22 +587,33 @@
             pltpu.SemaphoreType.DMA,
             pltpu.SemaphoreType.DMA((2, hid - 1)),
             pltpu.SemaphoreType.DMA((2, hid - 1)),
-            pltpu.SemaphoreType.DMA((15,)),
-            pltpu.SemaphoreType.DMA((15,)),
+            pltpu.SemaphoreType.DMA((21,)),
+            pltpu.SemaphoreType.DMA((21,)),
         ],
         compiler_params=pltpu.CompilerParams(
             collective_id=2, has_side_effects=True, vmem_limit_bytes=VMEM_LIMIT
         ),
         cost_estimate=COST,
         name="spread",
-    )(owner, flag, rec, key, val, kept)
-
-
-def join_kernel(terms, x_ref, mid_ref, own_ref, *scratch):
+    )(owner, flag, rec, key, val, kept, entry, exit_rows)
+
+
+def join_kernel(
+    terms, x_ref, before_ff, after_mate_ff, mid_ref, own_ref, far_ff, far_mate_ff, *scratch
+):
     place = hid_place()
     y, z, c, zu, z2, zd, peers = place
-    meet(peers)
+    x, w = lax.axis_index("req") // NW, lax.axis_index("req") % NW
+    along_x = {
+        "x up": {"req": (x + 1) % NX * NW + w},
+        "x down": {"req": (x + NX - 1) % NX * NW + w},
+    }
+    meet({**peers, **along_x})
     copies = Copies(*scratch[-2:])
+    last_hops = [
+        copies.start(before_ff, far_ff, along_x["x up"]),
+        copies.start(after_mate_ff, far_mate_ff, along_x["x down"]),
+    ]
     quarter = x_ref.shape[0] // 4
     every = slice(None)
     a, a0, a1 = slice(0, 2 * quarter), slice(0, quarter), slice(quarter, 2 * quarter)
@@ -629,26 +654,31 @@
     far_a_down.wait_recv()
     across_b[3].wait_recv()
     to_core.append(pass_on("core", c, z2))
-    for copy in to_core:
+    for copy in to_core + last_hops:
         copy.wait_recv()
     copies.finish()
 
 
-def join(terms, x_share):
+def join(terms, x_share, before, after_mate):
     rows, lw = x_share.shape
     shape = (NC, NZ, NY, rows, lw)
     return pl.pallas_call(
         join_kernel,
-        out_shape=(jax.ShapeDtypeStruct(shape, BF16), jax.ShapeDtypeStruct((rows, lw), BF16)),
-        in_specs=[VM, VM],
-        out_specs=(VM, VM),
+        out_shape=(
+            jax.ShapeDtypeStruct(shape, BF16),
+            jax.ShapeDtypeStruct((rows, lw), BF16),
+            jax.ShapeDtypeStruct(before.shape, BF16),
+            jax.ShapeDtypeStruct(before.shape, BF16),
+        ),
+        in_specs=[VM, VM, HB, HB],
+        out_specs=(VM, VM, HB, HB),
         scratch_shapes=sum_scratch(shape, SUM_COPIES + COLLECT_COPIES),
         compiler_params=pltpu.CompilerParams(
             collective_id=0, has_side_effects=True, vmem_limit_bytes=VMEM_LIMIT
         ),
         cost_estimate=COST,
         name="join",
-    )(terms.reshape(shape), x_share)
+    )(terms.reshape(shape), x_share, before, after_mate)
 
 
 def close_kernel(len_ref, terms, own_ref, gate_ref, out_ref, *scratch):
@@ -707,35 +737,28 @@
     lw = mixing_exit_projection.shape[0]
     hid = lax.axis_size("hid")
     block_rows = training_accept_pieces.shape[0]
-    resuming = continuing_flags[0]
-    gains = normalizer_scales.astype(F32)
-    carried = jnp.where(resuming == 1, previous_normed_entries[0].astype(F32), 0.0)
-
-    both = jnp.concatenate([feedforward_entry_proj, feedforward_exit_proj])
-    both = [both, send(both, 0, 1), send(both, 1, 0), send(both, NX - 1, 0)]
-    w, s0 = spread(
+    w, s0, mate, before, after = spread(
         owning_index, continuing_flags, training_accept_pieces, training_lookup_pieces,
-        training_content_pieces, kept_summary_places[0, 0], hid,
+        training_content_pieces, kept_summary_places[0, 0], feedforward_entry_proj,
+        feedforward_exit_proj, hid,
     )
-    both, w = lax.optimization_barrier((both, w))
-    both = second_hop(both)
+    before_mate, after_mate = send(mate, 1, 0), send(mate, NX - 1, 0)
     w = w.reshape(-1, 3 * block_rows, lw)
     terms, state, last_in, x_share = time_mix(
-        partition_arrangement, prompt_extents, x, carried[0:1], gains, prior_step_blends,
+        partition_arrangement, prompt_extents, continuing_flags, x, previous_normed_entries[0],
+        normalizer_scales, prior_step_blends,
         gating_projection, forgetting_left_lowrank, forgetting_right_lowrank,
         forgetting_bias_vector[None], instant_emphasis[None], group_normalizer_scale[None],
         s0, mixing_exit_projection, w,
     )
-    terms, both = lax.optimization_barrier((terms, both))
-    both = third_hop(both)
-    middle, own_middle = join(terms, x_share)
-    out_terms, gate_rows, last_chan = channel_mix(
-        prompt_extents, middle.reshape(hid, rows, lw), carried[1:2], gains, prior_step_blends,
-        feedforward_accept_proj, both,
+    middle, own_middle, far, far_mate = join(terms, x_share, before, after_mate)
+    out_terms, gate_rows, shift_out = channel_mix(
+        prompt_extents, continuing_flags, last_in, middle.reshape(hid, rows, lw),
+        previous_normed_entries[0], normalizer_scales, prior_step_blends, feedforward_accept_proj,
+        [feedforward_entry_proj, feedforward_exit_proj, mate, before, after, before_mate, after_mate, far, far_mate],
     )
     layer_out = close(prompt_extents, out_terms, own_middle, gate_rows)[None]
-    shift_out = jnp.concatenate([last_in, last_chan]).astype(BF16)[None]
-    return (layer_out, state[None], shift_out)
+    return (layer_out, state[None], shift_out[None])
 
 
 def solution(mesh):

time: 268 us -> 254 us (0.948)
  starting transfers between devices: 11.4 us -> 3.31 us
    ppermute x7 -> x2, starting transfers between devices: 11.4 us -> 3.31 us  [send(): return lax.ppermute(value, 'req', pairs)]
    pallas_call x1, Pallas kernels: 100 us -> 105 us  [spread(): pl.pallas_call(spread_kernel, out_shape=(jax.ShapeDtypeStruct((req, hid,...]
    pallas_call x1, Pallas kernels: 29.1 us -> 25.1 us  [channel_mix(): pl.pallas_call(channel_mix_kernel, out_shape=(jax.ShapeDtypeStruct((group...]
    ppermute x7 -> x2, waiting for transfers between devices: 6.62 us -> 5.82 us  [send(): return lax.ppermute(value, 'req', pairs)]
  transfers between devices with their start and end apart: 7 -> 2, of which waited for: 2 -> 1; matrix products, arithmetic and copies ran while one was open for 0% -> 0% of each run, Pallas kernels for 69% -> 32%
where the time goes in v5:
time: 254 us
  Pallas kernels  238 us (94%)
  waiting for transfers between devices  5.82 us (2%)
  local copies, waits for them, and re-layouts  4.16 us (2%)
  starting transfers between devices  3.31 us (1%)
  between operations  2.63 us (1%)
    pallas_call x1, Pallas kernels, spread(): pl.pallas_call(spread_kernel, out_shape=(jax.ShapeDtypeStruct((req, hid,...  105 us
    pallas_call x1, Pallas kernels, join(): pl.pallas_call(join_kernel, out_shape=(jax.ShapeDtypeStruct(shape, BF16),...  49 us
    pallas_call x1, Pallas kernels, time_mix(): pl.pallas_call(time_mix_kernel, out_shape=(jax.ShapeDtypeStruct((width //...  33.2 us
    pallas_call x1, Pallas kernels, channel_mix(): pl.pallas_call(channel_mix_kernel, out_shape=(jax.ShapeDtypeStruct((group...  25.1 us
    pallas_call x1, Pallas kernels, close(): pl.pallas_call(close_kernel, out_shape=jax.ShapeDtypeStruct((rows, lw), B...  25.1 us
    ppermute x2, waiting for transfers between devices, send(): return lax.ppermute(value, 'req', pairs)  5.82 us
  transfers between devices with their start and end apart: 2, of which 1 were waited for; matrix products, arithmetic and copies ran while one was open for 0% of the time, Pallas kernels for 32%

profile of v5, /device:TPU:0, one launch (start us, length us, event | category | flops | bytes accessed | tf_op | source)
XLA Modules:
  0.0 253.8 jit_solution(16644063888483629253)
XLA Ops:
  1.9 105.4 %spread.1 = (bf16[8,16,96,256]{3,2,1,0:T(8,128)(2,1)}, f32[64,256]{1,0:T(8,128)}, bf16[224,4096]{1,0:T(8,128)(2,1)}, bf16[224,4096]{1,0:T(8,128)(2,1)}, bf16[224,4096]{1,0:T(8,128)(2,1)}) custom-call(s32[1]{0:T(128)S(6)} %copy.28.owner_ref, s32[1]{0:T(128)S(6)} %copy.27.flag_ref, f32[32,4096]{1,0:T(8,128)} %rec_ref.1, f32[32,4096]{1,0:T(8,128)} %key_ref.1, ...), custom_call_target="tpu_custom_call" | custom-call | flops 40000000000 | bytes 40000000 | tf_op jit(solution)/shard_map/spread/pallas_call | solution.py:571
  107.3 1.6 collective-permute-start.1
  108.9 1.7 collective-permute-start
  111.3 33.2 %time_mix.1 = (bf16[16,512,256]{2,1,0:T(8,128)(2,1)}, f32[4,64,64]{2,1,0:T(8,128)}, f32[1,4096]{1,0:T(1,128)}, bf16[512,256]{1,0:T(8,128)(2,1)}) custom-call(s32[128]{0:T(128)} %perm_ref.1, s32[1]{0:T(128)S(6)} %copy.26.len_ref, s32[1]{0:T(128)S(6)} %copy.27.flag_ref, bf16[512,4096]{1,0:T(8,128)(2,1)} %bitcast.15, bf16[2,4096]{1,0:T(2,128)(2,1)} %bitcast.17, ...), custom_call_target="tpu_custom_call" | custom-call | flops 40000000000 | bytes 40000000 | tf_op jit(solution)/shard_map/time_mix/pallas_call | solution.py:215
  144.5 5.8 %collective-permute-done.after_mate_ff.refs_6_ = bf16[224,4096]{1,0:T(8,128)(2,1)S(1)} collective-permute-done((bf16[224,4096]{1,0:T(8,128)(2,1)}, bf16[224,4096]{1,0:T(8,128)(2,1)S(1)}, u32[]{:S(2)}, u32[]{:S(2)}) %collective-permute-start) | collective-permute-done | bytes 1835040 | tf_op jit(solution)/shard_map/ppermute | solution.py:44
  150.3 0.0 copy-start.1
  150.3 1.2 copy-done.1
  151.6 49.0 %join.1 = (bf16[2,4,2,512,256]{4,3,2,1,0:T(8,128)(2,1)}, bf16[512,256]{1,0:T(8,128)(2,1)}, bf16[224,4096]{1,0:T(8,128)(2,1)}, bf16[224,4096]{1,0:T(8,128)(2,1)}) custom-call(bf16[2,4,2,512,256]{4,3,2,1,0:T(8,128)(2,1)} %bitcast.24, bf16[512,256]{1,0:T(8,128)(2,1)} %get-tuple-element.23.x_ref, bf16[224,4096]{1,0:T(8,128)(2,1)} %get-tuple-element.24.before_ff.refs_3_, ...), custom_call_target="tpu_custom_call" | custom-call | flops 40000000000 | bytes 40000000 | tf_op jit(solution)/shard_map/join/pallas_call | solution.py:665
  200.6 0.0 collective-permute-done.1.refs_5_
  200.6 0.0 copy-start
  200.6 1.2 copy-done
  201.8 25.1 %channel_mix.1 = (bf16[16,512,256]{2,1,0:T(8,128)(2,1)}, f32[512,256]{1,0:T(8,128)}, bf16[2,4096]{1,0:T(2,128)(2,1)}) custom-call(s32[1]{0:T(128)S(6)} %copy.26.len_ref, s32[1]{0:T(128)S(6)} %copy.27.flag_ref, f32[1,4096]{1,0:T(1,128)} %get-tuple-element.21.last_in_ref, bf16[16,512,256]{2,1,0:T(8,128)(2,1)} %bitcast.23, bf16[2,4096]{1,0:T(2,128)(2,1)} %bitcast.18, ...), custom_call_target="tpu_custom_call" | custom-call | flops 40000000000 | bytes 40000000 | tf_op jit(solution)/shard_map/channel_mix/pallas_call | solution.py:312
  227.0 25.1 %close.1 = bf16[512,256]{1,0:T(8,128)(2,1)} custom-call(s32[1]{0:T(128)S(6)} %copy.26.len_ref, bf16[2,4,2,512,256]{4,3,2,1,0:T(8,128)(2,1)} %bitcast.13, bf16[512,256]{1,0:T(8,128)(2,1)} %get-tuple-element.31.own_ref, f32[512,256]{1,0:T(8,128)} %get-tuple-element.32.gate_ref), custom_call_target="tpu_custom_call" | custom-call | tf_op jit(solution)/shard_map/close/pallas_call | solution.py:698
  252.1 1.7 copy.29
Async XLA Ops:
  107.3 93.2 %collective-permute-start.1 = (bf16[224,4096]{1,0:T(8,128)(2,1)}, bf16[224,4096]{1,0:T(8,128)(2,1)S(1)}, u32[]{:S(2)}, u32[]{:S(2)}) collective-permute-start(bf16[224,4096]{1,0:T(8,128)(2,1)} %get-tuple-element.25.refs_2_), channel_id=1, source_target_pairs={{0,32},{16,48},{32,64},{48,80},{64,96},{80,112},{96,0},{112,16},{1... | collective-permute-start | bytes 5505032 | tf_op jit(solution)/shard_map/ppermute | solution.py:44
  108.9 41.5 %collective-permute-start = (bf16[224,4096]{1,0:T(8,128)(2,1)}, bf16[224,4096]{1,0:T(8,128)(2,1)S(1)}, u32[]{:S(2)}, u32[]{:S(2)}) collective-permute-start(bf16[224,4096]{1,0:T(8,128)(2,1)} %get-tuple-element.25.refs_2_), channel_id=1, source_target_pairs={{0,96},{16,112},{32,0},{48,16},{64,32},{80,48},{96,64},{112,80},{1... | collective-permute-start | bytes 5505032 | tf_op jit(solution)/shard_map/ppermute | solution.py:44
  150.3 1.2 copy-start.1
  200.6 1.3 copy-start

commit v6 on v5

--- a/solution.py
+++ b/solution.py
@@ -20,6 +20,8 @@
 NY, NZ, NC = 2, 4, 2
 NX, NW = 4, 2
 PIECES = NX * NW
+ROW_REFS = 1 + NX + 2 * NX
+REST = 32
 SPLIT = 9
 COST = pl.CostEstimate(flops=40_000_000_000, bytes_accessed=40_000_000, transcendentals=0)
 VM = pl.BlockSpec(memory_space=pltpu.VMEM)
@@ -242,24 +244,31 @@
 def channel_mix_kernel(
     len_ref, flag_ref, last_in_ref, x_ref, first_ref, gain_ref, mix_ref, accept_ref, *refs,
 ):
-    entry_ref, exit_ref, *pairs = refs[: PIECES + 1]
-    terms_ref, gate_ref, shift_ref = refs[PIECES + 1 : PIECES + 4]
-    key_scr, value_scr, inner, acc_gate, hidden, key_sems, value_sems = refs[PIECES + 4 :]
+    entry_ref, exit_ref = refs[:2]
+    whole, cut, rests = refs[2:NX + 1], refs[NX + 1 : 2 * NX + 1], refs[2 * NX + 1 : ROW_REFS]
+    terms_ref, gate_ref, shift_ref = refs[ROW_REFS : ROW_REFS + 3]
+    key_scr, value_scr, inner, acc_gate, hidden, key_sems, value_sems = refs[ROW_REFS + 3 :]
     groups, rows, lw = x_ref.shape
     units = entry_ref.shape[0]
 
-    def fetch(own, begin, scr, sems):
-        pieces = [own] + [piece.at[pl.ds(begin, units)] for piece in pairs]
-        copies = [
-            pltpu.make_async_copy(piece, scr.at[pl.ds(i * units, units)], sems.at[i])
-            for i, piece in enumerate(pieces)
-        ]
+    def fetch(pieces, scr, sems):
+        copies, begin = [], 0
+        for i, piece in enumerate(pieces):
+            count = piece.shape[0]
+            copies.append(
+                pltpu.make_async_copy(piece, scr.at[pl.ds(begin, count)], sems.at[i])
+            )
+            begin += count
         for copy in copies:
             copy.start()
         return copies
 
-    key_copies = fetch(entry_ref, 0, key_scr, key_sems)
-    value_copies = fetch(exit_ref, units, value_scr, value_sems)
+    keys = [entry_ref] + [piece.at[pl.ds(0, units)] for piece in whole + cut]
+    values = [exit_ref] + [piece.at[pl.ds(units, units)] for piece in whole]
+    for piece, rest in zip(cut, rests):
+        values += [piece.at[pl.ds(units, units - REST)], rest]
+    key_copies = fetch(keys, key_scr, key_sems)
+    value_copies = fetch(values, value_scr, value_sems)
 
     def part(g):
         return x_ref[g].astype(F32)
@@ -316,7 +325,7 @@
             jax.ShapeDtypeStruct((rows, lw), F32),
             jax.ShapeDtypeStruct((2, width), BF16),
         ),
-        in_specs=[SM, SM] + [VM] * 6 + [HB] * (PIECES + 1),
+        in_specs=[SM, SM] + [VM] * 6 + [HB] * ROW_REFS,
         out_specs=(VM, VM, VM),
         scratch_shapes=[
             pltpu.VMEM((units, width), BF16),
@@ -325,7 +334,7 @@
             pltpu.VMEM((rows, lw), F32),
             pltpu.VMEM((rows, units), BF16),
             pltpu.SemaphoreType.DMA((PIECES,)),
-            pltpu.SemaphoreType.DMA((PIECES,)),
+            pltpu.SemaphoreType.DMA((PIECES + NX,)),
         ],
         compiler_params=pltpu.CompilerParams(vmem_limit_bytes=VMEM_LIMIT),
         cost_estimate=COST,
@@ -431,7 +440,7 @@
     return (a, upper), (b, lower)
 
 
-SUM_COPIES, COLLECT_COPIES = 17, 19
+SUM_COPIES, COLLECT_COPIES = 17, 22
 
 
 def sum_scratch(shape, copies):
@@ -453,7 +462,7 @@
 
 def spread_kernel(
     owner_ref, flag_ref, rec_ref, key_ref, val_ref, kept_ref, entry_ref, exit_ref,
-    w_ref, s0_ref, mate_ff, before_ff, after_ff,
+    w_ref, s0_ref, mate_ff, rest_ff, before_ff, after_ff,
     own, got, own_state, got_state, local_sem, sems, state_sems, send_w, recv_w,
 ):
     me, at = lax.axis_index("hid"), lax.axis_index("req")
@@ -516,7 +525,13 @@
     first_hops = [copies.start(src, before_ff.at[half], peers["up"]) for src, half in halves]
     first_hops += [copies.start(src, after_ff.at[half], peers["down"]) for src, half in halves]
     lax.fori_loop(1, hid, fill_and_send, 0)
-    first_hops += [copies.start(src, mate_ff.at[half], peers["mate"]) for src, half in halves]
+    first_hops += [
+        copies.start(entry_ref, mate_ff.at[pl.ds(0, units)], peers["mate"]),
+        copies.start(
+            exit_ref.at[pl.ds(0, units - REST)], mate_ff.at[pl.ds(units, units - REST)], peers["mate"]
+        ),
+        copies.start(exit_ref.at[pl.ds(units - REST, REST)], rest_ff, peers["mate"]),
+    ]
     fill(me)
     got[me] = own[me]
     lax.fori_loop(1, hid, arrive, 0)
@@ -573,12 +588,13 @@
         out_shape=(
             jax.ShapeDtypeStruct((req, hid, 3 * block_rows, lw), BF16),
             jax.ShapeDtypeStruct((HEAD, lw), F32),
-            pair,
+            jax.ShapeDtypeStruct((2 * units - REST, entry.shape[1]), BF16),
+            jax.ShapeDtypeStruct((REST, entry.shape[1]), BF16),
             pair,
             pair,
         ),
         in_specs=[SM, SM, VM, VM, VM, VM, HB, HB],
-        out_specs=(HB, VM, HB, HB, HB),
+        out_specs=(HB, VM, HB, HB, HB, HB),
         scratch_shapes=[
             pltpu.VMEM((hid, 3 * block_rows, lw), BF16),
             pltpu.VMEM((hid, 3 * block_rows, lw), BF16),
@@ -587,8 +603,8 @@
             pltpu.SemaphoreType.DMA,
             pltpu.SemaphoreType.DMA((2, hid - 1)),
             pltpu.SemaphoreType.DMA((2, hid - 1)),
-            pltpu.SemaphoreType.DMA((21,)),
-            pltpu.SemaphoreType.DMA((21,)),
+            pltpu.SemaphoreType.DMA((22,)),
+            pltpu.SemaphoreType.DMA((22,)),
         ],
         compiler_params=pltpu.CompilerParams(
             collective_id=2, has_side_effects=True, vmem_limit_bytes=VMEM_LIMIT
@@ -599,7 +615,8 @@
 
 
 def join_kernel(
-    terms, x_ref, before_ff, after_mate_ff, mid_ref, own_ref, far_ff, far_mate_ff, *scratch
+    terms, x_ref, before_ff, after_mate_ff, rest_ff,
+    mid_ref, own_ref, far_ff, far_mate_ff, before_rest_ff, after_rest_ff, far_rest_ff, *scratch
 ):
     place = hid_place()
     y, z, c, zu, z2, zd, peers = place
@@ -610,7 +627,9 @@
     }
     meet({**peers, **along_x})
     copies = Copies(*scratch[-2:])
+    rest_down = copies.start(rest_ff, after_rest_ff, along_x["x down"])
     last_hops = [
+        copies.start(rest_ff, before_rest_ff, along_x["x up"]),
         copies.start(before_ff, far_ff, along_x["x up"]),
         copies.start(after_mate_ff, far_mate_ff, along_x["x down"]),
     ]
@@ -622,6 +641,8 @@
         own = (x_ref[rows].astype(F32) + total).astype(BF16)
         own_ref[rows] = own
         mid_ref[c, z, y, rows] = own
+    rest_down.wait_recv()
+    last_hops.append(copies.start(after_rest_ff, far_rest_ff, along_x["x down"]))
 
     def pass_on(device, *index):
         return copies.start(mid_ref.at[index], mid_ref.at[index], peers[device])
@@ -659,7 +680,7 @@
     copies.finish()
 
 
-def join(terms, x_share, before, after_mate):
+def join(terms, x_share, before, after_mate, rest):
     rows, lw = x_share.shape
     shape = (NC, NZ, NY, rows, lw)
     return pl.pallas_call(
@@ -668,17 +689,18 @@
             jax.ShapeDtypeStruct(shape, BF16),
             jax.ShapeDtypeStruct((rows, lw), BF16),
             jax.ShapeDtypeStruct(before.shape, BF16),
-            jax.ShapeDtypeStruct(before.shape, BF16),
-        ),
-        in_specs=[VM, VM, HB, HB],
-        out_specs=(VM, VM, HB, HB),
+            jax.ShapeDtypeStruct(after_mate.shape, BF16),
+        )
+        + (jax.ShapeDtypeStruct(rest.shape, BF16),) * 3,
+        in_specs=[VM, VM, HB, HB, HB],
+        out_specs=(VM, VM, HB, HB, HB, HB, HB),
         scratch_shapes=sum_scratch(shape, SUM_COPIES + COLLECT_COPIES),
         compiler_params=pltpu.CompilerParams(
             collective_id=0, has_side_effects=True, vmem_limit_bytes=VMEM_LIMIT
         ),
         cost_estimate=COST,
         name="join",
-    )(terms.reshape(shape), x_share, before, after_mate)
+    )(terms.reshape(shape), x_share, before, after_mate, rest)
 
 
 def close_kernel(len_ref, terms, own_ref, gate_ref, out_ref, *scratch):
@@ -737,7 +759,7 @@
     lw = mixing_exit_projection.shape[0]
     hid = lax.axis_size("hid")
     block_rows = training_accept_pieces.shape[0]
-    w, s0, mate, before, after = spread(
+    w, s0, mate, rest, before, after = spread(
         owning_index, continuing_flags, training_accept_pieces, training_lookup_pieces,
         training_content_pieces, kept_summary_places[0, 0], feedforward_entry_proj,
         feedforward_exit_proj, hid,
@@ -751,11 +773,14 @@
         forgetting_bias_vector[None], instant_emphasis[None], group_normalizer_scale[None],
         s0, mixing_exit_projection, w,
     )
-    middle, own_middle, far, far_mate = join(terms, x_share, before, after_mate)
+    middle, own_middle, far, far_mate, before_rest, after_rest, far_rest = join(
+        terms, x_share, before, after_mate, rest
+    )
     out_terms, gate_rows, shift_out = channel_mix(
         prompt_extents, continuing_flags, last_in, middle.reshape(hid, rows, lw),
         previous_normed_entries[0], normalizer_scales, prior_step_blends, feedforward_accept_proj,
-        [feedforward_entry_proj, feedforward_exit_proj, mate, before, after, before_mate, after_mate, far, far_mate],
+        [feedforward_entry_proj, feedforward_exit_proj, before, after, far]
+        + [mate, before_mate, after_mate, far_mate, rest, before_rest, after_rest, far_rest],
     )
     layer_out = close(prompt_extents, out_terms, own_middle, gate_rows)[None]
     return (layer_out, state[None], shift_out[None])

time: 254 us -> 254 us (level)
  waiting for transfers between devices: 5.82 us -> 0.26 us
  Pallas kernels: 238 us -> 243 us
    pallas_call x1, Pallas kernels: 49 us -> 54.6 us  [join(): pl.pallas_call(join_kernel, out_shape=(jax.ShapeDtypeStruct(shape, BF16),...]
    ppermute x2, waiting for transfers between devices: 5.82 us -> 0.26 us  [send(): return lax.ppermute(value, 'req', pairs)]
  transfers between devices with their start and end apart: 2 -> 2, of which waited for: 1 -> 1; matrix products, arithmetic and copies ran while one was open for 0% -> 0% of each run, Pallas kernels for 32% -> 35%
where the time goes in v6:
time: 254 us
  Pallas kernels  243 us (96%)
  local copies, waits for them, and re-layouts  4.04 us (2%)
  starting transfers between devices  3.31 us (1%)
  between operations  2.63 us (1%)
    pallas_call x1, Pallas kernels, spread(): pl.pallas_call(spread_kernel, out_shape=(jax.ShapeDtypeStruct((req, hid,...  105 us
    pallas_call x1, Pallas kernels, join(): pl.pallas_call(join_kernel, out_shape=(jax.ShapeDtypeStruct(shape, BF16),...  54.6 us
    pallas_call x1, Pallas kernels, time_mix(): pl.pallas_call(time_mix_kernel, out_shape=(jax.ShapeDtypeStruct((width //...  33.2 us
    pallas_call x1, Pallas kernels, close(): pl.pallas_call(close_kernel, out_shape=jax.ShapeDtypeStruct((rows, lw), B...  25.2 us
    pallas_call x1, Pallas kernels, channel_mix(): pl.pallas_call(channel_mix_kernel, out_shape=(jax.ShapeDtypeStruct((group...  25.1 us
  transfers between devices with their start and end apart: 2, of which 1 were waited for; matrix products, arithmetic and copies ran while one was open for 0% of the time, Pallas kernels for 35%

profile of v6, /device:TPU:0, one launch (start us, length us, event | category | flops | bytes accessed | tf_op | source)
XLA Modules:
  0.0 253.7 jit_solution(9324265966038761)
XLA Ops:
  1.9 105.4 %spread.1 = (bf16[8,16,96,256]{3,2,1,0:T(8,128)(2,1)}, f32[64,256]{1,0:T(8,128)}, bf16[192,4096]{1,0:T(8,128)(2,1)}, bf16[32,4096]{1,0:T(8,128)(2,1)}, bf16[224,...) custom-call(s32[1]{0:T(128)S(6)} %copy.28.owner_ref, s32[1]{0:T(128)S(6)} %copy.27.flag_ref, f32[32,4096]{1,0:T(8,128)} %rec_ref.1, ...), custom_call_target="tpu_custom_call" | custom-call | flops 40000000000 | bytes 40000000 | tf_op jit(solution)/shard_map/spread/pallas_call | solution.py:586
  107.3 1.6 collective-permute-start.1
  108.9 1.7 collective-permute-start
  111.3 33.2 %time_mix.1 = (bf16[16,512,256]{2,1,0:T(8,128)(2,1)}, f32[4,64,64]{2,1,0:T(8,128)}, f32[1,4096]{1,0:T(1,128)}, bf16[512,256]{1,0:T(8,128)(2,1)}) custom-call(s32[128]{0:T(128)} %perm_ref.1, s32[1]{0:T(128)S(6)} %copy.26.len_ref, s32[1]{0:T(128)S(6)} %copy.27.flag_ref, bf16[512,4096]{1,0:T(8,128)(2,1)} %bitcast.15, bf16[2,4096]{1,0:T(2,128)(2,1)} %bitcast.17, ...), custom_call_target="tpu_custom_call" | custom-call | flops 40000000000 | bytes 40000000 | tf_op jit(solution)/shard_map/time_mix/pallas_call | solution.py:217
  144.5 0.3 collective-permute-done.after_mate_ff.refs_7_
  144.7 0.0 copy-start.1
  144.7 1.2 copy-done.1
  145.9 54.6 %join.1 = (bf16[2,4,2,512,256]{4,3,2,1,0:T(8,128)(2,1)}, bf16[512,256]{1,0:T(8,128)(2,1)}, bf16[224,4096]{1,0:T(8,128)(2,1)}, bf16[192,4096]{1,0:T(8,128)(2,1)},...) custom-call(bf16[2,4,2,512,256]{4,3,2,1,0:T(8,128)(2,1)} %bitcast.24, ...), custom_call_target="tpu_custom_call" | custom-call | flops 40000000000 | bytes 40000000 | tf_op jit(solution)/shard_map/join/pallas_call | solution.py:686
  200.5 0.0 collective-permute-done.1.refs_6_
  200.5 0.0 copy-start
  200.5 1.2 copy-done
  201.7 25.1 %channel_mix.1 = (bf16[16,512,256]{2,1,0:T(8,128)(2,1)}, f32[512,256]{1,0:T(8,128)}, bf16[2,4096]{1,0:T(2,128)(2,1)}) custom-call(s32[1]{0:T(128)S(6)} %copy.26.len_ref, s32[1]{0:T(128)S(6)} %copy.27.flag_ref, f32[1,4096]{1,0:T(1,128)} %get-tuple-element.25.last_in_ref, bf16[16,512,256]{2,1,0:T(8,128)(2,1)} %bitcast.23, bf16[2,4096]{1,0:T(2,128)(2,1)} %bitcast.18, ...), custom_call_target="tpu_custom_call" | custom-call | flops 40000000000 | bytes 40000000 | tf_op jit(solution)/shard_map/channel_mix/pallas_call | solution.py:321
  226.8 25.2 %close.1 = bf16[512,256]{1,0:T(8,128)(2,1)} custom-call(s32[1]{0:T(128)S(6)} %copy.26.len_ref, bf16[2,4,2,512,256]{4,3,2,1,0:T(8,128)(2,1)} %bitcast.13, bf16[512,256]{1,0:T(8,128)(2,1)} %get-tuple-element.39.own_ref, f32[512,256]{1,0:T(8,128)} %get-tuple-element.40.gate_ref), custom_call_target="tpu_custom_call" | custom-call | tf_op jit(solution)/shard_map/close/pallas_call | solution.py:720
  252.0 1.7 copy.29
Async XLA Ops:
  107.3 93.2 %collective-permute-start.1 = (bf16[192,4096]{1,0:T(8,128)(2,1)}, bf16[192,4096]{1,0:T(8,128)(2,1)S(1)}, u32[]{:S(2)}, u32[]{:S(2)}) collective-permute-start(bf16[192,4096]{1,0:T(8,128)(2,1)} %get-tuple-element.29.refs_5_), channel_id=1, source_target_pairs={{0,32},{16,48},{32,64},{48,80},{64,96},{80,112},{96,0},{112,16},{1... | collective-permute-start | bytes 4718600 | tf_op jit(solution)/shard_map/ppermute | solution.py:46
  108.9 35.9 %collective-permute-start = (bf16[192,4096]{1,0:T(8,128)(2,1)}, bf16[192,4096]{1,0:T(8,128)(2,1)S(1)}, u32[]{:S(2)}, u32[]{:S(2)}) collective-permute-start(bf16[192,4096]{1,0:T(8,128)(2,1)} %get-tuple-element.29.refs_5_), channel_id=1, source_target_pairs={{0,96},{16,112},{32,0},{48,16},{64,32},{80,48},{96,64},{112,80},{1... | collective-permute-start | bytes 4718600 | tf_op jit(solution)/shard_map/ppermute | solution.py:46
  144.7 1.2 copy-start.1
  200.5 1.2 copy-start
